TPU v7x, 1024 devices: a whole 8x8x8 slice. The times are simulated.
1024 devices in a mesh: loop: 32 (over y_lo, z, core), layer: 32 (over y_hi, x).
Axes of the slice: x: 8, y: 8 (y_hi: 4, y_lo: 2; y = y_hi * 2 + y_lo), z: 8, core: 2. Of those that a mesh axis runs over, the one named last changes fastest.
Arguments:
- flow_cols: bfloat16 [262144, 256], P(('loop', 'layer')), may hold values from -6 to 6
- restart: bfloat16 [262144, 256], P(('loop', 'layer')), may hold values from -6 to 6
- tile_blocks: bfloat16 [24576, 256, 256], P(('loop', 'layer')), may hold values from -0.078125 to 0.078125
- tile_rows: int32 [24576], P(('loop', 'layer')), may hold values from 0 to 31
- tile_srcs: int32 [24576], P(('loop', 'layer')), may hold values from 0 to 31, as said below
- tile_count: int32 [1024], P(('loop', 'layer')), may hold values from 16 to 24, as said below
- dangling: int32 [262144], P(('loop', 'layer')), may hold values 0 or 1
Outputs:
- next_flow: bfloat16 [262144, 256], P(('loop', 'layer'))
Inputs may be any that keep to these rules, and one draw needn't show every extreme that they name: `tile_srcs`: within each device's aligned block of 24 slots the source row blocks never fall. `tile_count`: slots at or beyond a device's count hold no tile; some device uses all 24 slots.
All inputs are finite; a program needn't handle non-finite values. No bound on the sum of `dangling` on one device may be relied on, other than what follows from the above.
Results may differ from a plain program's by a relative error of at most 0.017.
Values may be sent and summed in bfloat16 or wider, within the bound.
No kernel may reach another device: no remote copies, remote signals or barrier semaphores. Data moves between devices by JAX's collectives and lax.ppermute only.
A program may use at most 64 MiB of HBM per device.

v0:
```python
import jax
import jax.numpy as jnp
from jax import lax
from jax.sharding import PartitionSpec as P

DAMP = 0.85


def slot_range(tile_srcs, used_tiles, first_block, block_count):
    slot_ids = jnp.arange(tile_srcs.shape[0], dtype=jnp.int32)
    in_use = slot_ids < used_tiles
    first_slot = jnp.sum(jnp.where(in_use & (tile_srcs < first_block), 1, 0)).astype(jnp.int32)
    stop_slot = jnp.sum(jnp.where(in_use & (tile_srcs < first_block + block_count), 1, 0)).astype(
        jnp.int32
    )
    return (first_slot, stop_slot)


def accumulate(running, tile_blocks, tile_rows, tile_srcs, panels, first_slot, stop_slot):
    tile_side = tile_blocks.shape[1]

    def add_tile(slot_index, current):
        offset = tile_srcs[slot_index] * tile_side
        source_panel = lax.dynamic_slice_in_dim(panels, offset, tile_side, 0)
        tile_block = lax.dynamic_index_in_dim(tile_blocks, slot_index, 0, keepdims=False)
        product = jnp.dot(tile_block, source_panel, preferred_element_type=jnp.float32)
        row_start = tile_rows[slot_index] * tile_side
        earlier = lax.dynamic_slice_in_dim(current, row_start, tile_side, 0)
        return lax.dynamic_update_slice_in_dim(current, earlier + product, row_start, 0)

    return lax.fori_loop(first_slot, stop_slot, add_tile, running)


def body(flow_cols, restart, tile_blocks, tile_rows, tile_srcs, tile_count, dangling):
    tile_side = tile_blocks.shape[1]
    columns = flow_cols.shape[1]
    layers = lax.axis_size("layer")
    used_tiles = tile_count[0]
    initial = jnp.zeros((layers * tile_side, columns), jnp.float32)
    piece = lax.all_gather(flow_cols, "loop", axis=0, tiled=True)
    first_block = jnp.int32(0) // tile_side
    block_count = piece.shape[0] // tile_side
    first_slot, stop_slot = slot_range(tile_srcs, used_tiles, first_block, block_count)
    partial_value = accumulate(
        initial, tile_blocks, tile_rows, tile_srcs, piece, first_slot, stop_slot
    )
    summed = lax.psum_scatter(
        partial_value.astype(jnp.bfloat16), "layer", scatter_dimension=0, tiled=True
    ).astype(jnp.float32)
    own_flow = flow_cols.astype(jnp.float32)
    mask_col = dangling.astype(jnp.float32)[:, None]
    result = DAMP * (summed + mask_col * own_flow) + (1.0 - DAMP) * restart.astype(jnp.float32)
    return result.astype(jnp.bfloat16)


def solution(mesh):
    in_specs = (
        P(("loop", "layer"), None),
        P(("loop", "layer"), None),
        P(("loop", "layer"), None, None),
        P(("loop", "layer")),
        P(("loop", "layer")),
        P(("loop", "layer")),
        P(("loop", "layer")),
    )
    out_specs = P(("loop", "layer"), None)
    return jax.shard_map(body, mesh=mesh, in_specs=in_specs, out_specs=out_specs, check_vma=False)
```

profile of v0, /device:TPU:14, one launch (start us, length us, event | category | flops | bytes accessed | tf_op | source)
XLA Modules:
  0.0 548.2 jit_solution(3331221707635083420)
XLA Ops:
  6.5 0.7 all-gather.2.cloned.1.call-update
  8.0 1.3 fusion.6
  9.3 85.8 %all-gather.2.cloned.1.call-done = bf16[8192,256]{1,0:T(8,128)(2,1)} async-done(((bf16[256,256]{1,0:T(8,128)(2,1)}), bf16[8192,256]{1,0:T(8,128)(2,1)}) %all-gather.2.cloned.1.call-update) | async-done | bytes 4194320 | tf_op jit(solution)/shard_map/all_gather | solution.py:40
  95.0 3.8 broadcast_in_dim.13
  98.8 201.0 %while.10 = (s32[]{:T(128)}, f32[8192,256]{1,0:T(8,128)}, s32[]{:T(128)}, s32[24]{0:T(128)S(1)}, bf16[24,256,256]{2,1,0:T(8,128)(2,1)}, /*index=5*/s32[24]{0:T(1...) while((s32[]{:T(128)}, f32[8192,256]{1,0:T(8,128)}, ...), condition=%wide.region_3.4_spmd, body=%wide.region_2.3_spmd.sunk | while | flops 33619980 | bytes 786711 | solution.py:31
  101.6 0.6 dynamic_slice.32
  102.8 0.6 dynamic_slice.31
  104.1 2.0 fusion.12
  109.9 0.6 dynamic_slice.32
  111.2 0.6 dynamic_slice.31
  112.4 2.0 fusion.12
  118.2 0.6 dynamic_slice.32
  119.5 0.6 dynamic_slice.31
  120.7 2.0 fusion.12
  126.6 0.6 dynamic_slice.32
  127.8 0.6 dynamic_slice.31
  129.1 2.0 fusion.12
  134.9 0.6 dynamic_slice.32
  136.1 0.6 dynamic_slice.31
  137.4 2.0 fusion.12
  143.2 0.6 dynamic_slice.32
  144.5 0.6 dynamic_slice.31
  145.7 2.0 fusion.12
  151.5 0.6 dynamic_slice.32
  152.8 0.6 dynamic_slice.31
  154.0 2.0 fusion.12
  159.8 0.6 dynamic_slice.32
  161.1 0.6 dynamic_slice.31
  162.3 2.0 fusion.12
  169.4 0.6 dynamic_slice.31
  170.7 2.0 fusion.12
  177.8 0.6 dynamic_slice.31
  179.0 2.0 fusion.12
  186.1 0.6 dynamic_slice.31
  187.3 2.0 fusion.12
  194.4 0.6 dynamic_slice.31
  195.7 2.0 fusion.12
  202.8 0.6 dynamic_slice.31
  204.0 2.0 fusion.12
  211.1 0.6 dynamic_slice.31
  212.3 2.0 fusion.12
  219.4 0.6 dynamic_slice.31
  220.6 2.0 fusion.12
  227.7 0.6 dynamic_slice.31
  228.9 2.0 fusion.12
  236.0 0.6 dynamic_slice.31
  237.2 2.0 fusion.12
  244.3 0.6 dynamic_slice.31
  245.6 2.0 fusion.12
  252.7 0.6 dynamic_slice.31
  253.9 2.0 fusion.12
  261.0 0.6 dynamic_slice.31
  262.3 2.0 fusion.12
  269.3 0.6 dynamic_slice.31
  270.6 2.0 fusion.12
  277.7 0.6 dynamic_slice.31
  278.9 2.0 fusion.12
  286.0 0.6 dynamic_slice.31
  287.3 2.0 fusion.12
  294.3 0.6 dynamic_slice.31
  295.6 2.0 fusion.12
  299.8 5.8 %convert_element_type.18 = bf16[8192,256]{1,0:T(8,128)(2,1)} convert(f32[8192,256]{1,0:T(8,128)} %get-tuple-element.43) | non-fusion elementwise | flops 2097152 | bytes 12582912 | tf_op jit(solution)/shard_map/convert_element_type | solution.py:48
  305.7 234.0 %reduce-scatter.2.cloned.1.call-done = bf16[256,256]{1,0:T(8,128)(2,1)} async-done(((bf16[8192,256]{1,0:T(8,128)(2,1)}), bf16[256,256]{1,0:T(8,128)(2,1)}) %reduce-scatter.2.cloned.1.call-update) | async-done | bytes 131088 | tf_op jit(solution)/shard_map/reduce_scatter | solution.py:47
  539.6 1.7 add_convert_fusion
  (30 shorter events, 9.5 us)
Async XLA Ops:
  6.5 92.2 %copy-start.3 = (s32[24]{0:T(128)S(1)}, s32[24]{0:T(128)}, u32[]{:S(2)}) copy-start(s32[24]{0:T(128)} %param.13) | copy-start | bytes 292
  6.5 92.2 %copy-start.4 = (s32[24]{0:T(128)S(1)}, s32[24]{0:T(128)}, u32[]{:S(2)}) copy-start(s32[24]{0:T(128)} %param.12) | copy-start | bytes 292
  6.5 88.5 %all-gather.2.cloned.1.call-start = ((), (), s32[]{:S(2)}) async-start(), calls=%async_computation.1 | async-start | bytes 4325376 | tf_op jit(solution)/shard_map/all_gather | solution.py:40
  7.3 532.4 %reduce-scatter.2.cloned.1.call-start = ((), (), s32[]{:S(2)}) async-start(), calls=%async_computation.2 | async-start | bytes 4325376 | tf_op jit(solution)/shard_map/reduce_scatter | solution.py:47
  299.8 5.8 %copy-start.2 = (s32[256]{0:T(256)S(1)}, s32[256]{0:T(256)}, u32[]{:S(2)}) copy-start(s32[256]{0:T(256)} %param.15) | copy-start | bytes 3076
  299.8 239.8 %copy-start = (bf16[256,256]{1,0:T(8,128)(2,1)S(1)}, bf16[256,256]{1,0:T(8,128)(2,1)}, u32[]{:S(2)}) copy-start(bf16[256,256]{1,0:T(8,128)(2,1)} %param.9) | copy-start | bytes 393220
  299.8 239.8 %copy-start.1 = (bf16[256,256]{1,0:T(8,128)(2,1)S(1)}, bf16[256,256]{1,0:T(8,128)(2,1)}, u32[]{:S(2)}) copy-start(bf16[256,256]{1,0:T(8,128)(2,1)} %param.10) | copy-start | bytes 393220
Sparse Core Ops, SparseCore 0:
  10.1 84.8 all-gather.1
  305.8 233.8 reduce-scatter.1
where the time goes:
time: 552 us; the launch traced here: 548 us
  waiting for transfers between devices  320 us (58%)
  loops' own time  125 us (23%)
  matrix products  47.8 us (9%)
  local copies, waits for them, and re-layouts  32 us (6%)
  between operations  14.1 us (3%)
  other arithmetic  8.77 us (2%)
    reduce_scatter x1, waiting for transfers between devices, body(): lax.psum_scatter(partial_value.astype(jnp.bfloat16), 'layer', scatter_dim...  234 us
    another operation x1, loops' own time, accumulate(): return lax.fori_loop(first_slot, stop_slot, add_tile, running)  125 us
    all_gather x1, waiting for transfers between devices, body(): piece = lax.all_gather(flow_cols, 'loop', axis=0, tiled=True)  85.8 us
    dot_general x24, matrix products, add_tile(): jnp.dot(tile_block, source_panel, preferred_element_type=jnp.float32)  47.8 us
    dynamic_slice x24, local copies, waits for them, and re-layouts, add_tile(): row_start = tile_rows[slot_index] * tile_side  14.1 us
    dynamic_slice x24, local copies, waits for them, and re-layouts, add_tile(): offset = tile_srcs[slot_index] * tile_side  14.1 us
  transfers between devices with their start and end apart: 2, of which 2 were waited for; matrix products, arithmetic and copies ran while one was open for 0% of the time, Pallas kernels for 0%

commit v1 on v0

v1 whole, which is shorter than its diff:
```python
import jax
import jax.numpy as jnp
from jax import lax
from jax.experimental import pallas as pl
from jax.experimental.pallas import tpu as pltpu
from jax.sharding import Mesh, PartitionSpec as P

DAMP = 0.85
LOOP = (("ylo", 2), ("z", 8), ("core", 2))
LAYER = (("yhi", 4), ("x", 8))
LOOP_AXES = tuple(name for name, _ in LOOP)
LAYER_AXES = tuple(name for name, _ in LAYER)
N_YHI, N_X = 4, 8
ROW_TILES = N_YHI * N_X


def tiles_kernel(count, rows, srcs, tiles, panels, out, head, following, acc):
    side = tiles.shape[1]

    def clear(r, carry):
        head[r] = -1
        return carry

    lax.fori_loop(0, ROW_TILES, clear, 0)

    def link(s, carry):
        r = rows[s]
        following[s] = head[r]
        head[r] = s
        return carry

    lax.fori_loop(0, count[0], link, 0)

    def block(p, carry):
        r = (p % N_YHI) * N_X + p // N_YHI
        first = head[r]
        where = pl.ds(pl.multiple_of(p * side, side), side)

        @pl.when(first < 0)
        def _():
            out[where, :] = jnp.zeros((side, out.shape[1]), out.dtype)

        @pl.when(first >= 0)
        def _():
            def product(s):
                source = pl.ds(pl.multiple_of(srcs[s] * side, side), side)
                return jnp.dot(tiles[s], panels[source, :], preferred_element_type=jnp.float32)

            acc[...] = product(first)

            def more(s):
                acc[...] += product(s)
                return following[s]

            lax.while_loop(lambda s: s >= 0, more, following[first])
            out[where, :] = acc[...].astype(out.dtype)

        return carry

    lax.fori_loop(0, ROW_TILES, block, 0)


def partial_products(tile_blocks, tile_rows, tile_srcs, tile_count, panels):
    slots, side = tile_blocks.shape[:2]
    columns = panels.shape[1]
    smem = pl.BlockSpec(memory_space=pltpu.SMEM)
    vmem = pl.BlockSpec(memory_space=pltpu.VMEM)
    return pl.pallas_call(
        tiles_kernel,
        out_shape=jax.ShapeDtypeStruct((ROW_TILES * side, columns), jnp.bfloat16),
        in_specs=[smem, smem, smem, vmem, vmem],
        out_specs=vmem,
        scratch_shapes=[
            pltpu.SMEM((ROW_TILES,), jnp.int32),
            pltpu.SMEM((slots,), jnp.int32),
            pltpu.VMEM((side, columns), jnp.float32),
        ],
        compiler_params=pltpu.CompilerParams(vmem_limit_bytes=40 << 20),
        name="tile_products",
    )(tile_count, tile_rows, tile_srcs, tile_blocks, panels)


def body(flow_cols, restart, tile_blocks, tile_rows, tile_srcs, tile_count, dangling):
    side, columns = flow_cols.shape
    panels = lax.all_gather(flow_cols, LOOP_AXES, axis=0, tiled=True)
    partial = partial_products(tile_blocks, tile_rows, tile_srcs, tile_count, panels)
    along_x = lax.psum_scatter(partial, "x", scatter_dimension=0, tiled=True)
    shares = lax.all_to_all(along_x.reshape(N_YHI, side, columns), "yhi", 0, 0)
    summed = jnp.sum(shares.astype(jnp.float32), axis=0)
    own_flow = flow_cols.astype(jnp.float32)
    mask_col = dangling.astype(jnp.float32)[:, None]
    result = DAMP * (summed + mask_col * own_flow) + (1.0 - DAMP) * restart.astype(jnp.float32)
    return result.astype(jnp.bfloat16)


def solution(mesh):
    names = LOOP_AXES + LAYER_AXES
    sizes = [size for _, size in LOOP + LAYER]
    fine = Mesh(mesh.devices.reshape(sizes), names)
    rows = P(names, None)
    in_specs = (rows, rows, P(names, None, None), P(names), P(names), P(names), P(names))
    return jax.shard_map(body, mesh=fine, in_specs=in_specs, out_specs=rows, check_vma=False)
```

time: 552 us -> 198 us (0.36)
  waiting for transfers between devices: 320 us -> 161 us
  loops' own time: 125 us -> 0 us
  matrix products: 47.8 us -> 0 us
  local copies, waits for them, and re-layouts: 32 us -> 7.34 us
  other arithmetic: 8.77 us -> 0.85 us
  starting transfers between devices: 0.04 us -> 6.86 us
  Pallas kernels: 0 us -> 6.62 us
    reduce_scatter x1, waiting for transfers between devices: 234 us -> 57.6 us  [body(): along_x = lax.psum_scatter(partial, 'x', scatter_dimension=0, tiled=True)]
    another operation x1 -> x0, loops' own time: 125 us -> none  [accumulate(): return lax.fori_loop(first_slot, stop_slot, add_tile, running)]
    dot_general x24 -> x0, matrix products: 47.8 us -> none  [add_tile(): jnp.dot(tile_block, source_panel, preferred_element_type=jnp.float32)]
    dynamic_slice x48 -> x0, local copies, waits for them, and re-layouts: 28.2 us -> none  [the longest x24 14.1 us: add_tile(): row_start = tile_rows[slot_index] * tile_side]
    all_to_all x0 -> x1, waiting for transfers between devices: none -> 15.5 us  [body(): shares = lax.all_to_all(along_x.reshape(N_YHI, side, columns), 'yhi', 0, 0)]
    unnamed x10 -> x16, local copies, waits for them, and re-layouts: 0.03 us -> 7.34 us
    all_to_all x0 -> x1, starting transfers between devices: none -> 6.82 us  [body(): shares = lax.all_to_all(along_x.reshape(N_YHI, side, columns), 'yhi', 0, 0)]
    pallas_call x0 -> x1, Pallas kernels: none -> 6.62 us  [partial_products(): pl.pallas_call(tiles_kernel, out_shape=jax.ShapeDtypeStruct((ROW_TILES *...]
  transfers between devices with their start and end apart: 2 -> 3, of which waited for: 2 -> 3; matrix products, arithmetic and copies ran while one was open for 0% -> 0% of each run, Pallas kernels for 0% -> 0%
where the time goes in v1:
time: 198 us; the launch traced here: 197 us
  waiting for transfers between devices  161 us (81%)
  between operations  14.1 us (7%)
  local copies, waits for them, and re-layouts  7.34 us (4%)
  starting transfers between devices  6.86 us (3%)
  Pallas kernels  6.62 us (3%)
    all_gather x1, waiting for transfers between devices, body(): panels = lax.all_gather(flow_cols, LOOP_AXES, axis=0, tiled=True)  87.1 us
    reduce_scatter x1, waiting for transfers between devices, body(): along_x = lax.psum_scatter(partial, 'x', scatter_dimension=0, tiled=True)  57.6 us
    all_to_all x1, waiting for transfers between devices, body(): shares = lax.all_to_all(along_x.reshape(N_YHI, side, columns), 'yhi', 0, 0)  15.5 us
    unnamed x16, local copies, waits for them, and re-layouts  7.34 us
    all_to_all x1, starting transfers between devices, body(): shares = lax.all_to_all(along_x.reshape(N_YHI, side, columns), 'yhi', 0, 0)  6.82 us
    pallas_call x1, Pallas kernels, partial_products(): pl.pallas_call(tiles_kernel, out_shape=jax.ShapeDtypeStruct((ROW_TILES *...  6.62 us
  transfers between devices with their start and end apart: 3, of which 3 were waited for; matrix products, arithmetic and copies ran while one was open for 0% of the time, Pallas kernels for 0%

profile of v1, /device:TPU:14, one launch (start us, length us, event | category | flops | bytes accessed | tf_op | source)
XLA Modules:
  0.0 196.6 jit_solution(1659577268430117013)
XLA Ops:
  6.5 0.0 all-gather.2.cloned.1.call-start
  6.5 0.7 all-gather.2.cloned.1.call-update
  7.3 0.0 reduce-scatter.2.cloned.1.call-start
  7.9 87.1 %all-gather.2.cloned.1.call-done.panels = bf16[8192,256]{1,0:T(8,128)(2,1)} async-done(((bf16[256,256]{1,0:T(8,128)(2,1)}), bf16[8192,256]{1,0:T(8,128)(2,1)}) %all-gather.2.cloned.1.call-update) | async-done | bytes 4194320 | tf_op jit(solution)/shard_map/all_gather | solution.py:85
  95.0 0.0 copy-start.1
  95.0 2.2 %copy-done.1 = bf16[8192,256]{1,0:T(8,128)(2,1)S(1)} copy-done((bf16[8192,256]{1,0:T(8,128)(2,1)S(1)}, bf16[8192,256]{1,0:T(8,128)(2,1)}, u32[]{:S(2)}) %copy-start.1) | copy-done | bytes 4194328
  97.2 0.0 copy-start.2
  97.2 1.9 copy-done.2
  99.1 0.0 copy-start.3
  99.1 0.7 copy-done.3
  99.7 0.0 copy-start.4
  99.8 0.7 copy-done.4
  100.4 6.6 %tile_products.1 = bf16[8192,256]{1,0:T(8,128)(2,1)S(1)} custom-call(s32[1]{0:T(128)S(6)} %copy.8.count, s32[24]{0:T(128)S(1)} %copy-done.3, s32[24]{0:T(128)S(1)} %copy-done.4, bf16[24,256,256]{2,1,0:T(8,128)(2,1)S(1)} %copy-done.2, bf16[8192,256]{1,0:T(8,128)(2,1)S(1)} %copy-done.1), custom_call_target="tpu_custom_call" | custom-call | tf_op jit(solution)/shard_map/tile_products/pallas_call | solution.py:68
  107.0 0.0 copy-start
  107.0 1.9 copy-done
  109.0 0.0 copy-start.7
  109.0 0.0 copy-start.5
  109.0 0.0 copy-start.6
  109.0 0.0 reduce-scatter.2.cloned.1.call-update
  109.0 57.6 %reduce-scatter.2.cloned.1.call-done = bf16[1024,256]{1,0:T(8,128)(2,1)} async-done(((bf16[8192,256]{1,0:T(8,128)(2,1)}), bf16[1024,256]{1,0:T(8,128)(2,1)}) %reduce-scatter.2.cloned.1.call-update) | async-done | bytes 524304 | tf_op jit(solution)/shard_map/reduce_scatter | solution.py:87
  166.6 6.8 %all-to-all-start = ((bf16[4,256,256]{2,1,0:T(8,128)(2,1)}), bf16[4,256,256]{2,1,0:T(8,128)(2,1)S(1)}, u32[]{:S(2)}, u32[]{:S(2)}) async-start(bf16[4,256,256]{2,1,0:T(8,128)(2,1)} %bitcast.1), calls=%async_computation.1 | async-start | bytes 1048576 | tf_op jit(solution)/shard_map/all_to_all | solution.py:88
  173.5 0.0 copy-done.7
  173.5 15.5 %all-to-all-done = bf16[4,256,256]{2,1,0:T(8,128)(2,1)S(1)} async-done(((bf16[4,256,256]{2,1,0:T(8,128)(2,1)}), bf16[4,256,256]{2,1,0:T(8,128)(2,1)S(1)}, u32[]{:S(2)}, u32[]{:S(2)}) %all-to-all-start) | async-done | bytes 524320 | tf_op jit(solution)/shard_map/all_to_all | solution.py:88
  188.9 0.1 convert_reduce_fusion
  189.0 0.0 copy-done.5
  189.0 0.0 copy-done.6
  189.0 0.8 add_convert_fusion
  (1 shorter events, 0.0 us)
Async XLA Ops:
  6.5 88.5 %all-gather.2.cloned.1.call-start = ((), (), s32[]{:S(2)}) async-start(), calls=%async_computation.2 | async-start | bytes 4325376 | tf_op jit(solution)/shard_map/all_gather | solution.py:85
  7.3 159.4 %reduce-scatter.2.cloned.1.call-start = ((), (), s32[]{:S(2)}) async-start(), calls=%async_computation.3 | async-start | bytes 4718592 | tf_op jit(solution)/shard_map/reduce_scatter | solution.py:87
  95.0 2.2 %copy-start.1 = (bf16[8192,256]{1,0:T(8,128)(2,1)S(1)}, bf16[8192,256]{1,0:T(8,128)(2,1)}, u32[]{:S(2)}) copy-start(bf16[8192,256]{1,0:T(8,128)(2,1)} %all-gather.2.cloned.1.call-done.panels) | copy-start | bytes 12582916
  97.2 1.9 copy-start.2
  99.1 0.7 copy-start.3
  99.7 0.7 copy-start.4
  107.0 1.9 copy-start
  109.0 64.5 %copy-start.7 = (s32[256]{0:T(256)S(1)}, s32[256]{0:T(256)}, u32[]{:S(2)}) copy-start(s32[256]{0:T(256)} %param.13) | copy-start | bytes 3076
  109.0 80.0 %copy-start.5 = (bf16[256,256]{1,0:T(8,128)(2,1)S(1)}, bf16[256,256]{1,0:T(8,128)(2,1)}, u32[]{:S(2)}) copy-start(bf16[256,256]{1,0:T(8,128)(2,1)} %param.7) | copy-start | bytes 393220
  109.0 80.0 %copy-start.6 = (bf16[256,256]{1,0:T(8,128)(2,1)S(1)}, bf16[256,256]{1,0:T(8,128)(2,1)}, u32[]{:S(2)}) copy-start(bf16[256,256]{1,0:T(8,128)(2,1)} %param.8) | copy-start | bytes 393220
  166.6 22.3 %all-to-all-start = ((bf16[4,256,256]{2,1,0:T(8,128)(2,1)}), bf16[4,256,256]{2,1,0:T(8,128)(2,1)S(1)}, u32[]{:S(2)}, u32[]{:S(2)}) async-start(bf16[4,256,256]{2,1,0:T(8,128)(2,1)} %bitcast.1), calls=%async_computation.1 | async-start | bytes 1048576 | tf_op jit(solution)/shard_map/all_to_all | solution.py:88
Sparse Core Ops, SparseCore 0:
  10.1 84.8 all-gather.1
  109.1 57.4 reduce-scatter.1

commit v2 on v1

v2 whole, which is shorter than its diff:
```python
import jax
import jax.numpy as jnp
from jax import lax
from jax.experimental import pallas as pl
from jax.experimental.pallas import tpu as pltpu
from jax.sharding import Mesh, PartitionSpec as P

DAMP = 0.85
LOOP = (("ylo", 2), ("z", 8), ("core", 2))
LAYER = (("yhi", 4), ("x", 8))
SIZES = dict(LOOP + LAYER)
N_YLO, N_Z, N_CORE = SIZES["ylo"], SIZES["z"], SIZES["core"]
N_YHI, N_X = SIZES["yhi"], SIZES["x"]
ROW_TILES = N_YHI * N_X


def shifted(value, axis, by):
    size = SIZES[axis]
    return lax.ppermute(value, axis, [(i, (i + by) % size) for i in range(size)])


def tiles_kernel(
    count, rows, srcs, tiles, near, across, far_up, far_down, rest, head, following, acc
):
    side = tiles.shape[1]
    my_ylo, my_z, my_core = lax.axis_index("ylo"), lax.axis_index("z"), lax.axis_index("core")
    my_x = lax.axis_index("x")

    def clear(r, carry):
        head[r] = -1
        return carry

    lax.fori_loop(0, ROW_TILES, clear, 0)

    def link(s, carry):
        r = rows[s]
        following[s] = head[r]
        head[r] = s
        return carry

    lax.fori_loop(0, count[0], link, 0)

    def add_product(s):
        src = srcs[s]
        dz = ((src // N_CORE) % N_Z + N_Z - my_z) % N_Z
        dy = (src // (N_CORE * N_Z) + N_YLO - my_ylo) % N_YLO
        slot = jnp.where(dz >= N_Z // 2, (N_Z - dz) * 2 - 1, 2 * dz)
        panel = pl.ds(pl.multiple_of((slot * N_YLO + dy) * side, side), side)
        same_core = src % N_CORE == my_core

        @pl.when(same_core)
        def _():
            acc[...] += jnp.dot(tiles[s], near[panel, :], preferred_element_type=jnp.float32)

        @pl.when(jnp.logical_not(same_core))
        def _():
            acc[...] += jnp.dot(tiles[s], across[panel, :], preferred_element_type=jnp.float32)

        return following[s]

    def fill(out, blocks, row_of):
        def block(p, carry):
            first = head[row_of(p)]
            where = pl.ds(pl.multiple_of(p * side, side), side)

            @pl.when(first < 0)
            def _():
                out[where, :] = jnp.zeros((side, out.shape[1]), out.dtype)

            @pl.when(first >= 0)
            def _():
                acc[...] = jnp.zeros_like(acc)
                lax.while_loop(lambda s: s >= 0, add_product, first)
                out[where, :] = acc[...].astype(out.dtype)

            return carry

        lax.fori_loop(0, blocks, block, 0)

    def row(k, yhi):
        return yhi * N_X + (my_x + k) % N_X

    half = N_YHI // 2
    fill(far_up, half, lambda p: row(N_X // 2, p))
    fill(far_down, half, lambda p: row(N_X // 2, p + half))

    def rest_row(p):
        i = p // N_YHI
        k = jnp.where(i % 2 == 0, N_X // 2 - 1 - i // 2, N_X // 2 + 1 + i // 2)
        return row(k, p % N_YHI)

    fill(rest, (N_X - 1) * N_YHI, rest_row)


def partial_products(tile_blocks, tile_rows, tile_srcs, tile_count, near, across):
    slots, side = tile_blocks.shape[:2]
    columns = near.shape[1]
    smem = pl.BlockSpec(memory_space=pltpu.SMEM)
    vmem = pl.BlockSpec(memory_space=pltpu.VMEM)

    def out(tiles):
        return jax.ShapeDtypeStruct((tiles * side, columns), jnp.bfloat16)

    return pl.pallas_call(
        tiles_kernel,
        out_shape=(out(N_YHI // 2), out(N_YHI // 2), out((N_X - 1) * N_YHI)),
        in_specs=[smem, smem, smem, vmem, vmem, vmem],
        out_specs=(vmem, vmem, vmem),
        scratch_shapes=[
            pltpu.SMEM((ROW_TILES,), jnp.int32),
            pltpu.SMEM((slots,), jnp.int32),
            pltpu.VMEM((side, columns), jnp.float32),
        ],
        compiler_params=pltpu.CompilerParams(vmem_limit_bytes=24 << 20),
        name="tile_products",
    )(tile_count, tile_rows, tile_srcs, tile_blocks, near, across)


def gather_panels(flow_cols):
    side = flow_cols.shape[0]
    own = jnp.concatenate([flow_cols, shifted(flow_cols, "ylo", 1)], 0)
    below1, above1 = shifted(own, "z", 1), shifted(own, "z", -1)
    below2, above2 = shifted(own, "z", 2), shifted(own, "z", -2)
    below3, above3 = shifted(below2, "z", 1), shifted(above2, "z", -1)
    below4, above4 = shifted(below2[:side], "z", 2), shifted(above2[side:], "z", -2)
    near = jnp.concatenate(
        [own, below1, above1, below2, above2, below3, above3, below4, above4], 0
    )
    return near, shifted(near, "core", 1)


def add(*terms):
    total = terms[0].astype(jnp.float32)
    for term in terms[1:]:
        total = total + term.astype(jnp.float32)
    return total.astype(jnp.bfloat16)


def reduce_along_x(far_up, far_down, rest):
    chunk = 2 * far_up.shape[0]
    half = far_up.shape[0]
    up3, down3, up2, down2, up1, down1, own = (
        rest[i * chunk : (i + 1) * chunk] for i in range(N_X - 1)
    )
    up, down = shifted(far_up, "x", 1), shifted(far_down, "x", -1)
    up = shifted(jnp.concatenate([add(up3[:half], up), up3[half:]], 0), "x", 1)
    down = shifted(jnp.concatenate([down3[:half], add(down3[half:], down)], 0), "x", -1)
    up, down = shifted(add(up2, up), "x", 1), shifted(add(down2, down), "x", -1)
    up, down = shifted(add(up1, up), "x", 1), shifted(add(down1, down), "x", -1)
    return add(own, up, down)


def body(flow_cols, restart, tile_blocks, tile_rows, tile_srcs, tile_count, dangling):
    side, columns = flow_cols.shape
    near, across = gather_panels(flow_cols)
    far_up, far_down, rest = partial_products(
        tile_blocks, tile_rows, tile_srcs, tile_count, near, across
    )
    along_x = reduce_along_x(far_up, far_down, rest)
    shares = lax.all_to_all(along_x.reshape(N_YHI, side, columns), "yhi", 0, 0)
    summed = jnp.sum(shares.astype(jnp.float32), axis=0)
    own_flow = flow_cols.astype(jnp.float32)
    mask_col = dangling.astype(jnp.float32)[:, None]
    result = DAMP * (summed + mask_col * own_flow) + (1.0 - DAMP) * restart.astype(jnp.float32)
    return result.astype(jnp.bfloat16)


def solution(mesh):
    names = tuple(SIZES)
    fine = Mesh(mesh.devices.reshape(tuple(SIZES.values())), names)
    rows = P(names, None)
    in_specs = (rows, rows, P(names, None, None), P(names), P(names), P(names), P(names))
    return jax.shard_map(body, mesh=fine, in_specs=in_specs, out_specs=rows, check_vma=False)
```

time: 198 us -> 167 us (0.84)
  waiting for transfers between devices: 161 us -> 70.9 us
  starting transfers between devices: 6.86 us -> 83 us
  between operations: 14.1 us -> 1.04 us
  local copies, waits for them, and re-layouts: 7.34 us -> 1.18 us
    all_gather x1 -> x0, waiting for transfers between devices: 87.1 us -> none  [body(): panels = lax.all_gather(flow_cols, LOOP_AXES, axis=0, tiled=True)]
    ppermute x0 -> x18, starting transfers between devices: none -> 72.8 us  [shifted(): lax.ppermute(value, axis, [(i, (i + by) % size) for i in range(size)])]
    reduce_scatter x1 -> x0, waiting for transfers between devices: 57.6 us -> none  [body(): along_x = lax.psum_scatter(partial, 'x', scatter_dimension=0, tiled=True)]
    ppermute x0 -> x18, waiting for transfers between devices: none -> 57.5 us  [shifted(): lax.ppermute(value, axis, [(i, (i + by) % size) for i in range(size)])]
    unnamed x16 -> x20, local copies, waits for them, and re-layouts: 7.34 us -> 1.1 us
    all_to_all x1, starting transfers between devices: 6.82 us -> 10.2 us  [body(): shares = lax.all_to_all(along_x.reshape(N_YHI, side, columns), 'yhi', 0, 0)]
    all_to_all x1, waiting for transfers between devices: 15.5 us -> 13.4 us  [body(): shares = lax.all_to_all(along_x.reshape(N_YHI, side, columns), 'yhi', 0, 0)]
  transfers between devices with their start and end apart: 3 -> 19, of which waited for: 3 -> 12; matrix products, arithmetic and copies ran while one was open for 0% -> 1% of each run, Pallas kernels for 0% -> 0%
where the time goes in v2:
time: 167 us; the launch traced here: 166 us
  starting transfers between devices  83 us (50%)
  waiting for transfers between devices  70.9 us (42%)
  Pallas kernels  7.22 us (4%)
  other arithmetic  2.67 us (2%)
    ppermute x18, starting transfers between devices, shifted(): lax.ppermute(value, axis, [(i, (i + by) % size) for i in range(size)])  72.8 us
    ppermute x18, waiting for transfers between devices, shifted(): lax.ppermute(value, axis, [(i, (i + by) % size) for i in range(size)])  57.5 us
    all_to_all x1, waiting for transfers between devices, body(): shares = lax.all_to_all(along_x.reshape(N_YHI, side, columns), 'yhi', 0, 0)  13.4 us
    all_to_all x1, starting transfers between devices, body(): shares = lax.all_to_all(along_x.reshape(N_YHI, side, columns), 'yhi', 0, 0)  10.2 us
    pallas_call x1, Pallas kernels, partial_products(): pl.pallas_call(tiles_kernel, out_shape=(out(N_YHI // 2), out(N_YHI // 2),...  7.22 us
  transfers between devices with their start and end apart: 19, of which 12 were waited for; matrix products, arithmetic and copies ran while one was open for 1% of the time, Pallas kernels for 0%

profile of v2, /device:TPU:14, one launch (start us, length us, event | category | flops | bytes accessed | tf_op | source)
XLA Modules:
  0.0 165.9 jit_solution(17252490320592518295)
XLA Ops:
  0.0 3.6 %collective-permute-start = (bf16[256,256]{1,0:T(8,128)(2,1)}, bf16[256,256]{1,0:T(8,128)(2,1)S(1)}, u32[]{:S(2)}, u32[]{:S(2)}) collective-permute-start(bf16[256,256]{1,0:T(8,128)(2,1)} %param.7), channel_id=1, source_target_pairs={{0,512},{512,0},{1,513},{513,1},{2,514},{514,2},{3,515},{515,3},{4... | collective-permute-start | bytes 393224 | tf_op jit(solution)/shard_map/ppermute | solution.py:19
  3.6 0.9 constant_dynamic-update-slice_fusion.1
  4.5 2.8 %collective-permute-done = bf16[256,256]{1,0:T(8,128)(2,1)S(1)} collective-permute-done((bf16[256,256]{1,0:T(8,128)(2,1)}, bf16[256,256]{1,0:T(8,128)(2,1)S(1)}, u32[]{:S(2)}, u32[]{:S(2)}) %collective-permute-start) | collective-permute-done | bytes 131104 | tf_op jit(solution)/shard_map/ppermute | solution.py:19
  7.4 0.0 copy-start
  7.4 0.0 copy-start.1
  7.4 0.0 copy-start.2
  7.4 8.2 %collective-permute-start.3 = (bf16[512,256]{1,0:T(8,128)(2,1)S(1)}, bf16[512,256]{1,0:T(8,128)(2,1)S(1)}, u32[]{:S(2)}, u32[]{:S(2)}) collective-permute-start(bf16[512,256]{1,0:T(8,128)(2,1)S(1)} %get-tuple-element.17), channel_id=1, source_target_pairs={{0,128},{64,192},{128,256},{192,320},{256,384},{320,448},{384,0},{... | collective-permute-start | bytes 786440 | tf_op jit(solution)/shard_map/ppermute | solution.py:19
  15.6 10.4 %collective-permute-start.4 = (bf16[512,256]{1,0:T(8,128)(2,1)S(1)}, bf16[512,256]{1,0:T(8,128)(2,1)S(1)}, u32[]{:S(2)}, u32[]{:S(2)}) collective-permute-start(bf16[512,256]{1,0:T(8,128)(2,1)S(1)} %get-tuple-element.17), channel_id=1, source_target_pairs={{0,384},{64,448},{128,0},{192,64},{256,128},{320,192},{384,256},{4... | collective-permute-start | bytes 786440 | tf_op jit(solution)/shard_map/ppermute | solution.py:19
  26.0 4.3 %collective-permute-start.1 = (bf16[512,256]{1,0:T(8,128)(2,1)S(1)}, bf16[512,256]{1,0:T(8,128)(2,1)S(1)}, u32[]{:S(2)}, u32[]{:S(2)}) collective-permute-start(bf16[512,256]{1,0:T(8,128)(2,1)S(1)} %get-tuple-element.17), channel_id=1, source_target_pairs={{0,64},{64,128},{128,192},{192,256},{256,320},{320,384},{384,448},... | collective-permute-start | bytes 786440 | tf_op jit(solution)/shard_map/ppermute | solution.py:19
  30.3 3.4 %collective-permute-start.2 = (bf16[512,256]{1,0:T(8,128)(2,1)S(1)}, bf16[512,256]{1,0:T(8,128)(2,1)S(1)}, u32[]{:S(2)}, u32[]{:S(2)}) collective-permute-start(bf16[512,256]{1,0:T(8,128)(2,1)S(1)} %get-tuple-element.17), channel_id=1, source_target_pairs={{0,448},{64,0},{128,64},{192,128},{256,192},{320,256},{384,320},{4... | collective-permute-start | bytes 786440 | tf_op jit(solution)/shard_map/ppermute | solution.py:19
  33.7 2.4 %collective-permute-done.3 = bf16[512,256]{1,0:T(8,128)(2,1)S(1)} collective-permute-done((bf16[512,256]{1,0:T(8,128)(2,1)S(1)}, bf16[512,256]{1,0:T(8,128)(2,1)S(1)}, u32[]{:S(2)}, u32[]{:S(2)}) %collective-permute-start.3) | collective-permute-done | bytes 262176 | tf_op jit(solution)/shard_map/ppermute | solution.py:19
  36.1 1.9 %collective-permute-start.7 = (bf16[256,256]{1,0:T(8,128)(2,1)S(1)}, bf16[256,256]{1,0:T(8,128)(2,1)S(1)}, u32[]{:S(2)}, u32[]{:S(2)}) collective-permute-start(bf16[256,256]{1,0:T(8,128)(2,1)S(1)} %slice.50), channel_id=1, source_target_pairs={{0,128},{64,192},{128,256},{192,320},{256,384},{320,448},{384,0},{... | collective-permute-start | bytes 393224 | tf_op jit(solution)/shard_map/ppermute | solution.py:19
  38.0 0.0 collective-permute-done.4
  38.0 6.0 %collective-permute-start.8 = (bf16[256,256]{1,0:T(8,128)(2,1)S(1)}, bf16[256,256]{1,0:T(8,128)(2,1)S(1)}, u32[]{:S(2)}, u32[]{:S(2)}) collective-permute-start(bf16[256,256]{1,0:T(8,128)(2,1)S(1)} %slice.51), channel_id=1, source_target_pairs={{0,384},{64,448},{128,0},{192,64},{256,128},{320,192},{384,256},{4... | collective-permute-start | bytes 393224 | tf_op jit(solution)/shard_map/ppermute | solution.py:19
  44.1 2.6 %collective-permute-start.5 = (bf16[512,256]{1,0:T(8,128)(2,1)S(1)}, bf16[512,256]{1,0:T(8,128)(2,1)S(1)}, u32[]{:S(2)}, u32[]{:S(2)}) collective-permute-start(bf16[512,256]{1,0:T(8,128)(2,1)S(1)} %collective-permute-done.3), channel_id=1, source_target_pairs={{0,64},{64,128},{128,192},{192,256},{256,320},{320,384},{384,448},... | collective-permute-start | bytes 786440 | tf_op jit(solution)/shard_map/ppermute | solution.py:19
  46.7 0.0 collective-permute-done.1
  46.7 4.4 %collective-permute-start.6 = (bf16[512,256]{1,0:T(8,128)(2,1)S(1)}, bf16[512,256]{1,0:T(8,128)(2,1)S(1)}, u32[]{:S(2)}, u32[]{:S(2)}) collective-permute-start(bf16[512,256]{1,0:T(8,128)(2,1)S(1)} %collective-permute-done.4), channel_id=1, source_target_pairs={{0,448},{64,0},{128,64},{192,128},{256,192},{320,256},{384,320},{4... | collective-permute-start | bytes 786440 | tf_op jit(solution)/shard_map/ppermute | solution.py:19
  51.2 0.0 collective-permute-done.2
  51.3 2.3 %collective-permute-done.5 = bf16[512,256]{1,0:T(8,128)(2,1)S(1)} collective-permute-done((bf16[512,256]{1,0:T(8,128)(2,1)S(1)}, bf16[512,256]{1,0:T(8,128)(2,1)S(1)}, u32[]{:S(2)}, u32[]{:S(2)}) %collective-permute-start.5) | collective-permute-done | bytes 262176 | tf_op jit(solution)/shard_map/ppermute | solution.py:19
  53.6 1.4 collective-permute-done.6
  55.1 0.0 collective-permute-done.7
  55.1 0.0 collective-permute-done.8
  55.1 1.9 %collective-permute-start.9 = (bf16[4096,256]{1,0:T(8,128)(2,1)S(1)}, bf16[4096,256]{1,0:T(8,128)(2,1)S(1)}, u32[]{:S(2)}, u32[]{:S(2)}) collective-permute-start(bf16[4096,256]{1,0:T(8,128)(2,1)S(1)} %constant_dynamic-update-slice_fusion.2.near), channel_id=1, source_target_pairs={{0,32},{32,0},{1,33},{33,1},{2,34},{34,2},{3,35},{35,3},{4,36},{36... | collective-permute-start | bytes 6291464 | tf_op jit(solution)/shard_map/ppermute | solution.py:19
  57.7 3.5 %collective-permute-done.9.across = bf16[4096,256]{1,0:T(8,128)(2,1)S(1)} collective-permute-done((bf16[4096,256]{1,0:T(8,128)(2,1)S(1)}, bf16[4096,256]{1,0:T(8,128)(2,1)S(1)}, u32[]{:S(2)}, u32[]{:S(2)}) %collective-permute-start.9) | collective-permute-done | bytes 2097184 | tf_op jit(solution)/shard_map/ppermute | solution.py:19
  61.2 0.0 copy-done
  61.2 0.0 copy-done.1
  61.2 0.0 copy-done.2
  61.2 7.2 %tile_products.1 = (bf16[512,256]{1,0:T(8,128)(2,1)S(1)}, bf16[512,256]{1,0:T(8,128)(2,1)S(1)}, bf16[7168,256]{1,0:T(8,128)(2,1)S(1)}) custom-call(s32[1]{0:T(128)S(6)} %copy.18.count, s32[24]{0:T(128)S(1)} %copy-done.1, s32[24]{0:T(128)S(1)} %copy-done.2, bf16[24,256,256]{2,1,0:T(8,128)(2,1)S(1)} %copy-done, ...), custom_call_target="tpu_custom_call" | custom-call | tf_op jit(solution)/shard_map/tile_products/pallas_call | solution.py:104
  68.4 3.8 %collective-permute-start.10 = (bf16[512,256]{1,0:T(8,128)(2,1)S(1)}, bf16[512,256]{1,0:T(8,128)(2,1)S(1)}, u32[]{:S(2)}, u32[]{:S(2)}) collective-permute-start(bf16[512,256]{1,0:T(8,128)(2,1)S(1)} %get-tuple-element.9), channel_id=1, source_target_pairs={{0,1},{1,2},{2,3},{3,4},{4,5},{5,6},{6,7},{7,0},{8,9},{9,10},{10,1... | collective-permute-start | bytes 786440 | tf_op jit(solution)/shard_map/ppermute | solution.py:19
  72.2 2.2 %collective-permute-start.14 = (bf16[512,256]{1,0:T(8,128)(2,1)S(1)}, bf16[512,256]{1,0:T(8,128)(2,1)S(1)}, u32[]{:S(2)}, u32[]{:S(2)}) collective-permute-start(bf16[512,256]{1,0:T(8,128)(2,1)S(1)} %get-tuple-element.10), channel_id=1, source_target_pairs={{0,7},{1,0},{2,1},{3,2},{4,3},{5,4},{6,5},{7,6},{8,15},{9,8},{10,9... | collective-permute-start | bytes 786440 | tf_op jit(solution)/shard_map/ppermute | solution.py:19
  74.4 3.8 %collective-permute-done.10 = bf16[512,256]{1,0:T(8,128)(2,1)S(1)} collective-permute-done((bf16[512,256]{1,0:T(8,128)(2,1)S(1)}, bf16[512,256]{1,0:T(8,128)(2,1)S(1)}, u32[]{:S(2)}, u32[]{:S(2)}) %collective-permute-start.10) | collective-permute-done | bytes 262176 | tf_op jit(solution)/shard_map/ppermute | solution.py:19
  78.3 4.1 %collective-permute-done.14 = bf16[512,256]{1,0:T(8,128)(2,1)S(1)} collective-permute-done((bf16[512,256]{1,0:T(8,128)(2,1)S(1)}, bf16[512,256]{1,0:T(8,128)(2,1)S(1)}, u32[]{:S(2)}, u32[]{:S(2)}) %collective-permute-start.14) | collective-permute-done | bytes 262176 | tf_op jit(solution)/shard_map/ppermute | solution.py:19
  82.4 0.1 add_convert_fusion.6
  82.6 2.0 %collective-permute-start.11 = (bf16[1024,256]{1,0:T(8,128)(2,1)S(1)}, bf16[1024,256]{1,0:T(8,128)(2,1)S(1)}, u32[]{:S(2)}, u32[]{:S(2)}) collective-permute-start(bf16[1024,256]{1,0:T(8,128)(2,1)S(1)} %pad_maximum_fusion), channel_id=1, source_target_pairs={{0,1},{1,2},{2,3},{3,4},{4,5},{5,6},{6,7},{7,0},{8,9},{9,10},{10,1... | collective-permute-start | bytes 1572872 | tf_op jit(solution)/shard_map/ppermute | solution.py:19
  84.7 3.8 %collective-permute-start.15 = (bf16[1024,256]{1,0:T(8,128)(2,1)S(1)}, bf16[1024,256]{1,0:T(8,128)(2,1)S(1)}, u32[]{:S(2)}, u32[]{:S(2)}) collective-permute-start(bf16[1024,256]{1,0:T(8,128)(2,1)S(1)} %pad_maximum_fusion.1), channel_id=1, source_target_pairs={{0,7},{1,0},{2,1},{3,2},{4,3},{5,4},{6,5},{7,6},{8,15},{9,8},{10,9... | collective-permute-start | bytes 1572872 | tf_op jit(solution)/shard_map/ppermute | solution.py:19
  88.5 7.8 %collective-permute-done.11 = bf16[1024,256]{1,0:T(8,128)(2,1)S(1)} collective-permute-done((bf16[1024,256]{1,0:T(8,128)(2,1)S(1)}, bf16[1024,256]{1,0:T(8,128)(2,1)S(1)}, u32[]{:S(2)}, u32[]{:S(2)}) %collective-permute-start.11) | collective-permute-done | bytes 524320 | tf_op jit(solution)/shard_map/ppermute | solution.py:19
  96.3 0.1 add_convert_fusion.4
  96.4 4.7 %collective-permute-start.12 = (bf16[1024,256]{1,0:T(8,128)(2,1)S(1)}, bf16[1024,256]{1,0:T(8,128)(2,1)S(1)}, u32[]{:S(2)}, u32[]{:S(2)}) collective-permute-start(bf16[1024,256]{1,0:T(8,128)(2,1)S(1)} %add_convert_fusion.4), channel_id=1, source_target_pairs={{0,1},{1,2},{2,3},{3,4},{4,5},{5,6},{6,7},{7,0},{8,9},{9,10},{10,1... | collective-permute-start | bytes 1572872 | tf_op jit(solution)/shard_map/ppermute | solution.py:19
  101.1 0.0 collective-permute-done.15
  101.1 9.8 %collective-permute-done.12 = bf16[1024,256]{1,0:T(8,128)(2,1)S(1)} collective-permute-done((bf16[1024,256]{1,0:T(8,128)(2,1)S(1)}, bf16[1024,256]{1,0:T(8,128)(2,1)S(1)}, u32[]{:S(2)}, u32[]{:S(2)}) %collective-permute-start.12) | collective-permute-done | bytes 524320 | tf_op jit(solution)/shard_map/ppermute | solution.py:19
  110.9 0.3 add_convert_fusion.3
  111.2 1.9 %collective-permute-start.16 = (bf16[1024,256]{1,0:T(8,128)(2,1)S(1)}, bf16[1024,256]{1,0:T(8,128)(2,1)S(1)}, u32[]{:S(2)}, u32[]{:S(2)}) collective-permute-start(bf16[1024,256]{1,0:T(8,128)(2,1)S(1)} %get-tuple-element.12), channel_id=1, source_target_pairs={{0,7},{1,0},{2,1},{3,2},{4,3},{5,4},{6,5},{7,6},{8,15},{9,8},{10,9... | collective-permute-start | bytes 1572872 | tf_op jit(solution)/shard_map/ppermute | solution.py:19
  113.1 0.0 copy-start.5
  113.1 5.6 %collective-permute-start.13 = (bf16[1024,256]{1,0:T(8,128)(2,1)S(1)}, bf16[1024,256]{1,0:T(8,128)(2,1)S(1)}, u32[]{:S(2)}, u32[]{:S(2)}) collective-permute-start(bf16[1024,256]{1,0:T(8,128)(2,1)S(1)} %get-tuple-element.11), channel_id=1, source_target_pairs={{0,1},{1,2},{2,3},{3,4},{4,5},{5,6},{6,7},{7,0},{8,9},{9,10},{10,1... | collective-permute-start | bytes 1572872 | tf_op jit(solution)/shard_map/ppermute | solution.py:19
  118.7 7.7 %collective-permute-done.16 = bf16[1024,256]{1,0:T(8,128)(2,1)S(1)} collective-permute-done((bf16[1024,256]{1,0:T(8,128)(2,1)S(1)}, bf16[1024,256]{1,0:T(8,128)(2,1)S(1)}, u32[]{:S(2)}, u32[]{:S(2)}) %collective-permute-start.16) | collective-permute-done | bytes 524320 | tf_op jit(solution)/shard_map/ppermute | solution.py:19
  126.4 0.1 add_convert_fusion.1
  126.5 0.0 copy-start.3
  126.6 0.0 copy-start.4
  126.6 2.1 %collective-permute-start.17 = (bf16[1024,256]{1,0:T(8,128)(2,1)S(1)}, bf16[1024,256]{1,0:T(8,128)(2,1)S(1)}, u32[]{:S(2)}, u32[]{:S(2)}) collective-permute-start(bf16[1024,256]{1,0:T(8,128)(2,1)S(1)} %add_convert_fusion.1), channel_id=1, source_target_pairs={{0,7},{1,0},{2,1},{3,2},{4,3},{5,4},{6,5},{7,6},{8,15},{9,8},{10,9... | collective-permute-start | bytes 1572872 | tf_op jit(solution)/shard_map/ppermute | solution.py:19
  128.6 0.0 collective-permute-done.13
  128.6 11.9 %collective-permute-done.17 = bf16[1024,256]{1,0:T(8,128)(2,1)S(1)} collective-permute-done((bf16[1024,256]{1,0:T(8,128)(2,1)S(1)}, bf16[1024,256]{1,0:T(8,128)(2,1)S(1)}, u32[]{:S(2)}, u32[]{:S(2)}) %collective-permute-start.17) | collective-permute-done | bytes 524320 | tf_op jit(solution)/shard_map/ppermute | solution.py:19
  140.5 1.0 add_convert_fusion
  141.6 10.2 %all-to-all-start = ((bf16[4,256,256]{2,1,0:T(8,128)(2,1)}), bf16[4,256,256]{2,1,0:T(8,128)(2,1)S(1)}, u32[]{:S(2)}, u32[]{:S(2)}) async-start(bf16[4,256,256]{2,1,0:T(8,128)(2,1)} %bitcast), calls=%async_computation | async-start | bytes 1048576 | tf_op jit(solution)/shard_map/all_to_all | solution.py:160
  151.7 0.0 copy-done.5
  151.7 13.4 %all-to-all-done = bf16[4,256,256]{2,1,0:T(8,128)(2,1)S(1)} async-done(((bf16[4,256,256]{2,1,0:T(8,128)(2,1)}), bf16[4,256,256]{2,1,0:T(8,128)(2,1)S(1)}, u32[]{:S(2)}, u32[]{:S(2)}) %all-to-all-start) | async-done | bytes 524320 | tf_op jit(solution)/shard_map/all_to_all | solution.py:160
  165.1 0.1 convert_reduce_fusion
  165.1 0.0 copy-done.3
  165.2 0.0 copy-done.4
  165.2 0.8 add_convert_fusion.7
  (15 shorter events, 0.3 us)
Async XLA Ops:
  0.0 7.3 %collective-permute-start = (bf16[256,256]{1,0:T(8,128)(2,1)}, bf16[256,256]{1,0:T(8,128)(2,1)S(1)}, u32[]{:S(2)}, u32[]{:S(2)}) collective-permute-start(bf16[256,256]{1,0:T(8,128)(2,1)} %param.7), channel_id=1, source_target_pairs={{0,512},{512,0},{1,513},{513,1},{2,514},{514,2},{3,515},{515,3},{4... | collective-permute-start | bytes 393224 | tf_op jit(solution)/shard_map/ppermute | solution.py:19
  7.4 53.8 %copy-start = (bf16[24,256,256]{2,1,0:T(8,128)(2,1)S(1)}, bf16[24,256,256]{2,1,0:T(8,128)(2,1)}, u32[]{:S(2)}) copy-start(bf16[24,256,256]{2,1,0:T(8,128)(2,1)} %tiles.1) | copy-start | bytes 9437188
  7.4 53.8 %copy-start.1 = (s32[24]{0:T(128)S(1)}, s32[24]{0:T(128)}, u32[]{:S(2)}) copy-start(s32[24]{0:T(128)} %rows.1) | copy-start | bytes 292
  7.4 53.8 %copy-start.2 = (s32[24]{0:T(128)S(1)}, s32[24]{0:T(128)}, u32[]{:S(2)}) copy-start(s32[24]{0:T(128)} %srcs.1) | copy-start | bytes 292
  7.4 28.7 %collective-permute-start.3 = (bf16[512,256]{1,0:T(8,128)(2,1)S(1)}, bf16[512,256]{1,0:T(8,128)(2,1)S(1)}, u32[]{:S(2)}, u32[]{:S(2)}) collective-permute-start(bf16[512,256]{1,0:T(8,128)(2,1)S(1)} %get-tuple-element.17), channel_id=1, source_target_pairs={{0,128},{64,192},{128,256},{192,320},{256,384},{320,448},{384,0},{... | collective-permute-start | bytes 786440 | tf_op jit(solution)/shard_map/ppermute | solution.py:19
  15.6 22.5 %collective-permute-start.4 = (bf16[512,256]{1,0:T(8,128)(2,1)S(1)}, bf16[512,256]{1,0:T(8,128)(2,1)S(1)}, u32[]{:S(2)}, u32[]{:S(2)}) collective-permute-start(bf16[512,256]{1,0:T(8,128)(2,1)S(1)} %get-tuple-element.17), channel_id=1, source_target_pairs={{0,384},{64,448},{128,0},{192,64},{256,128},{320,192},{384,256},{4... | collective-permute-start | bytes 786440 | tf_op jit(solution)/shard_map/ppermute | solution.py:19
  26.0 20.7 %collective-permute-start.1 = (bf16[512,256]{1,0:T(8,128)(2,1)S(1)}, bf16[512,256]{1,0:T(8,128)(2,1)S(1)}, u32[]{:S(2)}, u32[]{:S(2)}) collective-permute-start(bf16[512,256]{1,0:T(8,128)(2,1)S(1)} %get-tuple-element.17), channel_id=1, source_target_pairs={{0,64},{64,128},{128,192},{192,256},{256,320},{320,384},{384,448},... | collective-permute-start | bytes 786440 | tf_op jit(solution)/shard_map/ppermute | solution.py:19
  30.3 20.9 %collective-permute-start.2 = (bf16[512,256]{1,0:T(8,128)(2,1)S(1)}, bf16[512,256]{1,0:T(8,128)(2,1)S(1)}, u32[]{:S(2)}, u32[]{:S(2)}) collective-permute-start(bf16[512,256]{1,0:T(8,128)(2,1)S(1)} %get-tuple-element.17), channel_id=1, source_target_pairs={{0,448},{64,0},{128,64},{192,128},{256,192},{320,256},{384,320},{4... | collective-permute-start | bytes 786440 | tf_op jit(solution)/shard_map/ppermute | solution.py:19
  36.1 19.0 %collective-permute-start.7 = (bf16[256,256]{1,0:T(8,128)(2,1)S(1)}, bf16[256,256]{1,0:T(8,128)(2,1)S(1)}, u32[]{:S(2)}, u32[]{:S(2)}) collective-permute-start(bf16[256,256]{1,0:T(8,128)(2,1)S(1)} %slice.50), channel_id=1, source_target_pairs={{0,128},{64,192},{128,256},{192,320},{256,384},{320,448},{384,0},{... | collective-permute-start | bytes 393224 | tf_op jit(solution)/shard_map/ppermute | solution.py:19
  38.0 17.0 %collective-permute-start.8 = (bf16[256,256]{1,0:T(8,128)(2,1)S(1)}, bf16[256,256]{1,0:T(8,128)(2,1)S(1)}, u32[]{:S(2)}, u32[]{:S(2)}) collective-permute-start(bf16[256,256]{1,0:T(8,128)(2,1)S(1)} %slice.51), channel_id=1, source_target_pairs={{0,384},{64,448},{128,0},{192,64},{256,128},{320,192},{384,256},{4... | collective-permute-start | bytes 393224 | tf_op jit(solution)/shard_map/ppermute | solution.py:19
  44.1 9.5 %collective-permute-start.5 = (bf16[512,256]{1,0:T(8,128)(2,1)S(1)}, bf16[512,256]{1,0:T(8,128)(2,1)S(1)}, u32[]{:S(2)}, u32[]{:S(2)}) collective-permute-start(bf16[512,256]{1,0:T(8,128)(2,1)S(1)} %collective-permute-done.3), channel_id=1, source_target_pairs={{0,64},{64,128},{128,192},{192,256},{256,320},{320,384},{384,448},... | collective-permute-start | bytes 786440 | tf_op jit(solution)/shard_map/ppermute | solution.py:19
  46.7 8.3 %collective-permute-start.6 = (bf16[512,256]{1,0:T(8,128)(2,1)S(1)}, bf16[512,256]{1,0:T(8,128)(2,1)S(1)}, u32[]{:S(2)}, u32[]{:S(2)}) collective-permute-start(bf16[512,256]{1,0:T(8,128)(2,1)S(1)} %collective-permute-done.4), channel_id=1, source_target_pairs={{0,448},{64,0},{128,64},{192,128},{256,192},{320,256},{384,320},{4... | collective-permute-start | bytes 786440 | tf_op jit(solution)/shard_map/ppermute | solution.py:19
  55.1 6.1 %collective-permute-start.9 = (bf16[4096,256]{1,0:T(8,128)(2,1)S(1)}, bf16[4096,256]{1,0:T(8,128)(2,1)S(1)}, u32[]{:S(2)}, u32[]{:S(2)}) collective-permute-start(bf16[4096,256]{1,0:T(8,128)(2,1)S(1)} %constant_dynamic-update-slice_fusion.2.near), channel_id=1, source_target_pairs={{0,32},{32,0},{1,33},{33,1},{2,34},{34,2},{3,35},{35,3},{4,36},{36... | collective-permute-start | bytes 6291464 | tf_op jit(solution)/shard_map/ppermute | solution.py:19
  68.4 9.9 %collective-permute-start.10 = (bf16[512,256]{1,0:T(8,128)(2,1)S(1)}, bf16[512,256]{1,0:T(8,128)(2,1)S(1)}, u32[]{:S(2)}, u32[]{:S(2)}) collective-permute-start(bf16[512,256]{1,0:T(8,128)(2,1)S(1)} %get-tuple-element.9), channel_id=1, source_target_pairs={{0,1},{1,2},{2,3},{3,4},{4,5},{5,6},{6,7},{7,0},{8,9},{9,10},{10,1... | collective-permute-start | bytes 786440 | tf_op jit(solution)/shard_map/ppermute | solution.py:19
  72.2 10.2 %collective-permute-start.14 = (bf16[512,256]{1,0:T(8,128)(2,1)S(1)}, bf16[512,256]{1,0:T(8,128)(2,1)S(1)}, u32[]{:S(2)}, u32[]{:S(2)}) collective-permute-start(bf16[512,256]{1,0:T(8,128)(2,1)S(1)} %get-tuple-element.10), channel_id=1, source_target_pairs={{0,7},{1,0},{2,1},{3,2},{4,3},{5,4},{6,5},{7,6},{8,15},{9,8},{10,9... | collective-permute-start | bytes 786440 | tf_op jit(solution)/shard_map/ppermute | solution.py:19
  82.6 13.7 %collective-permute-start.11 = (bf16[1024,256]{1,0:T(8,128)(2,1)S(1)}, bf16[1024,256]{1,0:T(8,128)(2,1)S(1)}, u32[]{:S(2)}, u32[]{:S(2)}) collective-permute-start(bf16[1024,256]{1,0:T(8,128)(2,1)S(1)} %pad_maximum_fusion), channel_id=1, source_target_pairs={{0,1},{1,2},{2,3},{3,4},{4,5},{5,6},{6,7},{7,0},{8,9},{9,10},{10,1... | collective-permute-start | bytes 1572872 | tf_op jit(solution)/shard_map/ppermute | solution.py:19
  84.7 16.4 %collective-permute-start.15 = (bf16[1024,256]{1,0:T(8,128)(2,1)S(1)}, bf16[1024,256]{1,0:T(8,128)(2,1)S(1)}, u32[]{:S(2)}, u32[]{:S(2)}) collective-permute-start(bf16[1024,256]{1,0:T(8,128)(2,1)S(1)} %pad_maximum_fusion.1), channel_id=1, source_target_pairs={{0,7},{1,0},{2,1},{3,2},{4,3},{5,4},{6,5},{7,6},{8,15},{9,8},{10,9... | collective-permute-start | bytes 1572872 | tf_op jit(solution)/shard_map/ppermute | solution.py:19
  96.4 14.5 %collective-permute-start.12 = (bf16[1024,256]{1,0:T(8,128)(2,1)S(1)}, bf16[1024,256]{1,0:T(8,128)(2,1)S(1)}, u32[]{:S(2)}, u32[]{:S(2)}) collective-permute-start(bf16[1024,256]{1,0:T(8,128)(2,1)S(1)} %add_convert_fusion.4), channel_id=1, source_target_pairs={{0,1},{1,2},{2,3},{3,4},{4,5},{5,6},{6,7},{7,0},{8,9},{9,10},{10,1... | collective-permute-start | bytes 1572872 | tf_op jit(solution)/shard_map/ppermute | solution.py:19
  111.2 15.2 %collective-permute-start.16 = (bf16[1024,256]{1,0:T(8,128)(2,1)S(1)}, bf16[1024,256]{1,0:T(8,128)(2,1)S(1)}, u32[]{:S(2)}, u32[]{:S(2)}) collective-permute-start(bf16[1024,256]{1,0:T(8,128)(2,1)S(1)} %get-tuple-element.12), channel_id=1, source_target_pairs={{0,7},{1,0},{2,1},{3,2},{4,3},{5,4},{6,5},{7,6},{8,15},{9,8},{10,9... | collective-permute-start | bytes 1572872 | tf_op jit(solution)/shard_map/ppermute | solution.py:19
  113.1 38.6 %copy-start.5 = (s32[256]{0:T(256)S(1)}, s32[256]{0:T(256)}, u32[]{:S(2)}) copy-start(s32[256]{0:T(256)} %param.13) | copy-start | bytes 3076
  113.1 15.5 %collective-permute-start.13 = (bf16[1024,256]{1,0:T(8,128)(2,1)S(1)}, bf16[1024,256]{1,0:T(8,128)(2,1)S(1)}, u32[]{:S(2)}, u32[]{:S(2)}) collective-permute-start(bf16[1024,256]{1,0:T(8,128)(2,1)S(1)} %get-tuple-element.11), channel_id=1, source_target_pairs={{0,1},{1,2},{2,3},{3,4},{4,5},{5,6},{6,7},{7,0},{8,9},{9,10},{10,1... | collective-permute-start | bytes 1572872 | tf_op jit(solution)/shard_map/ppermute | solution.py:19
  126.5 38.6 %copy-start.3 = (bf16[256,256]{1,0:T(8,128)(2,1)S(1)}, bf16[256,256]{1,0:T(8,128)(2,1)}, u32[]{:S(2)}) copy-start(bf16[256,256]{1,0:T(8,128)(2,1)} %param.7) | copy-start | bytes 393220
  126.6 38.6 %copy-start.4 = (bf16[256,256]{1,0:T(8,128)(2,1)S(1)}, bf16[256,256]{1,0:T(8,128)(2,1)}, u32[]{:S(2)}) copy-start(bf16[256,256]{1,0:T(8,128)(2,1)} %param.8) | copy-start | bytes 393220
  126.6 14.0 %collective-permute-start.17 = (bf16[1024,256]{1,0:T(8,128)(2,1)S(1)}, bf16[1024,256]{1,0:T(8,128)(2,1)S(1)}, u32[]{:S(2)}, u32[]{:S(2)}) collective-permute-start(bf16[1024,256]{1,0:T(8,128)(2,1)S(1)} %add_convert_fusion.1), channel_id=1, source_target_pairs={{0,7},{1,0},{2,1},{3,2},{4,3},{5,4},{6,5},{7,6},{8,15},{9,8},{10,9... | collective-permute-start | bytes 1572872 | tf_op jit(solution)/shard_map/ppermute | solution.py:19
  141.6 23.5 %all-to-all-start = ((bf16[4,256,256]{2,1,0:T(8,128)(2,1)}), bf16[4,256,256]{2,1,0:T(8,128)(2,1)S(1)}, u32[]{:S(2)}, u32[]{:S(2)}) async-start(bf16[4,256,256]{2,1,0:T(8,128)(2,1)} %bitcast), calls=%async_computation | async-start | bytes 1048576 | tf_op jit(solution)/shard_map/all_to_all | solution.py:160

commit v3 on v2

--- a/solution.py
+++ b/solution.py
@@ -1,3 +1,5 @@
+import functools
+
 import jax
 import jax.numpy as jnp
 from jax import lax
@@ -19,9 +21,8 @@
     return lax.ppermute(value, axis, [(i, (i + by) % size) for i in range(size)])
 
 
-def tiles_kernel(
-    count, rows, srcs, tiles, near, across, far_up, far_down, rest, head, following, acc
-):
+def tiles_kernel(chunks, count, rows, srcs, tiles, near, across, *refs):
+    outs, (head, following, acc) = refs[: len(chunks)], refs[len(chunks) :]
     side = tiles.shape[1]
     my_ylo, my_z, my_core = lax.axis_index("ylo"), lax.axis_index("z"), lax.axis_index("core")
     my_x = lax.axis_index("x")
@@ -58,9 +59,11 @@
 
         return following[s]
 
-    def fill(out, blocks, row_of):
-        def block(p, carry):
-            first = head[row_of(p)]
+    for out, (k, yhis) in zip(outs, chunks):
+        x = (my_x + k) % N_X
+
+        def block(p, carry, out=out, x=x, yhis=yhis):
+            first = head[(yhis.start + p) * N_X + x]
             where = pl.ds(pl.multiple_of(p * side, side), side)
 
             @pl.when(first < 0)
@@ -75,43 +78,33 @@
 
             return carry
 
-        lax.fori_loop(0, blocks, block, 0)
-
-    def row(k, yhi):
-        return yhi * N_X + (my_x + k) % N_X
-
-    half = N_YHI // 2
-    fill(far_up, half, lambda p: row(N_X // 2, p))
-    fill(far_down, half, lambda p: row(N_X // 2, p + half))
-
-    def rest_row(p):
-        i = p // N_YHI
-        k = jnp.where(i % 2 == 0, N_X // 2 - 1 - i // 2, N_X // 2 + 1 + i // 2)
-        return row(k, p % N_YHI)
-
-    fill(rest, (N_X - 1) * N_YHI, rest_row)
+        lax.fori_loop(0, len(yhis), block, 0)
 
 
-def partial_products(tile_blocks, tile_rows, tile_srcs, tile_count, near, across):
+def partial_products(chunks, tile_blocks, tile_rows, tile_srcs, tile_count, near, across):
     slots, side = tile_blocks.shape[:2]
     columns = near.shape[1]
     smem = pl.BlockSpec(memory_space=pltpu.SMEM)
     vmem = pl.BlockSpec(memory_space=pltpu.VMEM)
-
-    def out(tiles):
-        return jax.ShapeDtypeStruct((tiles * side, columns), jnp.bfloat16)
-
+    row_tiles = sum(len(yhis) for _, yhis in chunks)
     return pl.pallas_call(
-        tiles_kernel,
-        out_shape=(out(N_YHI // 2), out(N_YHI // 2), out((N_X - 1) * N_YHI)),
+        functools.partial(tiles_kernel, chunks),
+        out_shape=[
+            jax.ShapeDtypeStruct((len(yhis) * side, columns), jnp.bfloat16) for _, yhis in chunks
+        ],
         in_specs=[smem, smem, smem, vmem, vmem, vmem],
-        out_specs=(vmem, vmem, vmem),
+        out_specs=[vmem] * len(chunks),
         scratch_shapes=[
             pltpu.SMEM((ROW_TILES,), jnp.int32),
             pltpu.SMEM((slots,), jnp.int32),
             pltpu.VMEM((side, columns), jnp.float32),
         ],
         compiler_params=pltpu.CompilerParams(vmem_limit_bytes=24 << 20),
+        cost_estimate=pl.CostEstimate(
+            flops=2 * row_tiles * side * side * columns,
+            transcendentals=0,
+            bytes_accessed=4 * row_tiles * side * columns,
+        ),
         name="tile_products",
     )(tile_count, tile_rows, tile_srcs, tile_blocks, near, across)
 
@@ -136,16 +129,18 @@
     return total.astype(jnp.bfloat16)
 
 
-def reduce_along_x(far_up, far_down, rest):
-    chunk = 2 * far_up.shape[0]
-    half = far_up.shape[0]
-    up3, down3, up2, down2, up1, down1, own = (
-        rest[i * chunk : (i + 1) * chunk] for i in range(N_X - 1)
+def reduce_along_x(products):
+    every, half = range(N_YHI), N_YHI // 2
+    up4, down4, up3, down3 = products([(4, every[:half]), (4, every[half:]), (3, every), (5, every)])
+    up2, down2, up1, down1, own = products([(k, every) for k in (2, 6, 1, 7, 0)])
+    up, up_far = shifted(up3, "x", 1), shifted(up4, "x", 2)
+    down, down_far = shifted(down3, "x", -1), shifted(down4, "x", -2)
+    rows = up4.shape[0]
+    up = jnp.concatenate([add(up2[:rows], up[:rows], up_far), add(up2[rows:], up[rows:])], 0)
+    down = jnp.concatenate(
+        [add(down2[:rows], down[:rows]), add(down2[rows:], down[rows:], down_far)], 0
     )
-    up, down = shifted(far_up, "x", 1), shifted(far_down, "x", -1)
-    up = shifted(jnp.concatenate([add(up3[:half], up), up3[half:]], 0), "x", 1)
-    down = shifted(jnp.concatenate([down3[:half], add(down3[half:], down)], 0), "x", -1)
-    up, down = shifted(add(up2, up), "x", 1), shifted(add(down2, down), "x", -1)
+    up, down = shifted(up, "x", 1), shifted(down, "x", -1)
     up, down = shifted(add(up1, up), "x", 1), shifted(add(down1, down), "x", -1)
     return add(own, up, down)
 
@@ -153,10 +148,13 @@
 def body(flow_cols, restart, tile_blocks, tile_rows, tile_srcs, tile_count, dangling):
     side, columns = flow_cols.shape
     near, across = gather_panels(flow_cols)
-    far_up, far_down, rest = partial_products(
-        tile_blocks, tile_rows, tile_srcs, tile_count, near, across
-    )
-    along_x = reduce_along_x(far_up, far_down, rest)
+
+    def products(chunks):
+        return partial_products(
+            chunks, tile_blocks, tile_rows, tile_srcs, tile_count, near, across
+        )
+
+    along_x = reduce_along_x(products)
     shares = lax.all_to_all(along_x.reshape(N_YHI, side, columns), "yhi", 0, 0)
     summed = jnp.sum(shares.astype(jnp.float32), axis=0)
     own_flow = flow_cols.astype(jnp.float32)

time: 167 us -> 152 us (0.910)
  waiting for transfers between devices: 70.9 us -> 58.5 us
  starting transfers between devices: 83 us -> 80.3 us
    ppermute x18, waiting for transfers between devices: 57.5 us -> 46.1 us  [shifted(): lax.ppermute(value, axis, [(i, (i + by) % size) for i in range(size)])]
    all_to_all x1, starting transfers between devices: 10.2 us -> 6.56 us  [body(): shares = lax.all_to_all(along_x.reshape(N_YHI, side, columns), 'yhi', 0, 0)]
    pallas_call x1 -> x2, Pallas kernels: 7.22 us -> 7.95 us  [partial_products(): pl.pallas_call(functools.partial(tiles_kernel, chunks), out_shape=[jax.Sh...]
  transfers between devices with their start and end apart: 19 -> 19, of which waited for: 12 -> 12; matrix products, arithmetic and copies ran while one was open for 1% -> 1% of each run, Pallas kernels for 0% -> 3%
where the time goes in v3:
time: 152 us
  starting transfers between devices  80.3 us (53%)
  waiting for transfers between devices  58.5 us (38%)
  Pallas kernels  7.95 us (5%)
  other arithmetic  2.62 us (2%)
    ppermute x18, starting transfers between devices, shifted(): lax.ppermute(value, axis, [(i, (i + by) % size) for i in range(size)])  73.7 us
    ppermute x18, waiting for transfers between devices, shifted(): lax.ppermute(value, axis, [(i, (i + by) % size) for i in range(size)])  46.1 us
    all_to_all x1, waiting for transfers between devices, body(): shares = lax.all_to_all(along_x.reshape(N_YHI, side, columns), 'yhi', 0, 0)  12.4 us
    pallas_call x2, Pallas kernels, partial_products(): pl.pallas_call(functools.partial(tiles_kernel, chunks), out_shape=[jax.Sh...  7.95 us
    all_to_all x1, starting transfers between devices, body(): shares = lax.all_to_all(along_x.reshape(N_YHI, side, columns), 'yhi', 0, 0)  6.56 us
  transfers between devices with their start and end apart: 19, of which 12 were waited for; matrix products, arithmetic and copies ran while one was open for 1% of the time, Pallas kernels for 3%

profile of v3, /device:TPU:14, one launch (start us, length us, event | category | flops | bytes accessed | tf_op | source)
XLA Modules:
  0.0 151.5 jit_solution(17877000674182569404)
XLA Ops:
  0.0 3.6 %collective-permute-start = (bf16[256,256]{1,0:T(8,128)(2,1)}, bf16[256,256]{1,0:T(8,128)(2,1)S(1)}, u32[]{:S(2)}, u32[]{:S(2)}) collective-permute-start(bf16[256,256]{1,0:T(8,128)(2,1)} %param.7), channel_id=1, source_target_pairs={{0,512},{512,0},{1,513},{513,1},{2,514},{514,2},{3,515},{515,3},{4... | collective-permute-start | bytes 393224 | tf_op jit(solution)/shard_map/ppermute | solution.py:21
  3.6 0.9 constant_dynamic-update-slice_fusion.1
  4.5 2.8 %collective-permute-done = bf16[256,256]{1,0:T(8,128)(2,1)S(1)} collective-permute-done((bf16[256,256]{1,0:T(8,128)(2,1)}, bf16[256,256]{1,0:T(8,128)(2,1)S(1)}, u32[]{:S(2)}, u32[]{:S(2)}) %collective-permute-start) | collective-permute-done | bytes 131104 | tf_op jit(solution)/shard_map/ppermute | solution.py:21
  7.4 0.0 copy-start
  7.4 0.0 copy-start.1
  7.4 0.0 copy-start.2
  7.4 8.2 %collective-permute-start.3 = (bf16[512,256]{1,0:T(8,128)(2,1)S(1)}, bf16[512,256]{1,0:T(8,128)(2,1)S(1)}, u32[]{:S(2)}, u32[]{:S(2)}) collective-permute-start(bf16[512,256]{1,0:T(8,128)(2,1)S(1)} %get-tuple-element.27), channel_id=1, source_target_pairs={{0,128},{64,192},{128,256},{192,320},{256,384},{320,448},{384,0},{... | collective-permute-start | bytes 786440 | tf_op jit(solution)/shard_map/ppermute | solution.py:21
  15.6 10.4 %collective-permute-start.4 = (bf16[512,256]{1,0:T(8,128)(2,1)S(1)}, bf16[512,256]{1,0:T(8,128)(2,1)S(1)}, u32[]{:S(2)}, u32[]{:S(2)}) collective-permute-start(bf16[512,256]{1,0:T(8,128)(2,1)S(1)} %get-tuple-element.27), channel_id=1, source_target_pairs={{0,384},{64,448},{128,0},{192,64},{256,128},{320,192},{384,256},{4... | collective-permute-start | bytes 786440 | tf_op jit(solution)/shard_map/ppermute | solution.py:21
  26.0 4.3 %collective-permute-start.1 = (bf16[512,256]{1,0:T(8,128)(2,1)S(1)}, bf16[512,256]{1,0:T(8,128)(2,1)S(1)}, u32[]{:S(2)}, u32[]{:S(2)}) collective-permute-start(bf16[512,256]{1,0:T(8,128)(2,1)S(1)} %get-tuple-element.27), channel_id=1, source_target_pairs={{0,64},{64,128},{128,192},{192,256},{256,320},{320,384},{384,448},... | collective-permute-start | bytes 786440 | tf_op jit(solution)/shard_map/ppermute | solution.py:21
  30.3 3.4 %collective-permute-start.2 = (bf16[512,256]{1,0:T(8,128)(2,1)S(1)}, bf16[512,256]{1,0:T(8,128)(2,1)S(1)}, u32[]{:S(2)}, u32[]{:S(2)}) collective-permute-start(bf16[512,256]{1,0:T(8,128)(2,1)S(1)} %get-tuple-element.27), channel_id=1, source_target_pairs={{0,448},{64,0},{128,64},{192,128},{256,192},{320,256},{384,320},{4... | collective-permute-start | bytes 786440 | tf_op jit(solution)/shard_map/ppermute | solution.py:21
  33.7 2.4 %collective-permute-done.3 = bf16[512,256]{1,0:T(8,128)(2,1)S(1)} collective-permute-done((bf16[512,256]{1,0:T(8,128)(2,1)S(1)}, bf16[512,256]{1,0:T(8,128)(2,1)S(1)}, u32[]{:S(2)}, u32[]{:S(2)}) %collective-permute-start.3) | collective-permute-done | bytes 262176 | tf_op jit(solution)/shard_map/ppermute | solution.py:21
  36.1 1.9 %collective-permute-start.7 = (bf16[256,256]{1,0:T(8,128)(2,1)S(1)}, bf16[256,256]{1,0:T(8,128)(2,1)S(1)}, u32[]{:S(2)}, u32[]{:S(2)}) collective-permute-start(bf16[256,256]{1,0:T(8,128)(2,1)S(1)} %slice.40), channel_id=1, source_target_pairs={{0,128},{64,192},{128,256},{192,320},{256,384},{320,448},{384,0},{... | collective-permute-start | bytes 393224 | tf_op jit(solution)/shard_map/ppermute | solution.py:21
  38.0 0.0 collective-permute-done.4
  38.0 6.0 %collective-permute-start.8 = (bf16[256,256]{1,0:T(8,128)(2,1)S(1)}, bf16[256,256]{1,0:T(8,128)(2,1)S(1)}, u32[]{:S(2)}, u32[]{:S(2)}) collective-permute-start(bf16[256,256]{1,0:T(8,128)(2,1)S(1)} %slice.41), channel_id=1, source_target_pairs={{0,384},{64,448},{128,0},{192,64},{256,128},{320,192},{384,256},{4... | collective-permute-start | bytes 393224 | tf_op jit(solution)/shard_map/ppermute | solution.py:21
  44.1 2.6 %collective-permute-start.5 = (bf16[512,256]{1,0:T(8,128)(2,1)S(1)}, bf16[512,256]{1,0:T(8,128)(2,1)S(1)}, u32[]{:S(2)}, u32[]{:S(2)}) collective-permute-start(bf16[512,256]{1,0:T(8,128)(2,1)S(1)} %collective-permute-done.3), channel_id=1, source_target_pairs={{0,64},{64,128},{128,192},{192,256},{256,320},{320,384},{384,448},... | collective-permute-start | bytes 786440 | tf_op jit(solution)/shard_map/ppermute | solution.py:21
  46.7 0.0 collective-permute-done.1
  46.7 4.4 %collective-permute-start.6 = (bf16[512,256]{1,0:T(8,128)(2,1)S(1)}, bf16[512,256]{1,0:T(8,128)(2,1)S(1)}, u32[]{:S(2)}, u32[]{:S(2)}) collective-permute-start(bf16[512,256]{1,0:T(8,128)(2,1)S(1)} %collective-permute-done.4), channel_id=1, source_target_pairs={{0,448},{64,0},{128,64},{192,128},{256,192},{320,256},{384,320},{4... | collective-permute-start | bytes 786440 | tf_op jit(solution)/shard_map/ppermute | solution.py:21
  51.2 0.0 collective-permute-done.2
  51.3 2.3 %collective-permute-done.5 = bf16[512,256]{1,0:T(8,128)(2,1)S(1)} collective-permute-done((bf16[512,256]{1,0:T(8,128)(2,1)S(1)}, bf16[512,256]{1,0:T(8,128)(2,1)S(1)}, u32[]{:S(2)}, u32[]{:S(2)}) %collective-permute-start.5) | collective-permute-done | bytes 262176 | tf_op jit(solution)/shard_map/ppermute | solution.py:21
  53.6 1.4 collective-permute-done.6
  55.1 0.0 collective-permute-done.7
  55.1 0.0 collective-permute-done.8
  55.1 1.9 %collective-permute-start.9 = (bf16[4096,256]{1,0:T(8,128)(2,1)S(1)}, bf16[4096,256]{1,0:T(8,128)(2,1)S(1)}, u32[]{:S(2)}, u32[]{:S(2)}) collective-permute-start(bf16[4096,256]{1,0:T(8,128)(2,1)S(1)} %constant_dynamic-update-slice_fusion.2.near), channel_id=1, source_target_pairs={{0,32},{32,0},{1,33},{33,1},{2,34},{34,2},{3,35},{35,3},{4,36},{36... | collective-permute-start | bytes 6291464 | tf_op jit(solution)/shard_map/ppermute | solution.py:21
  57.7 3.5 %collective-permute-done.9.across = bf16[4096,256]{1,0:T(8,128)(2,1)S(1)} collective-permute-done((bf16[4096,256]{1,0:T(8,128)(2,1)S(1)}, bf16[4096,256]{1,0:T(8,128)(2,1)S(1)}, u32[]{:S(2)}, u32[]{:S(2)}) %collective-permute-start.9) | collective-permute-done | bytes 2097184 | tf_op jit(solution)/shard_map/ppermute | solution.py:21
  61.2 0.0 copy-done
  61.2 0.0 copy-done.1
  61.2 0.0 copy-done.2
  61.2 2.7 %tile_products.3 = (bf16[512,256]{1,0:T(8,128)(2,1)S(1)}, bf16[512,256]{1,0:T(8,128)(2,1)S(1)}, bf16[1024,256]{1,0:T(8,128)(2,1)S(1)}, bf16[1024,256]{1,0:T(8,128)(2,1)S(1)}) custom-call(s32[1]{0:T(128)S(6)} %copy.18.count, s32[24]{0:T(128)S(1)} %copy-done.1, s32[24]{0:T(128)S(1)} %copy-done.2, bf16[24,256,256]{2,1,0:T(8,128)(2,1)S(1)} %copy-done, ...), custom_call_target="tpu_custom_call" | custom-call | flops 402653184 | bytes 3145728 | tf_op jit(solution)/shard_map/tile_products/pallas_call | solution.py:90
  63.9 3.7 %collective-permute-start.10 = (bf16[1024,256]{1,0:T(8,128)(2,1)S(1)}, bf16[1024,256]{1,0:T(8,128)(2,1)S(1)}, u32[]{:S(2)}, u32[]{:S(2)}) collective-permute-start(bf16[1024,256]{1,0:T(8,128)(2,1)S(1)} %get-tuple-element.17), channel_id=1, source_target_pairs={{0,1},{1,2},{2,3},{3,4},{4,5},{5,6},{6,7},{7,0},{8,9},{9,10},{10,1... | collective-permute-start | bytes 1572872 | tf_op jit(solution)/shard_map/ppermute | solution.py:21
  67.6 4.2 %collective-permute-start.11 = (bf16[512,256]{1,0:T(8,128)(2,1)S(1)}, bf16[512,256]{1,0:T(8,128)(2,1)S(1)}, u32[]{:S(2)}, u32[]{:S(2)}) collective-permute-start(bf16[512,256]{1,0:T(8,128)(2,1)S(1)} %get-tuple-element.18), channel_id=1, source_target_pairs={{0,2},{1,3},{2,4},{3,5},{4,6},{5,7},{6,0},{7,1},{8,10},{9,11},{10,... | collective-permute-start | bytes 786440 | tf_op jit(solution)/shard_map/ppermute | solution.py:21
  71.9 1.9 %collective-permute-start.14 = (bf16[1024,256]{1,0:T(8,128)(2,1)S(1)}, bf16[1024,256]{1,0:T(8,128)(2,1)S(1)}, u32[]{:S(2)}, u32[]{:S(2)}) collective-permute-start(bf16[1024,256]{1,0:T(8,128)(2,1)S(1)} %get-tuple-element.21), channel_id=1, source_target_pairs={{0,7},{1,0},{2,1},{3,2},{4,3},{5,4},{6,5},{7,6},{8,15},{9,8},{10,9... | collective-permute-start | bytes 1572872 | tf_op jit(solution)/shard_map/ppermute | solution.py:21
  73.8 2.8 %collective-permute-start.15 = (bf16[512,256]{1,0:T(8,128)(2,1)S(1)}, bf16[512,256]{1,0:T(8,128)(2,1)S(1)}, u32[]{:S(2)}, u32[]{:S(2)}) collective-permute-start(bf16[512,256]{1,0:T(8,128)(2,1)S(1)} %get-tuple-element.22), channel_id=1, source_target_pairs={{0,6},{1,7},{2,0},{3,1},{4,2},{5,3},{6,4},{7,5},{8,14},{9,15},{10,... | collective-permute-start | bytes 786440 | tf_op jit(solution)/shard_map/ppermute | solution.py:21
  76.6 5.3 %tile_products.2 = (bf16[1024,256]{1,0:T(8,128)(2,1)S(1)}, bf16[1024,256]{1,0:T(8,128)(2,1)S(1)}, bf16[1024,256]{1,0:T(8,128)(2,1)S(1)}, bf16[1024,256]{1,0:T(8,128)(2,1)S(1)}, bf16[1024,256]{1,0:T(8,128)(2,1)S(1)}) custom-call(s32[1]{0:T(128)S(6)} %copy.18.count, s32[24]{0:T(128)S(1)} %copy-done.1, s32[24]{0:T(128)S(1)} %copy-done.2, ...), custom_call_target="tpu_custom_call" | custom-call | flops 671088640 | bytes 5242880 | tf_op jit(solution)/shard_map/tile_products/pallas_call | solution.py:90
  81.9 11.0 %collective-permute-done.11 = bf16[512,256]{1,0:T(8,128)(2,1)S(1)} collective-permute-done((bf16[512,256]{1,0:T(8,128)(2,1)S(1)}, bf16[512,256]{1,0:T(8,128)(2,1)S(1)}, u32[]{:S(2)}, u32[]{:S(2)}) %collective-permute-start.11) | collective-permute-done | bytes 262176 | tf_op jit(solution)/shard_map/ppermute | solution.py:21
  93.0 0.0 collective-permute-done.10
  93.0 0.2 add_convert_fusion.6
  93.2 1.9 %collective-permute-start.12 = (bf16[1024,256]{1,0:T(8,128)(2,1)S(1)}, bf16[1024,256]{1,0:T(8,128)(2,1)S(1)}, u32[]{:S(2)}, u32[]{:S(2)}) collective-permute-start(bf16[1024,256]{1,0:T(8,128)(2,1)S(1)} %pad_maximum_fusion), channel_id=1, source_target_pairs={{0,1},{1,2},{2,3},{3,4},{4,5},{5,6},{6,7},{7,0},{8,9},{9,10},{10,1... | collective-permute-start | bytes 1572872 | tf_op jit(solution)/shard_map/ppermute | solution.py:21
  95.1 0.3 collective-permute-done.15
  95.5 0.0 collective-permute-done.14
  95.5 0.2 add_convert_fusion.4
  95.7 6.8 %collective-permute-start.16 = (bf16[1024,256]{1,0:T(8,128)(2,1)S(1)}, bf16[1024,256]{1,0:T(8,128)(2,1)S(1)}, u32[]{:S(2)}, u32[]{:S(2)}) collective-permute-start(bf16[1024,256]{1,0:T(8,128)(2,1)S(1)} %pad_maximum_fusion.1), channel_id=1, source_target_pairs={{0,7},{1,0},{2,1},{3,2},{4,3},{5,4},{6,5},{7,6},{8,15},{9,8},{10,9... | collective-permute-start | bytes 1572872 | tf_op jit(solution)/shard_map/ppermute | solution.py:21
  102.5 6.1 %collective-permute-done.12 = bf16[1024,256]{1,0:T(8,128)(2,1)S(1)} collective-permute-done((bf16[1024,256]{1,0:T(8,128)(2,1)S(1)}, bf16[1024,256]{1,0:T(8,128)(2,1)S(1)}, u32[]{:S(2)}, u32[]{:S(2)}) %collective-permute-start.12) | collective-permute-done | bytes 524320 | tf_op jit(solution)/shard_map/ppermute | solution.py:21
  108.7 0.1 add_convert_fusion.2
  108.8 3.4 %collective-permute-start.13 = (bf16[1024,256]{1,0:T(8,128)(2,1)S(1)}, bf16[1024,256]{1,0:T(8,128)(2,1)S(1)}, u32[]{:S(2)}, u32[]{:S(2)}) collective-permute-start(bf16[1024,256]{1,0:T(8,128)(2,1)S(1)} %add_convert_fusion.2), channel_id=1, source_target_pairs={{0,1},{1,2},{2,3},{3,4},{4,5},{5,6},{6,7},{7,0},{8,9},{9,10},{10,1... | collective-permute-start | bytes 1572872 | tf_op jit(solution)/shard_map/ppermute | solution.py:21
  112.2 2.6 %collective-permute-done.16 = bf16[1024,256]{1,0:T(8,128)(2,1)S(1)} collective-permute-done((bf16[1024,256]{1,0:T(8,128)(2,1)S(1)}, bf16[1024,256]{1,0:T(8,128)(2,1)S(1)}, u32[]{:S(2)}, u32[]{:S(2)}) %collective-permute-start.16) | collective-permute-done | bytes 524320 | tf_op jit(solution)/shard_map/ppermute | solution.py:21
  114.8 0.0 copy-start.5
  114.8 0.1 add_convert_fusion.1
  115.0 0.0 copy-start.3
  115.0 0.0 copy-start.4
  115.0 2.1 %collective-permute-start.17 = (bf16[1024,256]{1,0:T(8,128)(2,1)S(1)}, bf16[1024,256]{1,0:T(8,128)(2,1)S(1)}, u32[]{:S(2)}, u32[]{:S(2)}) collective-permute-start(bf16[1024,256]{1,0:T(8,128)(2,1)S(1)} %add_convert_fusion.1), channel_id=1, source_target_pairs={{0,7},{1,0},{2,1},{3,2},{4,3},{5,4},{6,5},{7,6},{8,15},{9,8},{10,9... | collective-permute-start | bytes 1572872 | tf_op jit(solution)/shard_map/ppermute | solution.py:21
  117.0 7.0 %collective-permute-done.13 = bf16[1024,256]{1,0:T(8,128)(2,1)S(1)} collective-permute-done((bf16[1024,256]{1,0:T(8,128)(2,1)S(1)}, bf16[1024,256]{1,0:T(8,128)(2,1)S(1)}, u32[]{:S(2)}, u32[]{:S(2)}) %collective-permute-start.13) | collective-permute-done | bytes 524320 | tf_op jit(solution)/shard_map/ppermute | solution.py:21
  124.0 6.6 %collective-permute-done.17 = bf16[1024,256]{1,0:T(8,128)(2,1)S(1)} collective-permute-done((bf16[1024,256]{1,0:T(8,128)(2,1)S(1)}, bf16[1024,256]{1,0:T(8,128)(2,1)S(1)}, u32[]{:S(2)}, u32[]{:S(2)}) %collective-permute-start.17) | collective-permute-done | bytes 524320 | tf_op jit(solution)/shard_map/ppermute | solution.py:21
  130.7 1.0 add_convert_fusion
  131.7 6.6 %all-to-all-start = ((bf16[4,256,256]{2,1,0:T(8,128)(2,1)}), bf16[4,256,256]{2,1,0:T(8,128)(2,1)S(1)}, u32[]{:S(2)}, u32[]{:S(2)}) async-start(bf16[4,256,256]{2,1,0:T(8,128)(2,1)} %bitcast), calls=%async_computation | async-start | bytes 1048576 | tf_op jit(solution)/shard_map/all_to_all | solution.py:158
  138.3 0.0 copy-done.5
  138.3 12.4 %all-to-all-done = bf16[4,256,256]{2,1,0:T(8,128)(2,1)S(1)} async-done(((bf16[4,256,256]{2,1,0:T(8,128)(2,1)}), bf16[4,256,256]{2,1,0:T(8,128)(2,1)S(1)}, u32[]{:S(2)}, u32[]{:S(2)}) %all-to-all-start) | async-done | bytes 524320 | tf_op jit(solution)/shard_map/all_to_all | solution.py:158
  150.6 0.1 convert_reduce_fusion
  150.7 0.0 copy-done.3
  150.7 0.0 copy-done.4
  150.7 0.8 add_convert_fusion.7
  (14 shorter events, 0.2 us)
Async XLA Ops:
  0.0 7.3 %collective-permute-start = (bf16[256,256]{1,0:T(8,128)(2,1)}, bf16[256,256]{1,0:T(8,128)(2,1)S(1)}, u32[]{:S(2)}, u32[]{:S(2)}) collective-permute-start(bf16[256,256]{1,0:T(8,128)(2,1)} %param.7), channel_id=1, source_target_pairs={{0,512},{512,0},{1,513},{513,1},{2,514},{514,2},{3,515},{515,3},{4... | collective-permute-start | bytes 393224 | tf_op jit(solution)/shard_map/ppermute | solution.py:21
  7.4 53.8 %copy-start = (bf16[24,256,256]{2,1,0:T(8,128)(2,1)S(1)}, bf16[24,256,256]{2,1,0:T(8,128)(2,1)}, u32[]{:S(2)}) copy-start(bf16[24,256,256]{2,1,0:T(8,128)(2,1)} %tiles.3) | copy-start | bytes 9437188
  7.4 53.8 %copy-start.1 = (s32[24]{0:T(128)S(1)}, s32[24]{0:T(128)}, u32[]{:S(2)}) copy-start(s32[24]{0:T(128)} %rows.3) | copy-start | bytes 292
  7.4 53.8 %copy-start.2 = (s32[24]{0:T(128)S(1)}, s32[24]{0:T(128)}, u32[]{:S(2)}) copy-start(s32[24]{0:T(128)} %srcs.3) | copy-start | bytes 292
  7.4 28.7 %collective-permute-start.3 = (bf16[512,256]{1,0:T(8,128)(2,1)S(1)}, bf16[512,256]{1,0:T(8,128)(2,1)S(1)}, u32[]{:S(2)}, u32[]{:S(2)}) collective-permute-start(bf16[512,256]{1,0:T(8,128)(2,1)S(1)} %get-tuple-element.27), channel_id=1, source_target_pairs={{0,128},{64,192},{128,256},{192,320},{256,384},{320,448},{384,0},{... | collective-permute-start | bytes 786440 | tf_op jit(solution)/shard_map/ppermute | solution.py:21
  15.6 22.5 %collective-permute-start.4 = (bf16[512,256]{1,0:T(8,128)(2,1)S(1)}, bf16[512,256]{1,0:T(8,128)(2,1)S(1)}, u32[]{:S(2)}, u32[]{:S(2)}) collective-permute-start(bf16[512,256]{1,0:T(8,128)(2,1)S(1)} %get-tuple-element.27), channel_id=1, source_target_pairs={{0,384},{64,448},{128,0},{192,64},{256,128},{320,192},{384,256},{4... | collective-permute-start | bytes 786440 | tf_op jit(solution)/shard_map/ppermute | solution.py:21
  26.0 20.7 %collective-permute-start.1 = (bf16[512,256]{1,0:T(8,128)(2,1)S(1)}, bf16[512,256]{1,0:T(8,128)(2,1)S(1)}, u32[]{:S(2)}, u32[]{:S(2)}) collective-permute-start(bf16[512,256]{1,0:T(8,128)(2,1)S(1)} %get-tuple-element.27), channel_id=1, source_target_pairs={{0,64},{64,128},{128,192},{192,256},{256,320},{320,384},{384,448},... | collective-permute-start | bytes 786440 | tf_op jit(solution)/shard_map/ppermute | solution.py:21
  30.3 20.9 %collective-permute-start.2 = (bf16[512,256]{1,0:T(8,128)(2,1)S(1)}, bf16[512,256]{1,0:T(8,128)(2,1)S(1)}, u32[]{:S(2)}, u32[]{:S(2)}) collective-permute-start(bf16[512,256]{1,0:T(8,128)(2,1)S(1)} %get-tuple-element.27), channel_id=1, source_target_pairs={{0,448},{64,0},{128,64},{192,128},{256,192},{320,256},{384,320},{4... | collective-permute-start | bytes 786440 | tf_op jit(solution)/shard_map/ppermute | solution.py:21
  36.1 19.0 %collective-permute-start.7 = (bf16[256,256]{1,0:T(8,128)(2,1)S(1)}, bf16[256,256]{1,0:T(8,128)(2,1)S(1)}, u32[]{:S(2)}, u32[]{:S(2)}) collective-permute-start(bf16[256,256]{1,0:T(8,128)(2,1)S(1)} %slice.40), channel_id=1, source_target_pairs={{0,128},{64,192},{128,256},{192,320},{256,384},{320,448},{384,0},{... | collective-permute-start | bytes 393224 | tf_op jit(solution)/shard_map/ppermute | solution.py:21
  38.0 17.0 %collective-permute-start.8 = (bf16[256,256]{1,0:T(8,128)(2,1)S(1)}, bf16[256,256]{1,0:T(8,128)(2,1)S(1)}, u32[]{:S(2)}, u32[]{:S(2)}) collective-permute-start(bf16[256,256]{1,0:T(8,128)(2,1)S(1)} %slice.41), channel_id=1, source_target_pairs={{0,384},{64,448},{128,0},{192,64},{256,128},{320,192},{384,256},{4... | collective-permute-start | bytes 393224 | tf_op jit(solution)/shard_map/ppermute | solution.py:21
  44.1 9.5 %collective-permute-start.5 = (bf16[512,256]{1,0:T(8,128)(2,1)S(1)}, bf16[512,256]{1,0:T(8,128)(2,1)S(1)}, u32[]{:S(2)}, u32[]{:S(2)}) collective-permute-start(bf16[512,256]{1,0:T(8,128)(2,1)S(1)} %collective-permute-done.3), channel_id=1, source_target_pairs={{0,64},{64,128},{128,192},{192,256},{256,320},{320,384},{384,448},... | collective-permute-start | bytes 786440 | tf_op jit(solution)/shard_map/ppermute | solution.py:21
  46.7 8.3 %collective-permute-start.6 = (bf16[512,256]{1,0:T(8,128)(2,1)S(1)}, bf16[512,256]{1,0:T(8,128)(2,1)S(1)}, u32[]{:S(2)}, u32[]{:S(2)}) collective-permute-start(bf16[512,256]{1,0:T(8,128)(2,1)S(1)} %collective-permute-done.4), channel_id=1, source_target_pairs={{0,448},{64,0},{128,64},{192,128},{256,192},{320,256},{384,320},{4... | collective-permute-start | bytes 786440 | tf_op jit(solution)/shard_map/ppermute | solution.py:21
  55.1 6.1 %collective-permute-start.9 = (bf16[4096,256]{1,0:T(8,128)(2,1)S(1)}, bf16[4096,256]{1,0:T(8,128)(2,1)S(1)}, u32[]{:S(2)}, u32[]{:S(2)}) collective-permute-start(bf16[4096,256]{1,0:T(8,128)(2,1)S(1)} %constant_dynamic-update-slice_fusion.2.near), channel_id=1, source_target_pairs={{0,32},{32,0},{1,33},{33,1},{2,34},{34,2},{3,35},{35,3},{4,36},{36... | collective-permute-start | bytes 6291464 | tf_op jit(solution)/shard_map/ppermute | solution.py:21
  63.9 29.1 %collective-permute-start.10 = (bf16[1024,256]{1,0:T(8,128)(2,1)S(1)}, bf16[1024,256]{1,0:T(8,128)(2,1)S(1)}, u32[]{:S(2)}, u32[]{:S(2)}) collective-permute-start(bf16[1024,256]{1,0:T(8,128)(2,1)S(1)} %get-tuple-element.17), channel_id=1, source_target_pairs={{0,1},{1,2},{2,3},{3,4},{4,5},{5,6},{6,7},{7,0},{8,9},{9,10},{10,1... | collective-permute-start | bytes 1572872 | tf_op jit(solution)/shard_map/ppermute | solution.py:21
  67.6 25.3 %collective-permute-start.11 = (bf16[512,256]{1,0:T(8,128)(2,1)S(1)}, bf16[512,256]{1,0:T(8,128)(2,1)S(1)}, u32[]{:S(2)}, u32[]{:S(2)}) collective-permute-start(bf16[512,256]{1,0:T(8,128)(2,1)S(1)} %get-tuple-element.18), channel_id=1, source_target_pairs={{0,2},{1,3},{2,4},{3,5},{4,6},{5,7},{6,0},{7,1},{8,10},{9,11},{10,... | collective-permute-start | bytes 786440 | tf_op jit(solution)/shard_map/ppermute | solution.py:21
  71.9 23.6 %collective-permute-start.14 = (bf16[1024,256]{1,0:T(8,128)(2,1)S(1)}, bf16[1024,256]{1,0:T(8,128)(2,1)S(1)}, u32[]{:S(2)}, u32[]{:S(2)}) collective-permute-start(bf16[1024,256]{1,0:T(8,128)(2,1)S(1)} %get-tuple-element.21), channel_id=1, source_target_pairs={{0,7},{1,0},{2,1},{3,2},{4,3},{5,4},{6,5},{7,6},{8,15},{9,8},{10,9... | collective-permute-start | bytes 1572872 | tf_op jit(solution)/shard_map/ppermute | solution.py:21
  73.8 21.7 %collective-permute-start.15 = (bf16[512,256]{1,0:T(8,128)(2,1)S(1)}, bf16[512,256]{1,0:T(8,128)(2,1)S(1)}, u32[]{:S(2)}, u32[]{:S(2)}) collective-permute-start(bf16[512,256]{1,0:T(8,128)(2,1)S(1)} %get-tuple-element.22), channel_id=1, source_target_pairs={{0,6},{1,7},{2,0},{3,1},{4,2},{5,3},{6,4},{7,5},{8,14},{9,15},{10,... | collective-permute-start | bytes 786440 | tf_op jit(solution)/shard_map/ppermute | solution.py:21
  93.2 15.5 %collective-permute-start.12 = (bf16[1024,256]{1,0:T(8,128)(2,1)S(1)}, bf16[1024,256]{1,0:T(8,128)(2,1)S(1)}, u32[]{:S(2)}, u32[]{:S(2)}) collective-permute-start(bf16[1024,256]{1,0:T(8,128)(2,1)S(1)} %pad_maximum_fusion), channel_id=1, source_target_pairs={{0,1},{1,2},{2,3},{3,4},{4,5},{5,6},{6,7},{7,0},{8,9},{9,10},{10,1... | collective-permute-start | bytes 1572872 | tf_op jit(solution)/shard_map/ppermute | solution.py:21
  95.7 19.1 %collective-permute-start.16 = (bf16[1024,256]{1,0:T(8,128)(2,1)S(1)}, bf16[1024,256]{1,0:T(8,128)(2,1)S(1)}, u32[]{:S(2)}, u32[]{:S(2)}) collective-permute-start(bf16[1024,256]{1,0:T(8,128)(2,1)S(1)} %pad_maximum_fusion.1), channel_id=1, source_target_pairs={{0,7},{1,0},{2,1},{3,2},{4,3},{5,4},{6,5},{7,6},{8,15},{9,8},{10,9... | collective-permute-start | bytes 1572872 | tf_op jit(solution)/shard_map/ppermute | solution.py:21
  108.8 15.2 %collective-permute-start.13 = (bf16[1024,256]{1,0:T(8,128)(2,1)S(1)}, bf16[1024,256]{1,0:T(8,128)(2,1)S(1)}, u32[]{:S(2)}, u32[]{:S(2)}) collective-permute-start(bf16[1024,256]{1,0:T(8,128)(2,1)S(1)} %add_convert_fusion.2), channel_id=1, source_target_pairs={{0,1},{1,2},{2,3},{3,4},{4,5},{5,6},{6,7},{7,0},{8,9},{9,10},{10,1... | collective-permute-start | bytes 1572872 | tf_op jit(solution)/shard_map/ppermute | solution.py:21
  114.8 23.4 %copy-start.5 = (s32[256]{0:T(256)S(1)}, s32[256]{0:T(256)}, u32[]{:S(2)}) copy-start(s32[256]{0:T(256)} %param.13) | copy-start | bytes 3076
  115.0 35.8 %copy-start.3 = (bf16[256,256]{1,0:T(8,128)(2,1)S(1)}, bf16[256,256]{1,0:T(8,128)(2,1)}, u32[]{:S(2)}) copy-start(bf16[256,256]{1,0:T(8,128)(2,1)} %param.7) | copy-start | bytes 393220
  115.0 35.7 %copy-start.4 = (bf16[256,256]{1,0:T(8,128)(2,1)S(1)}, bf16[256,256]{1,0:T(8,128)(2,1)}, u32[]{:S(2)}) copy-start(bf16[256,256]{1,0:T(8,128)(2,1)} %param.8) | copy-start | bytes 393220
  115.0 15.7 %collective-permute-start.17 = (bf16[1024,256]{1,0:T(8,128)(2,1)S(1)}, bf16[1024,256]{1,0:T(8,128)(2,1)S(1)}, u32[]{:S(2)}, u32[]{:S(2)}) collective-permute-start(bf16[1024,256]{1,0:T(8,128)(2,1)S(1)} %add_convert_fusion.1), channel_id=1, source_target_pairs={{0,7},{1,0},{2,1},{3,2},{4,3},{5,4},{6,5},{7,6},{8,15},{9,8},{10,9... | collective-permute-start | bytes 1572872 | tf_op jit(solution)/shard_map/ppermute | solution.py:21
  131.7 18.9 %all-to-all-start = ((bf16[4,256,256]{2,1,0:T(8,128)(2,1)}), bf16[4,256,256]{2,1,0:T(8,128)(2,1)S(1)}, u32[]{:S(2)}, u32[]{:S(2)}) async-start(bf16[4,256,256]{2,1,0:T(8,128)(2,1)} %bitcast), calls=%async_computation | async-start | bytes 1048576 | tf_op jit(solution)/shard_map/all_to_all | solution.py:158

commit v4 on v3

--- a/solution.py
+++ b/solution.py
@@ -131,10 +131,11 @@
 
 def reduce_along_x(products):
     every, half = range(N_YHI), N_YHI // 2
-    up4, down4, up3, down3 = products([(4, every[:half]), (4, every[half:]), (3, every), (5, every)])
+    up4, up3 = products([(4, every[:half]), (3, every)])
+    down4, down3 = products([(4, every[half:]), (5, every)])
     up2, down2, up1, down1, own = products([(k, every) for k in (2, 6, 1, 7, 0)])
-    up, up_far = shifted(up3, "x", 1), shifted(up4, "x", 2)
-    down, down_far = shifted(down3, "x", -1), shifted(down4, "x", -2)
+    up, down = shifted(up3, "x", 1), shifted(down3, "x", -1)
+    up_far, down_far = shifted(up4, "x", 2), shifted(down4, "x", -2)
     rows = up4.shape[0]
     up = jnp.concatenate([add(up2[:rows], up[:rows], up_far), add(up2[rows:], up[rows:])], 0)
     down = jnp.concatenate(
@@ -154,13 +155,13 @@
             chunks, tile_blocks, tile_rows, tile_srcs, tile_count, near, across
         )
 
-    along_x = reduce_along_x(products)
-    shares = lax.all_to_all(along_x.reshape(N_YHI, side, columns), "yhi", 0, 0)
-    summed = jnp.sum(shares.astype(jnp.float32), axis=0)
     own_flow = flow_cols.astype(jnp.float32)
     mask_col = dangling.astype(jnp.float32)[:, None]
-    result = DAMP * (summed + mask_col * own_flow) + (1.0 - DAMP) * restart.astype(jnp.float32)
-    return result.astype(jnp.bfloat16)
+    constant = DAMP * (mask_col * own_flow) + (1.0 - DAMP) * restart.astype(jnp.float32)
+    along_x, constant = lax.optimization_barrier((reduce_along_x(products), constant))
+    shares = lax.all_to_all(along_x, "yhi", 0, 0, tiled=True).reshape(N_YHI, side, columns)
+    summed = jnp.sum(shares.astype(jnp.float32), axis=0)
+    return (DAMP * summed + constant).astype(jnp.bfloat16)
 
 
 def solution(mesh):

time: 152 us -> 155 us (1.020)
  blocking collectives: 0 us -> 23.3 us
  waiting for transfers between devices: 58.5 us -> 46.1 us
  starting transfers between devices: 80.3 us -> 72.7 us
    all_to_all x0 -> x1, blocking collectives: none -> 23.3 us  [body(): lax.all_to_all(along_x, 'yhi', 0, 0, tiled=True)]
    all_to_all x1 -> x0, waiting for transfers between devices: 12.4 us -> none  [body(): shares = lax.all_to_all(along_x.reshape(N_YHI, side, columns), 'yhi', 0, 0)]
    all_to_all x1 -> x0, starting transfers between devices: 6.56 us -> none  [body(): shares = lax.all_to_all(along_x.reshape(N_YHI, side, columns), 'yhi', 0, 0)]
    pallas_call x2 -> x3, Pallas kernels: 7.95 us -> 8.4 us  [partial_products(): pl.pallas_call(functools.partial(tiles_kernel, chunks), out_shape=[jax.Sh...]
  transfers between devices with their start and end apart: 19 -> 18, of which waited for: 12 -> 11; matrix products, arithmetic and copies ran while one was open for 1% -> 1% of each run, Pallas kernels for 3% -> 4%
where the time goes in v4:
time: 155 us
  starting transfers between devices  72.7 us (47%)
  waiting for transfers between devices  46.1 us (30%)
  blocking collectives  23.3 us (15%)
  Pallas kernels  8.4 us (5%)
  other arithmetic  1.82 us (1%)
    ppermute x18, starting transfers between devices, shifted(): lax.ppermute(value, axis, [(i, (i + by) % size) for i in range(size)])  72.7 us
    ppermute x18, waiting for transfers between devices, shifted(): lax.ppermute(value, axis, [(i, (i + by) % size) for i in range(size)])  46.1 us
    all_to_all x1, blocking collectives, body(): lax.all_to_all(along_x, 'yhi', 0, 0, tiled=True)  23.3 us
    pallas_call x3, Pallas kernels, partial_products(): pl.pallas_call(functools.partial(tiles_kernel, chunks), out_shape=[jax.Sh...  8.4 us
  transfers between devices with their start and end apart: 18, of which 11 were waited for; matrix products, arithmetic and copies ran while one was open for 1% of the time, Pallas kernels for 4%

profile of v4, /device:TPU:14, one launch (start us, length us, event | category | flops | bytes accessed | tf_op | source)
XLA Modules:
  0.0 154.6 jit_solution(11885524199226750963)
XLA Ops:
  0.0 3.6 %collective-permute-start = (bf16[256,256]{1,0:T(8,128)(2,1)}, bf16[256,256]{1,0:T(8,128)(2,1)S(1)}, u32[]{:S(2)}, u32[]{:S(2)}) collective-permute-start(bf16[256,256]{1,0:T(8,128)(2,1)} %param.7), channel_id=1, source_target_pairs={{0,512},{512,0},{1,513},{513,1},{2,514},{514,2},{3,515},{515,3},{4... | collective-permute-start | bytes 393224 | tf_op jit(solution)/shard_map/ppermute | solution.py:21
  3.6 0.9 constant_dynamic-update-slice_fusion.1
  4.5 2.8 %collective-permute-done = bf16[256,256]{1,0:T(8,128)(2,1)S(1)} collective-permute-done((bf16[256,256]{1,0:T(8,128)(2,1)}, bf16[256,256]{1,0:T(8,128)(2,1)S(1)}, u32[]{:S(2)}, u32[]{:S(2)}) %collective-permute-start) | collective-permute-done | bytes 131104 | tf_op jit(solution)/shard_map/ppermute | solution.py:21
  7.4 0.0 copy-start
  7.4 0.0 copy-start.1
  7.4 0.0 copy-start.2
  7.4 8.2 %collective-permute-start.3 = (bf16[512,256]{1,0:T(8,128)(2,1)S(1)}, bf16[512,256]{1,0:T(8,128)(2,1)S(1)}, u32[]{:S(2)}, u32[]{:S(2)}) collective-permute-start(bf16[512,256]{1,0:T(8,128)(2,1)S(1)} %get-tuple-element.31), channel_id=1, source_target_pairs={{0,128},{64,192},{128,256},{192,320},{256,384},{320,448},{384,0},{... | collective-permute-start | bytes 786440 | tf_op jit(solution)/shard_map/ppermute | solution.py:21
  15.6 10.4 %collective-permute-start.4 = (bf16[512,256]{1,0:T(8,128)(2,1)S(1)}, bf16[512,256]{1,0:T(8,128)(2,1)S(1)}, u32[]{:S(2)}, u32[]{:S(2)}) collective-permute-start(bf16[512,256]{1,0:T(8,128)(2,1)S(1)} %get-tuple-element.31), channel_id=1, source_target_pairs={{0,384},{64,448},{128,0},{192,64},{256,128},{320,192},{384,256},{4... | collective-permute-start | bytes 786440 | tf_op jit(solution)/shard_map/ppermute | solution.py:21
  26.0 4.3 %collective-permute-start.1 = (bf16[512,256]{1,0:T(8,128)(2,1)S(1)}, bf16[512,256]{1,0:T(8,128)(2,1)S(1)}, u32[]{:S(2)}, u32[]{:S(2)}) collective-permute-start(bf16[512,256]{1,0:T(8,128)(2,1)S(1)} %get-tuple-element.31), channel_id=1, source_target_pairs={{0,64},{64,128},{128,192},{192,256},{256,320},{320,384},{384,448},... | collective-permute-start | bytes 786440 | tf_op jit(solution)/shard_map/ppermute | solution.py:21
  30.3 3.4 %collective-permute-start.2 = (bf16[512,256]{1,0:T(8,128)(2,1)S(1)}, bf16[512,256]{1,0:T(8,128)(2,1)S(1)}, u32[]{:S(2)}, u32[]{:S(2)}) collective-permute-start(bf16[512,256]{1,0:T(8,128)(2,1)S(1)} %get-tuple-element.31), channel_id=1, source_target_pairs={{0,448},{64,0},{128,64},{192,128},{256,192},{320,256},{384,320},{4... | collective-permute-start | bytes 786440 | tf_op jit(solution)/shard_map/ppermute | solution.py:21
  33.7 2.4 %collective-permute-done.3 = bf16[512,256]{1,0:T(8,128)(2,1)S(1)} collective-permute-done((bf16[512,256]{1,0:T(8,128)(2,1)S(1)}, bf16[512,256]{1,0:T(8,128)(2,1)S(1)}, u32[]{:S(2)}, u32[]{:S(2)}) %collective-permute-start.3) | collective-permute-done | bytes 262176 | tf_op jit(solution)/shard_map/ppermute | solution.py:21
  36.1 1.9 %collective-permute-start.7 = (bf16[256,256]{1,0:T(8,128)(2,1)S(1)}, bf16[256,256]{1,0:T(8,128)(2,1)S(1)}, u32[]{:S(2)}, u32[]{:S(2)}) collective-permute-start(bf16[256,256]{1,0:T(8,128)(2,1)S(1)} %slice.40), channel_id=1, source_target_pairs={{0,128},{64,192},{128,256},{192,320},{256,384},{320,448},{384,0},{... | collective-permute-start | bytes 393224 | tf_op jit(solution)/shard_map/ppermute | solution.py:21
  38.0 0.0 collective-permute-done.4
  38.0 6.0 %collective-permute-start.8 = (bf16[256,256]{1,0:T(8,128)(2,1)S(1)}, bf16[256,256]{1,0:T(8,128)(2,1)S(1)}, u32[]{:S(2)}, u32[]{:S(2)}) collective-permute-start(bf16[256,256]{1,0:T(8,128)(2,1)S(1)} %slice.41), channel_id=1, source_target_pairs={{0,384},{64,448},{128,0},{192,64},{256,128},{320,192},{384,256},{4... | collective-permute-start | bytes 393224 | tf_op jit(solution)/shard_map/ppermute | solution.py:21
  44.1 2.6 %collective-permute-start.5 = (bf16[512,256]{1,0:T(8,128)(2,1)S(1)}, bf16[512,256]{1,0:T(8,128)(2,1)S(1)}, u32[]{:S(2)}, u32[]{:S(2)}) collective-permute-start(bf16[512,256]{1,0:T(8,128)(2,1)S(1)} %collective-permute-done.3), channel_id=1, source_target_pairs={{0,64},{64,128},{128,192},{192,256},{256,320},{320,384},{384,448},... | collective-permute-start | bytes 786440 | tf_op jit(solution)/shard_map/ppermute | solution.py:21
  46.7 0.0 collective-permute-done.1
  46.7 4.4 %collective-permute-start.6 = (bf16[512,256]{1,0:T(8,128)(2,1)S(1)}, bf16[512,256]{1,0:T(8,128)(2,1)S(1)}, u32[]{:S(2)}, u32[]{:S(2)}) collective-permute-start(bf16[512,256]{1,0:T(8,128)(2,1)S(1)} %collective-permute-done.4), channel_id=1, source_target_pairs={{0,448},{64,0},{128,64},{192,128},{256,192},{320,256},{384,320},{4... | collective-permute-start | bytes 786440 | tf_op jit(solution)/shard_map/ppermute | solution.py:21
  51.2 0.0 collective-permute-done.2
  51.3 2.3 %collective-permute-done.5 = bf16[512,256]{1,0:T(8,128)(2,1)S(1)} collective-permute-done((bf16[512,256]{1,0:T(8,128)(2,1)S(1)}, bf16[512,256]{1,0:T(8,128)(2,1)S(1)}, u32[]{:S(2)}, u32[]{:S(2)}) %collective-permute-start.5) | collective-permute-done | bytes 262176 | tf_op jit(solution)/shard_map/ppermute | solution.py:21
  53.6 1.4 collective-permute-done.6
  55.1 0.0 collective-permute-done.7
  55.1 0.0 collective-permute-done.8
  55.1 1.9 %collective-permute-start.9 = (bf16[4096,256]{1,0:T(8,128)(2,1)S(1)}, bf16[4096,256]{1,0:T(8,128)(2,1)S(1)}, u32[]{:S(2)}, u32[]{:S(2)}) collective-permute-start(bf16[4096,256]{1,0:T(8,128)(2,1)S(1)} %constant_dynamic-update-slice_fusion.2.near), channel_id=1, source_target_pairs={{0,32},{32,0},{1,33},{33,1},{2,34},{34,2},{3,35},{35,3},{4,36},{36... | collective-permute-start | bytes 6291464 | tf_op jit(solution)/shard_map/ppermute | solution.py:21
  57.7 3.5 %collective-permute-done.9.across = bf16[4096,256]{1,0:T(8,128)(2,1)S(1)} collective-permute-done((bf16[4096,256]{1,0:T(8,128)(2,1)S(1)}, bf16[4096,256]{1,0:T(8,128)(2,1)S(1)}, u32[]{:S(2)}, u32[]{:S(2)}) %collective-permute-start.9) | collective-permute-done | bytes 2097184 | tf_op jit(solution)/shard_map/ppermute | solution.py:21
  61.2 0.0 copy-done
  61.2 0.0 copy-done.1
  61.2 0.0 copy-done.2
  61.2 2.0 %tile_products.4 = (bf16[512,256]{1,0:T(8,128)(2,1)S(1)}, bf16[1024,256]{1,0:T(8,128)(2,1)S(1)}) custom-call(s32[1]{0:T(128)S(6)} %copy.18.count, s32[24]{0:T(128)S(1)} %copy-done.1, s32[24]{0:T(128)S(1)} %copy-done.2, bf16[24,256,256]{2,1,0:T(8,128)(2,1)S(1)} %copy-done, bf16[4096,256]{1,0:T(8,128)(2,1)S(1)} %constant_dynamic-update-slice_fusion.2.near, ...), custom_call_target="tpu_custom_call" | custom-call | flops 201326592 | bytes 1572864 | tf_op jit(solution)/shard_map/tile_products/pallas_call | solution.py:90
  63.2 3.4 %collective-permute-start.10 = (bf16[1024,256]{1,0:T(8,128)(2,1)S(1)}, bf16[1024,256]{1,0:T(8,128)(2,1)S(1)}, u32[]{:S(2)}, u32[]{:S(2)}) collective-permute-start(bf16[1024,256]{1,0:T(8,128)(2,1)S(1)} %get-tuple-element.19), channel_id=1, source_target_pairs={{0,1},{1,2},{2,3},{3,4},{4,5},{5,6},{6,7},{7,0},{8,9},{9,10},{10,1... | collective-permute-start | bytes 1572872 | tf_op jit(solution)/shard_map/ppermute | solution.py:21
  66.6 3.4 %collective-permute-start.11 = (bf16[512,256]{1,0:T(8,128)(2,1)S(1)}, bf16[512,256]{1,0:T(8,128)(2,1)S(1)}, u32[]{:S(2)}, u32[]{:S(2)}) collective-permute-start(bf16[512,256]{1,0:T(8,128)(2,1)S(1)} %get-tuple-element.20), channel_id=1, source_target_pairs={{0,2},{1,3},{2,4},{3,5},{4,6},{5,7},{6,0},{7,1},{8,10},{9,11},{10,... | collective-permute-start | bytes 786440 | tf_op jit(solution)/shard_map/ppermute | solution.py:21
  70.1 1.6 %tile_products.5 = (bf16[512,256]{1,0:T(8,128)(2,1)S(1)}, bf16[1024,256]{1,0:T(8,128)(2,1)S(1)}) custom-call(s32[1]{0:T(128)S(6)} %copy.18.count, s32[24]{0:T(128)S(1)} %copy-done.1, s32[24]{0:T(128)S(1)} %copy-done.2, bf16[24,256,256]{2,1,0:T(8,128)(2,1)S(1)} %copy-done, bf16[4096,256]{1,0:T(8,128)(2,1)S(1)} %constant_dynamic-update-slice_fusion.2.near, ...), custom_call_target="tpu_custom_call" | custom-call | flops 201326592 | bytes 1572864 | tf_op jit(solution)/shard_map/tile_products/pallas_call | solution.py:90
  71.6 2.7 %collective-permute-start.14 = (bf16[1024,256]{1,0:T(8,128)(2,1)S(1)}, bf16[1024,256]{1,0:T(8,128)(2,1)S(1)}, u32[]{:S(2)}, u32[]{:S(2)}) collective-permute-start(bf16[1024,256]{1,0:T(8,128)(2,1)S(1)} %get-tuple-element.23), channel_id=1, source_target_pairs={{0,7},{1,0},{2,1},{3,2},{4,3},{5,4},{6,5},{7,6},{8,15},{9,8},{10,9... | collective-permute-start | bytes 1572872 | tf_op jit(solution)/shard_map/ppermute | solution.py:21
  74.3 3.5 %collective-permute-start.15 = (bf16[512,256]{1,0:T(8,128)(2,1)S(1)}, bf16[512,256]{1,0:T(8,128)(2,1)S(1)}, u32[]{:S(2)}, u32[]{:S(2)}) collective-permute-start(bf16[512,256]{1,0:T(8,128)(2,1)S(1)} %get-tuple-element.24), channel_id=1, source_target_pairs={{0,6},{1,7},{2,0},{3,1},{4,2},{5,3},{6,4},{7,5},{8,14},{9,15},{10,... | collective-permute-start | bytes 786440 | tf_op jit(solution)/shard_map/ppermute | solution.py:21
  77.9 4.8 %tile_products.3 = (bf16[1024,256]{1,0:T(8,128)(2,1)S(1)}, bf16[1024,256]{1,0:T(8,128)(2,1)S(1)}, bf16[1024,256]{1,0:T(8,128)(2,1)S(1)}, bf16[1024,256]{1,0:T(8,128)(2,1)S(1)}, bf16[1024,256]{1,0:T(8,128)(2,1)S(1)}) custom-call(s32[1]{0:T(128)S(6)} %copy.18.count, s32[24]{0:T(128)S(1)} %copy-done.1, s32[24]{0:T(128)S(1)} %copy-done.2, ...), custom_call_target="tpu_custom_call" | custom-call | flops 671088640 | bytes 5242880 | tf_op jit(solution)/shard_map/tile_products/pallas_call | solution.py:90
  82.6 8.7 %collective-permute-done.11 = bf16[512,256]{1,0:T(8,128)(2,1)S(1)} collective-permute-done((bf16[512,256]{1,0:T(8,128)(2,1)S(1)}, bf16[512,256]{1,0:T(8,128)(2,1)S(1)}, u32[]{:S(2)}, u32[]{:S(2)}) %collective-permute-start.11) | collective-permute-done | bytes 262176 | tf_op jit(solution)/shard_map/ppermute | solution.py:21
  91.3 0.0 collective-permute-done.10
  91.3 0.2 add_convert_fusion.6
  91.6 1.9 %collective-permute-start.12 = (bf16[1024,256]{1,0:T(8,128)(2,1)S(1)}, bf16[1024,256]{1,0:T(8,128)(2,1)S(1)}, u32[]{:S(2)}, u32[]{:S(2)}) collective-permute-start(bf16[1024,256]{1,0:T(8,128)(2,1)S(1)} %pad_maximum_fusion), channel_id=1, source_target_pairs={{0,1},{1,2},{2,3},{3,4},{4,5},{5,6},{6,7},{7,0},{8,9},{9,10},{10,1... | collective-permute-start | bytes 1572872 | tf_op jit(solution)/shard_map/ppermute | solution.py:21
  93.5 5.0 %collective-permute-done.15 = bf16[512,256]{1,0:T(8,128)(2,1)S(1)} collective-permute-done((bf16[512,256]{1,0:T(8,128)(2,1)S(1)}, bf16[512,256]{1,0:T(8,128)(2,1)S(1)}, u32[]{:S(2)}, u32[]{:S(2)}) %collective-permute-start.15) | collective-permute-done | bytes 262176 | tf_op jit(solution)/shard_map/ppermute | solution.py:21
  98.5 0.0 collective-permute-done.14
  98.5 0.2 add_convert_fusion.4
  98.7 0.0 copy-start.5
  98.7 0.0 copy-start.3
  98.7 0.0 copy-start.4
  98.8 4.8 %collective-permute-start.16 = (bf16[1024,256]{1,0:T(8,128)(2,1)S(1)}, bf16[1024,256]{1,0:T(8,128)(2,1)S(1)}, u32[]{:S(2)}, u32[]{:S(2)}) collective-permute-start(bf16[1024,256]{1,0:T(8,128)(2,1)S(1)} %pad_maximum_fusion.1), channel_id=1, source_target_pairs={{0,7},{1,0},{2,1},{3,2},{4,3},{5,4},{6,5},{7,6},{8,15},{9,8},{10,9... | collective-permute-start | bytes 1572872 | tf_op jit(solution)/shard_map/ppermute | solution.py:21
  103.6 3.1 %collective-permute-done.12 = bf16[1024,256]{1,0:T(8,128)(2,1)S(1)} collective-permute-done((bf16[1024,256]{1,0:T(8,128)(2,1)S(1)}, bf16[1024,256]{1,0:T(8,128)(2,1)S(1)}, u32[]{:S(2)}, u32[]{:S(2)}) %collective-permute-start.12) | collective-permute-done | bytes 524320 | tf_op jit(solution)/shard_map/ppermute | solution.py:21
  106.7 0.1 add_convert_fusion.2
  106.8 3.4 %collective-permute-start.13 = (bf16[1024,256]{1,0:T(8,128)(2,1)S(1)}, bf16[1024,256]{1,0:T(8,128)(2,1)S(1)}, u32[]{:S(2)}, u32[]{:S(2)}) collective-permute-start(bf16[1024,256]{1,0:T(8,128)(2,1)S(1)} %add_convert_fusion.2), channel_id=1, source_target_pairs={{0,1},{1,2},{2,3},{3,4},{4,5},{5,6},{6,7},{7,0},{8,9},{9,10},{10,1... | collective-permute-start | bytes 1572872 | tf_op jit(solution)/shard_map/ppermute | solution.py:21
  110.3 5.4 %collective-permute-done.16 = bf16[1024,256]{1,0:T(8,128)(2,1)S(1)} collective-permute-done((bf16[1024,256]{1,0:T(8,128)(2,1)S(1)}, bf16[1024,256]{1,0:T(8,128)(2,1)S(1)}, u32[]{:S(2)}, u32[]{:S(2)}) %collective-permute-start.16) | collective-permute-done | bytes 524320 | tf_op jit(solution)/shard_map/ppermute | solution.py:21
  115.7 0.1 add_convert_fusion.1
  115.8 2.8 %collective-permute-start.17 = (bf16[1024,256]{1,0:T(8,128)(2,1)S(1)}, bf16[1024,256]{1,0:T(8,128)(2,1)S(1)}, u32[]{:S(2)}, u32[]{:S(2)}) collective-permute-start(bf16[1024,256]{1,0:T(8,128)(2,1)S(1)} %add_convert_fusion.1), channel_id=1, source_target_pairs={{0,7},{1,0},{2,1},{3,2},{4,3},{5,4},{6,5},{7,6},{8,15},{9,8},{10,9... | collective-permute-start | bytes 1572872 | tf_op jit(solution)/shard_map/ppermute | solution.py:21
  118.6 0.0 copy-done.5
  118.7 0.0 copy-done.3
  118.7 0.0 copy-done.4
  118.7 0.1 multiply_add_fusion
  118.8 2.3 %collective-permute-done.13 = bf16[1024,256]{1,0:T(8,128)(2,1)S(1)} collective-permute-done((bf16[1024,256]{1,0:T(8,128)(2,1)S(1)}, bf16[1024,256]{1,0:T(8,128)(2,1)S(1)}, u32[]{:S(2)}, u32[]{:S(2)}) %collective-permute-start.13) | collective-permute-done | bytes 524320 | tf_op jit(solution)/shard_map/ppermute | solution.py:21
  121.1 9.2 %collective-permute-done.17 = bf16[1024,256]{1,0:T(8,128)(2,1)S(1)} collective-permute-done((bf16[1024,256]{1,0:T(8,128)(2,1)S(1)}, bf16[1024,256]{1,0:T(8,128)(2,1)S(1)}, u32[]{:S(2)}, u32[]{:S(2)}) %collective-permute-start.17) | collective-permute-done | bytes 524320 | tf_op jit(solution)/shard_map/ppermute | solution.py:21
  130.2 0.2 add_convert_fusion
  130.5 23.3 %all_to_all.9 = bf16[4,256,256]{2,1,0:T(8,128)(2,1)S(1)} all-to-all(bf16[4,256,256]{2,1,0:T(8,128)(2,1)S(1)} %bitcast.1), channel_id=1, replica_groups=mesh['ylo'=2,'z'=8,'core'=2,'yhi'=4,'x'=8] {'yhi'}, dimensions={0} | all-to-all | bytes 1048576 | tf_op jit(solution)/shard_map/all_to_all | solution.py:162
  153.8 0.1 convert_reduce_fusion
  153.9 0.7 add_convert_fusion.7
  (14 shorter events, 0.3 us)
Async XLA Ops:
  0.0 7.3 %collective-permute-start = (bf16[256,256]{1,0:T(8,128)(2,1)}, bf16[256,256]{1,0:T(8,128)(2,1)S(1)}, u32[]{:S(2)}, u32[]{:S(2)}) collective-permute-start(bf16[256,256]{1,0:T(8,128)(2,1)} %param.7), channel_id=1, source_target_pairs={{0,512},{512,0},{1,513},{513,1},{2,514},{514,2},{3,515},{515,3},{4... | collective-permute-start | bytes 393224 | tf_op jit(solution)/shard_map/ppermute | solution.py:21
  7.4 53.8 %copy-start = (bf16[24,256,256]{2,1,0:T(8,128)(2,1)S(1)}, bf16[24,256,256]{2,1,0:T(8,128)(2,1)}, u32[]{:S(2)}) copy-start(bf16[24,256,256]{2,1,0:T(8,128)(2,1)} %tiles.5) | copy-start | bytes 9437188
  7.4 53.8 %copy-start.1 = (s32[24]{0:T(128)S(1)}, s32[24]{0:T(128)}, u32[]{:S(2)}) copy-start(s32[24]{0:T(128)} %rows.5) | copy-start | bytes 292
  7.4 53.8 %copy-start.2 = (s32[24]{0:T(128)S(1)}, s32[24]{0:T(128)}, u32[]{:S(2)}) copy-start(s32[24]{0:T(128)} %srcs.5) | copy-start | bytes 292
  7.4 28.7 %collective-permute-start.3 = (bf16[512,256]{1,0:T(8,128)(2,1)S(1)}, bf16[512,256]{1,0:T(8,128)(2,1)S(1)}, u32[]{:S(2)}, u32[]{:S(2)}) collective-permute-start(bf16[512,256]{1,0:T(8,128)(2,1)S(1)} %get-tuple-element.31), channel_id=1, source_target_pairs={{0,128},{64,192},{128,256},{192,320},{256,384},{320,448},{384,0},{... | collective-permute-start | bytes 786440 | tf_op jit(solution)/shard_map/ppermute | solution.py:21
  15.6 22.5 %collective-permute-start.4 = (bf16[512,256]{1,0:T(8,128)(2,1)S(1)}, bf16[512,256]{1,0:T(8,128)(2,1)S(1)}, u32[]{:S(2)}, u32[]{:S(2)}) collective-permute-start(bf16[512,256]{1,0:T(8,128)(2,1)S(1)} %get-tuple-element.31), channel_id=1, source_target_pairs={{0,384},{64,448},{128,0},{192,64},{256,128},{320,192},{384,256},{4... | collective-permute-start | bytes 786440 | tf_op jit(solution)/shard_map/ppermute | solution.py:21
  26.0 20.7 %collective-permute-start.1 = (bf16[512,256]{1,0:T(8,128)(2,1)S(1)}, bf16[512,256]{1,0:T(8,128)(2,1)S(1)}, u32[]{:S(2)}, u32[]{:S(2)}) collective-permute-start(bf16[512,256]{1,0:T(8,128)(2,1)S(1)} %get-tuple-element.31), channel_id=1, source_target_pairs={{0,64},{64,128},{128,192},{192,256},{256,320},{320,384},{384,448},... | collective-permute-start | bytes 786440 | tf_op jit(solution)/shard_map/ppermute | solution.py:21
  30.3 20.9 %collective-permute-start.2 = (bf16[512,256]{1,0:T(8,128)(2,1)S(1)}, bf16[512,256]{1,0:T(8,128)(2,1)S(1)}, u32[]{:S(2)}, u32[]{:S(2)}) collective-permute-start(bf16[512,256]{1,0:T(8,128)(2,1)S(1)} %get-tuple-element.31), channel_id=1, source_target_pairs={{0,448},{64,0},{128,64},{192,128},{256,192},{320,256},{384,320},{4... | collective-permute-start | bytes 786440 | tf_op jit(solution)/shard_map/ppermute | solution.py:21
  36.1 19.0 %collective-permute-start.7 = (bf16[256,256]{1,0:T(8,128)(2,1)S(1)}, bf16[256,256]{1,0:T(8,128)(2,1)S(1)}, u32[]{:S(2)}, u32[]{:S(2)}) collective-permute-start(bf16[256,256]{1,0:T(8,128)(2,1)S(1)} %slice.40), channel_id=1, source_target_pairs={{0,128},{64,192},{128,256},{192,320},{256,384},{320,448},{384,0},{... | collective-permute-start | bytes 393224 | tf_op jit(solution)/shard_map/ppermute | solution.py:21
  38.0 17.0 %collective-permute-start.8 = (bf16[256,256]{1,0:T(8,128)(2,1)S(1)}, bf16[256,256]{1,0:T(8,128)(2,1)S(1)}, u32[]{:S(2)}, u32[]{:S(2)}) collective-permute-start(bf16[256,256]{1,0:T(8,128)(2,1)S(1)} %slice.41), channel_id=1, source_target_pairs={{0,384},{64,448},{128,0},{192,64},{256,128},{320,192},{384,256},{4... | collective-permute-start | bytes 393224 | tf_op jit(solution)/shard_map/ppermute | solution.py:21
  44.1 9.5 %collective-permute-start.5 = (bf16[512,256]{1,0:T(8,128)(2,1)S(1)}, bf16[512,256]{1,0:T(8,128)(2,1)S(1)}, u32[]{:S(2)}, u32[]{:S(2)}) collective-permute-start(bf16[512,256]{1,0:T(8,128)(2,1)S(1)} %collective-permute-done.3), channel_id=1, source_target_pairs={{0,64},{64,128},{128,192},{192,256},{256,320},{320,384},{384,448},... | collective-permute-start | bytes 786440 | tf_op jit(solution)/shard_map/ppermute | solution.py:21
  46.7 8.3 %collective-permute-start.6 = (bf16[512,256]{1,0:T(8,128)(2,1)S(1)}, bf16[512,256]{1,0:T(8,128)(2,1)S(1)}, u32[]{:S(2)}, u32[]{:S(2)}) collective-permute-start(bf16[512,256]{1,0:T(8,128)(2,1)S(1)} %collective-permute-done.4), channel_id=1, source_target_pairs={{0,448},{64,0},{128,64},{192,128},{256,192},{320,256},{384,320},{4... | collective-permute-start | bytes 786440 | tf_op jit(solution)/shard_map/ppermute | solution.py:21
  55.1 6.1 %collective-permute-start.9 = (bf16[4096,256]{1,0:T(8,128)(2,1)S(1)}, bf16[4096,256]{1,0:T(8,128)(2,1)S(1)}, u32[]{:S(2)}, u32[]{:S(2)}) collective-permute-start(bf16[4096,256]{1,0:T(8,128)(2,1)S(1)} %constant_dynamic-update-slice_fusion.2.near), channel_id=1, source_target_pairs={{0,32},{32,0},{1,33},{33,1},{2,34},{34,2},{3,35},{35,3},{4,36},{36... | collective-permute-start | bytes 6291464 | tf_op jit(solution)/shard_map/ppermute | solution.py:21
  63.2 28.1 %collective-permute-start.10 = (bf16[1024,256]{1,0:T(8,128)(2,1)S(1)}, bf16[1024,256]{1,0:T(8,128)(2,1)S(1)}, u32[]{:S(2)}, u32[]{:S(2)}) collective-permute-start(bf16[1024,256]{1,0:T(8,128)(2,1)S(1)} %get-tuple-element.19), channel_id=1, source_target_pairs={{0,1},{1,2},{2,3},{3,4},{4,5},{5,6},{6,7},{7,0},{8,9},{9,10},{10,1... | collective-permute-start | bytes 1572872 | tf_op jit(solution)/shard_map/ppermute | solution.py:21
  66.6 24.7 %collective-permute-start.11 = (bf16[512,256]{1,0:T(8,128)(2,1)S(1)}, bf16[512,256]{1,0:T(8,128)(2,1)S(1)}, u32[]{:S(2)}, u32[]{:S(2)}) collective-permute-start(bf16[512,256]{1,0:T(8,128)(2,1)S(1)} %get-tuple-element.20), channel_id=1, source_target_pairs={{0,2},{1,3},{2,4},{3,5},{4,6},{5,7},{6,0},{7,1},{8,10},{9,11},{10,... | collective-permute-start | bytes 786440 | tf_op jit(solution)/shard_map/ppermute | solution.py:21
  71.6 26.9 %collective-permute-start.14 = (bf16[1024,256]{1,0:T(8,128)(2,1)S(1)}, bf16[1024,256]{1,0:T(8,128)(2,1)S(1)}, u32[]{:S(2)}, u32[]{:S(2)}) collective-permute-start(bf16[1024,256]{1,0:T(8,128)(2,1)S(1)} %get-tuple-element.23), channel_id=1, source_target_pairs={{0,7},{1,0},{2,1},{3,2},{4,3},{5,4},{6,5},{7,6},{8,15},{9,8},{10,9... | collective-permute-start | bytes 1572872 | tf_op jit(solution)/shard_map/ppermute | solution.py:21
  74.3 24.2 %collective-permute-start.15 = (bf16[512,256]{1,0:T(8,128)(2,1)S(1)}, bf16[512,256]{1,0:T(8,128)(2,1)S(1)}, u32[]{:S(2)}, u32[]{:S(2)}) collective-permute-start(bf16[512,256]{1,0:T(8,128)(2,1)S(1)} %get-tuple-element.24), channel_id=1, source_target_pairs={{0,6},{1,7},{2,0},{3,1},{4,2},{5,3},{6,4},{7,5},{8,14},{9,15},{10,... | collective-permute-start | bytes 786440 | tf_op jit(solution)/shard_map/ppermute | solution.py:21
  91.6 15.1 %collective-permute-start.12 = (bf16[1024,256]{1,0:T(8,128)(2,1)S(1)}, bf16[1024,256]{1,0:T(8,128)(2,1)S(1)}, u32[]{:S(2)}, u32[]{:S(2)}) collective-permute-start(bf16[1024,256]{1,0:T(8,128)(2,1)S(1)} %pad_maximum_fusion), channel_id=1, source_target_pairs={{0,1},{1,2},{2,3},{3,4},{4,5},{5,6},{6,7},{7,0},{8,9},{9,10},{10,1... | collective-permute-start | bytes 1572872 | tf_op jit(solution)/shard_map/ppermute | solution.py:21
  98.7 20.0 %copy-start.5 = (s32[256]{0:T(256)S(1)}, s32[256]{0:T(256)}, u32[]{:S(2)}) copy-start(s32[256]{0:T(256)} %param.13) | copy-start | bytes 3076
  98.7 20.0 %copy-start.3 = (bf16[256,256]{1,0:T(8,128)(2,1)S(1)}, bf16[256,256]{1,0:T(8,128)(2,1)}, u32[]{:S(2)}) copy-start(bf16[256,256]{1,0:T(8,128)(2,1)} %param.7) | copy-start | bytes 393220
  98.7 20.0 %copy-start.4 = (bf16[256,256]{1,0:T(8,128)(2,1)S(1)}, bf16[256,256]{1,0:T(8,128)(2,1)}, u32[]{:S(2)}) copy-start(bf16[256,256]{1,0:T(8,128)(2,1)} %param.8) | copy-start | bytes 393220
  98.8 16.9 %collective-permute-start.16 = (bf16[1024,256]{1,0:T(8,128)(2,1)S(1)}, bf16[1024,256]{1,0:T(8,128)(2,1)S(1)}, u32[]{:S(2)}, u32[]{:S(2)}) collective-permute-start(bf16[1024,256]{1,0:T(8,128)(2,1)S(1)} %pad_maximum_fusion.1), channel_id=1, source_target_pairs={{0,7},{1,0},{2,1},{3,2},{4,3},{5,4},{6,5},{7,6},{8,15},{9,8},{10,9... | collective-permute-start | bytes 1572872 | tf_op jit(solution)/shard_map/ppermute | solution.py:21
  106.8 14.2 %collective-permute-start.13 = (bf16[1024,256]{1,0:T(8,128)(2,1)S(1)}, bf16[1024,256]{1,0:T(8,128)(2,1)S(1)}, u32[]{:S(2)}, u32[]{:S(2)}) collective-permute-start(bf16[1024,256]{1,0:T(8,128)(2,1)S(1)} %add_convert_fusion.2), channel_id=1, source_target_pairs={{0,1},{1,2},{2,3},{3,4},{4,5},{5,6},{6,7},{7,0},{8,9},{9,10},{10,1... | collective-permute-start | bytes 1572872 | tf_op jit(solution)/shard_map/ppermute | solution.py:21
  115.8 14.4 %collective-permute-start.17 = (bf16[1024,256]{1,0:T(8,128)(2,1)S(1)}, bf16[1024,256]{1,0:T(8,128)(2,1)S(1)}, u32[]{:S(2)}, u32[]{:S(2)}) collective-permute-start(bf16[1024,256]{1,0:T(8,128)(2,1)S(1)} %add_convert_fusion.1), channel_id=1, source_target_pairs={{0,7},{1,0},{2,1},{3,2},{4,3},{5,4},{6,5},{7,6},{8,15},{9,8},{10,9... | collective-permute-start | bytes 1572872 | tf_op jit(solution)/shard_map/ppermute | solution.py:21

commit v5 on v4

--- a/solution.py
+++ b/solution.py
@@ -19,6 +19,15 @@
 def shifted(value, axis, by):
     size = SIZES[axis]
     return lax.ppermute(value, axis, [(i, (i + by) % size) for i in range(size)])
+
+
+def sent_outward(value, by):
+    pairs = [
+        (core * N_X + x, core * N_X + (x + (by if core == 0 else -by)) % N_X)
+        for core in range(N_CORE)
+        for x in range(N_X)
+    ]
+    return lax.ppermute(value, ("core", "x"), pairs)
 
 
 def tiles_kernel(chunks, count, rows, srcs, tiles, near, across, *refs):
@@ -59,12 +68,12 @@
 
         return following[s]
 
-    for out, (k, yhis) in zip(outs, chunks):
-        x = (my_x + k) % N_X
+    def chunk(out, base, k):
+        x = (my_x + jnp.where(my_core == 0, k, -k) + N_X) % N_X
 
-        def block(p, carry, out=out, x=x, yhis=yhis):
-            first = head[(yhis.start + p) * N_X + x]
-            where = pl.ds(pl.multiple_of(p * side, side), side)
+        def block(yhi, carry):
+            first = head[yhi * N_X + x]
+            where = pl.ds(pl.multiple_of((base + yhi) * side, side), side)
 
             @pl.when(first < 0)
             def _():
@@ -78,7 +87,11 @@
 
             return carry
 
-        lax.fori_loop(0, len(yhis), block, 0)
+        lax.fori_loop(0, N_YHI, block, 0)
+
+    for out, ks in zip(outs, chunks):
+        for i, k in enumerate(ks):
+            chunk(out, i * N_YHI, k)
 
 
 def partial_products(chunks, tile_blocks, tile_rows, tile_srcs, tile_count, near, across):
@@ -86,11 +99,11 @@
     columns = near.shape[1]
     smem = pl.BlockSpec(memory_space=pltpu.SMEM)
     vmem = pl.BlockSpec(memory_space=pltpu.VMEM)
-    row_tiles = sum(len(yhis) for _, yhis in chunks)
+    row_tiles = N_YHI * sum(len(ks) for ks in chunks)
     return pl.pallas_call(
         functools.partial(tiles_kernel, chunks),
         out_shape=[
-            jax.ShapeDtypeStruct((len(yhis) * side, columns), jnp.bfloat16) for _, yhis in chunks
+            jax.ShapeDtypeStruct((len(ks) * N_YHI * side, columns), jnp.bfloat16) for ks in chunks
         ],
         in_specs=[smem, smem, smem, vmem, vmem, vmem],
         out_specs=[vmem] * len(chunks),
@@ -130,20 +143,17 @@
 
 
 def reduce_along_x(products):
-    every, half = range(N_YHI), N_YHI // 2
-    up4, up3 = products([(4, every[:half]), (3, every)])
-    down4, down3 = products([(4, every[half:]), (5, every)])
-    up2, down2, up1, down1, own = products([(k, every) for k in (2, 6, 1, 7, 0)])
-    up, down = shifted(up3, "x", 1), shifted(down3, "x", -1)
-    up_far, down_far = shifted(up4, "x", 2), shifted(down4, "x", -2)
-    rows = up4.shape[0]
-    up = jnp.concatenate([add(up2[:rows], up[:rows], up_far), add(up2[rows:], up[rows:])], 0)
-    down = jnp.concatenate(
-        [add(down2[:rows], down[:rows]), add(down2[rows:], down[rows:], down_far)], 0
-    )
-    up, down = shifted(up, "x", 1), shifted(down, "x", -1)
-    up, down = shifted(add(up1, up), "x", 1), shifted(add(down1, down), "x", -1)
-    return add(own, up, down)
+    give3, keep4, keep3 = products([(-3,), (4,), (3,)])
+    give21, keep2, keep1, own = products([(-2, -1), (2,), (1,), (0,)])
+    chunk = own.shape[0]
+    got3, got21 = shifted(give3, "core", 1), shifted(give21, "core", 1)
+    other = sent_outward(got3, 1)
+    mine = add(keep2, sent_outward(keep3, 1), sent_outward(keep4, 2))
+    other = sent_outward(add(got21[:chunk], other), 1)
+    mine = sent_outward(mine, 1)
+    other = sent_outward(add(got21[chunk:], other), 1)
+    mine = sent_outward(add(keep1, mine), 1)
+    return add(own, mine, shifted(other, "core", 1))
 
 
 def body(flow_cols, restart, tile_blocks, tile_rows, tile_srcs, tile_count, dangling):

time: 155 us -> 151 us (0.974)
  waiting for transfers between devices: 46.1 us -> 32.5 us
  starting transfers between devices: 72.7 us -> 82.7 us
    ppermute x18 -> x13, waiting for transfers between devices: 46.1 us -> 12.4 us  [shifted(): lax.ppermute(value, axis, [(i, (i + by) % size) for i in range(size)])]
    ppermute x0 -> x7, starting transfers between devices: none -> 29.3 us  [sent_outward(): return lax.ppermute(value, ('core', 'x'), pairs)]
    ppermute x0 -> x7, waiting for transfers between devices: none -> 20.1 us  [sent_outward(): return lax.ppermute(value, ('core', 'x'), pairs)]
    ppermute x18 -> x13, starting transfers between devices: 72.7 us -> 53.4 us  [shifted(): lax.ppermute(value, axis, [(i, (i + by) % size) for i in range(size)])]
    pallas_call x3 -> x2, Pallas kernels: 8.4 us -> 7.75 us  [partial_products(): pl.pallas_call(functools.partial(tiles_kernel, chunks), out_shape=[jax.Sh...]
  transfers between devices with their start and end apart: 18 -> 20, of which waited for: 11 -> 11; matrix products, arithmetic and copies ran while one was open for 1% -> 1% of each run, Pallas kernels for 4% -> 3%
where the time goes in v5:
time: 151 us; the launch traced here: 149 us
  starting transfers between devices  82.7 us (55%)
  waiting for transfers between devices  32.5 us (22%)
  blocking collectives  22.2 us (15%)
  Pallas kernels  7.75 us (5%)
  other arithmetic  1.72 us (1%)
    ppermute x13, starting transfers between devices, shifted(): lax.ppermute(value, axis, [(i, (i + by) % size) for i in range(size)])  53.4 us
    ppermute x7, starting transfers between devices, sent_outward(): return lax.ppermute(value, ('core', 'x'), pairs)  29.3 us
    all_to_all x1, blocking collectives, body(): lax.all_to_all(along_x, 'yhi', 0, 0, tiled=True)  22.2 us
    ppermute x7, waiting for transfers between devices, sent_outward(): return lax.ppermute(value, ('core', 'x'), pairs)  20.1 us
    ppermute x13, waiting for transfers between devices, shifted(): lax.ppermute(value, axis, [(i, (i + by) % size) for i in range(size)])  12.4 us
    pallas_call x2, Pallas kernels, partial_products(): pl.pallas_call(functools.partial(tiles_kernel, chunks), out_shape=[jax.Sh...  7.75 us
  transfers between devices with their start and end apart: 20, of which 11 were waited for; matrix products, arithmetic and copies ran while one was open for 1% of the time, Pallas kernels for 3%

profile of v5, /device:TPU:14, one launch (start us, length us, event | category | flops | bytes accessed | tf_op | source)
XLA Modules:
  0.0 149.2 jit_solution(13913387295916661306)
XLA Ops:
  0.0 3.6 %collective-permute-start = (bf16[256,256]{1,0:T(8,128)(2,1)}, bf16[256,256]{1,0:T(8,128)(2,1)S(1)}, u32[]{:S(2)}, u32[]{:S(2)}) collective-permute-start(bf16[256,256]{1,0:T(8,128)(2,1)} %param.7), channel_id=1, source_target_pairs={{0,512},{512,0},{1,513},{513,1},{2,514},{514,2},{3,515},{515,3},{4... | collective-permute-start | bytes 393224 | tf_op jit(solution)/shard_map/ppermute | solution.py:21
  3.6 0.9 constant_dynamic-update-slice_fusion.1
  4.5 2.8 %collective-permute-done = bf16[256,256]{1,0:T(8,128)(2,1)S(1)} collective-permute-done((bf16[256,256]{1,0:T(8,128)(2,1)}, bf16[256,256]{1,0:T(8,128)(2,1)S(1)}, u32[]{:S(2)}, u32[]{:S(2)}) %collective-permute-start) | collective-permute-done | bytes 131104 | tf_op jit(solution)/shard_map/ppermute | solution.py:21
  7.4 0.0 copy-start
  7.4 0.0 copy-start.1
  7.4 0.0 copy-start.2
  7.4 8.2 %collective-permute-start.3 = (bf16[512,256]{1,0:T(8,128)(2,1)S(1)}, bf16[512,256]{1,0:T(8,128)(2,1)S(1)}, u32[]{:S(2)}, u32[]{:S(2)}) collective-permute-start(bf16[512,256]{1,0:T(8,128)(2,1)S(1)} %get-tuple-element.23), channel_id=1, source_target_pairs={{0,128},{64,192},{128,256},{192,320},{256,384},{320,448},{384,0},{... | collective-permute-start | bytes 786440 | tf_op jit(solution)/shard_map/ppermute | solution.py:21
  15.6 10.4 %collective-permute-start.4 = (bf16[512,256]{1,0:T(8,128)(2,1)S(1)}, bf16[512,256]{1,0:T(8,128)(2,1)S(1)}, u32[]{:S(2)}, u32[]{:S(2)}) collective-permute-start(bf16[512,256]{1,0:T(8,128)(2,1)S(1)} %get-tuple-element.23), channel_id=1, source_target_pairs={{0,384},{64,448},{128,0},{192,64},{256,128},{320,192},{384,256},{4... | collective-permute-start | bytes 786440 | tf_op jit(solution)/shard_map/ppermute | solution.py:21
  26.0 4.3 %collective-permute-start.1 = (bf16[512,256]{1,0:T(8,128)(2,1)S(1)}, bf16[512,256]{1,0:T(8,128)(2,1)S(1)}, u32[]{:S(2)}, u32[]{:S(2)}) collective-permute-start(bf16[512,256]{1,0:T(8,128)(2,1)S(1)} %get-tuple-element.23), channel_id=1, source_target_pairs={{0,64},{64,128},{128,192},{192,256},{256,320},{320,384},{384,448},... | collective-permute-start | bytes 786440 | tf_op jit(solution)/shard_map/ppermute | solution.py:21
  30.3 3.4 %collective-permute-start.2 = (bf16[512,256]{1,0:T(8,128)(2,1)S(1)}, bf16[512,256]{1,0:T(8,128)(2,1)S(1)}, u32[]{:S(2)}, u32[]{:S(2)}) collective-permute-start(bf16[512,256]{1,0:T(8,128)(2,1)S(1)} %get-tuple-element.23), channel_id=1, source_target_pairs={{0,448},{64,0},{128,64},{192,128},{256,192},{320,256},{384,320},{4... | collective-permute-start | bytes 786440 | tf_op jit(solution)/shard_map/ppermute | solution.py:21
  33.7 2.4 %collective-permute-done.3 = bf16[512,256]{1,0:T(8,128)(2,1)S(1)} collective-permute-done((bf16[512,256]{1,0:T(8,128)(2,1)S(1)}, bf16[512,256]{1,0:T(8,128)(2,1)S(1)}, u32[]{:S(2)}, u32[]{:S(2)}) %collective-permute-start.3) | collective-permute-done | bytes 262176 | tf_op jit(solution)/shard_map/ppermute | solution.py:21
  36.1 1.9 %collective-permute-start.7 = (bf16[256,256]{1,0:T(8,128)(2,1)S(1)}, bf16[256,256]{1,0:T(8,128)(2,1)S(1)}, u32[]{:S(2)}, u32[]{:S(2)}) collective-permute-start(bf16[256,256]{1,0:T(8,128)(2,1)S(1)} %slice.16), channel_id=1, source_target_pairs={{0,128},{64,192},{128,256},{192,320},{256,384},{320,448},{384,0},{... | collective-permute-start | bytes 393224 | tf_op jit(solution)/shard_map/ppermute | solution.py:21
  38.0 0.0 collective-permute-done.4
  38.0 6.0 %collective-permute-start.8 = (bf16[256,256]{1,0:T(8,128)(2,1)S(1)}, bf16[256,256]{1,0:T(8,128)(2,1)S(1)}, u32[]{:S(2)}, u32[]{:S(2)}) collective-permute-start(bf16[256,256]{1,0:T(8,128)(2,1)S(1)} %slice.17), channel_id=1, source_target_pairs={{0,384},{64,448},{128,0},{192,64},{256,128},{320,192},{384,256},{4... | collective-permute-start | bytes 393224 | tf_op jit(solution)/shard_map/ppermute | solution.py:21
  44.1 2.6 %collective-permute-start.5 = (bf16[512,256]{1,0:T(8,128)(2,1)S(1)}, bf16[512,256]{1,0:T(8,128)(2,1)S(1)}, u32[]{:S(2)}, u32[]{:S(2)}) collective-permute-start(bf16[512,256]{1,0:T(8,128)(2,1)S(1)} %collective-permute-done.3), channel_id=1, source_target_pairs={{0,64},{64,128},{128,192},{192,256},{256,320},{320,384},{384,448},... | collective-permute-start | bytes 786440 | tf_op jit(solution)/shard_map/ppermute | solution.py:21
  46.7 0.0 collective-permute-done.1
  46.7 4.4 %collective-permute-start.6 = (bf16[512,256]{1,0:T(8,128)(2,1)S(1)}, bf16[512,256]{1,0:T(8,128)(2,1)S(1)}, u32[]{:S(2)}, u32[]{:S(2)}) collective-permute-start(bf16[512,256]{1,0:T(8,128)(2,1)S(1)} %collective-permute-done.4), channel_id=1, source_target_pairs={{0,448},{64,0},{128,64},{192,128},{256,192},{320,256},{384,320},{4... | collective-permute-start | bytes 786440 | tf_op jit(solution)/shard_map/ppermute | solution.py:21
  51.2 0.0 collective-permute-done.2
  51.3 2.3 %collective-permute-done.5 = bf16[512,256]{1,0:T(8,128)(2,1)S(1)} collective-permute-done((bf16[512,256]{1,0:T(8,128)(2,1)S(1)}, bf16[512,256]{1,0:T(8,128)(2,1)S(1)}, u32[]{:S(2)}, u32[]{:S(2)}) %collective-permute-start.5) | collective-permute-done | bytes 262176 | tf_op jit(solution)/shard_map/ppermute | solution.py:21
  53.6 1.4 collective-permute-done.6
  55.1 0.0 collective-permute-done.7
  55.1 0.0 collective-permute-done.8
  55.1 1.9 %collective-permute-start.9 = (bf16[4096,256]{1,0:T(8,128)(2,1)S(1)}, bf16[4096,256]{1,0:T(8,128)(2,1)S(1)}, u32[]{:S(2)}, u32[]{:S(2)}) collective-permute-start(bf16[4096,256]{1,0:T(8,128)(2,1)S(1)} %constant_dynamic-update-slice_fusion.2.near), channel_id=1, source_target_pairs={{0,32},{32,0},{1,33},{33,1},{2,34},{34,2},{3,35},{35,3},{4,36},{36... | collective-permute-start | bytes 6291464 | tf_op jit(solution)/shard_map/ppermute | solution.py:21
  57.7 3.5 %collective-permute-done.9.across = bf16[4096,256]{1,0:T(8,128)(2,1)S(1)} collective-permute-done((bf16[4096,256]{1,0:T(8,128)(2,1)S(1)}, bf16[4096,256]{1,0:T(8,128)(2,1)S(1)}, u32[]{:S(2)}, u32[]{:S(2)}) %collective-permute-start.9) | collective-permute-done | bytes 2097184 | tf_op jit(solution)/shard_map/ppermute | solution.py:21
  61.2 0.0 copy-done
  61.2 0.0 copy-done.1
  61.2 0.0 copy-done.2
  61.2 3.1 %tile_products.3 = (bf16[1024,256]{1,0:T(8,128)(2,1)S(1)}, bf16[1024,256]{1,0:T(8,128)(2,1)S(1)}, bf16[1024,256]{1,0:T(8,128)(2,1)S(1)}) custom-call(s32[1]{0:T(128)S(6)} %copy.18.count, s32[24]{0:T(128)S(1)} %copy-done.1, s32[24]{0:T(128)S(1)} %copy-done.2, bf16[24,256,256]{2,1,0:T(8,128)(2,1)S(1)} %copy-done, ...), custom_call_target="tpu_custom_call" | custom-call | flops 402653184 | bytes 3145728 | tf_op jit(solution)/shard_map/tile_products/pallas_call | solution.py:103
  64.3 2.3 %collective-permute-start.15 = (bf16[1024,256]{1,0:T(8,128)(2,1)S(1)}, bf16[1024,256]{1,0:T(8,128)(2,1)S(1)}, u32[]{:S(2)}, u32[]{:S(2)}) collective-permute-start(bf16[1024,256]{1,0:T(8,128)(2,1)S(1)} %get-tuple-element.20), channel_id=1, source_target_pairs={{0,32},{32,0},{1,33},{33,1},{2,34},{34,2},{3,35},{35,3},{4,36},{36... | collective-permute-start | bytes 1572872 | tf_op jit(solution)/shard_map/ppermute | solution.py:21
  66.6 4.6 %tile_products.2 = (bf16[2048,256]{1,0:T(8,128)(2,1)S(1)}, bf16[1024,256]{1,0:T(8,128)(2,1)S(1)}, bf16[1024,256]{1,0:T(8,128)(2,1)S(1)}, bf16[1024,256]{1,0:T(8,128)(2,1)S(1)}) custom-call(s32[1]{0:T(128)S(6)} %copy.18.count, s32[24]{0:T(128)S(1)} %copy-done.1, s32[24]{0:T(128)S(1)} %copy-done.2, bf16[24,256,256]{2,1,0:T(8,128)(2,1)S(1)} %copy-done, ...), custom_call_target="tpu_custom_call" | custom-call | flops 671088640 | bytes 5242880 | tf_op jit(solution)/shard_map/tile_products/pallas_call | solution.py:103
  71.2 2.5 %collective-permute-start.14 = (bf16[2048,256]{1,0:T(8,128)(2,1)S(1)}, bf16[2048,256]{1,0:T(8,128)(2,1)S(1)}, u32[]{:S(2)}, u32[]{:S(2)}) collective-permute-start(bf16[2048,256]{1,0:T(8,128)(2,1)S(1)} %get-tuple-element.19), channel_id=1, source_target_pairs={{0,32},{32,0},{1,33},{33,1},{2,34},{34,2},{3,35},{35,3},{4,36},{36... | collective-permute-start | bytes 3145736 | tf_op jit(solution)/shard_map/ppermute | solution.py:21
  73.7 0.0 collective-permute-done.15
  73.7 1.9 %collective-permute-start.16 = (bf16[1024,256]{1,0:T(8,128)(2,1)S(1)}, bf16[1024,256]{1,0:T(8,128)(2,1)S(1)}, u32[]{:S(2)}, u32[]{:S(2)}) collective-permute-start(bf16[1024,256]{1,0:T(8,128)(2,1)S(1)} %collective-permute-done.15), channel_id=1, source_target_pairs={{0,1},{1,2},{2,3},{3,4},{4,5},{5,6},{6,7},{7,0},{32,39},{33,32},{3... | collective-permute-start | bytes 1572872 | tf_op jit(solution)/shard_map/ppermute | solution.py:30
  75.6 4.3 %collective-permute-start.10 = (bf16[1024,256]{1,0:T(8,128)(2,1)S(1)}, bf16[1024,256]{1,0:T(8,128)(2,1)S(1)}, u32[]{:S(2)}, u32[]{:S(2)}) collective-permute-start(bf16[1024,256]{1,0:T(8,128)(2,1)S(1)} %get-tuple-element.17), channel_id=1, source_target_pairs={{0,1},{1,2},{2,3},{3,4},{4,5},{5,6},{6,7},{7,0},{32,39},{33,32},{3... | collective-permute-start | bytes 1572872 | tf_op jit(solution)/shard_map/ppermute | solution.py:30
  79.9 5.0 %collective-permute-start.11 = (bf16[1024,256]{1,0:T(8,128)(2,1)S(1)}, bf16[1024,256]{1,0:T(8,128)(2,1)S(1)}, u32[]{:S(2)}, u32[]{:S(2)}) collective-permute-start(bf16[1024,256]{1,0:T(8,128)(2,1)S(1)} %get-tuple-element.18), channel_id=1, source_target_pairs={{0,2},{1,3},{2,4},{3,5},{4,6},{5,7},{6,0},{7,1},{32,38},{33,39},{3... | collective-permute-start | bytes 1572872 | tf_op jit(solution)/shard_map/ppermute | solution.py:30
  84.9 0.0 collective-permute-done.16
  84.9 0.0 collective-permute-done.14
  84.9 0.1 add_convert_fusion.2
  85.1 3.0 %collective-permute-start.17 = (bf16[1024,256]{1,0:T(8,128)(2,1)S(1)}, bf16[1024,256]{1,0:T(8,128)(2,1)S(1)}, u32[]{:S(2)}, u32[]{:S(2)}) collective-permute-start(bf16[1024,256]{1,0:T(8,128)(2,1)S(1)} %add_convert_fusion.2), channel_id=1, source_target_pairs={{0,1},{1,2},{2,3},{3,4},{4,5},{5,6},{6,7},{7,0},{32,39},{33,32},{3... | collective-permute-start | bytes 1572872 | tf_op jit(solution)/shard_map/ppermute | solution.py:30
  88.1 2.5 %collective-permute-done.10 = bf16[1024,256]{1,0:T(8,128)(2,1)S(1)} collective-permute-done((bf16[1024,256]{1,0:T(8,128)(2,1)S(1)}, bf16[1024,256]{1,0:T(8,128)(2,1)S(1)}, u32[]{:S(2)}, u32[]{:S(2)}) %collective-permute-start.10) | collective-permute-done | bytes 524320 | tf_op jit(solution)/shard_map/ppermute | solution.py:30
  90.5 9.0 %collective-permute-done.11 = bf16[1024,256]{1,0:T(8,128)(2,1)S(1)} collective-permute-done((bf16[1024,256]{1,0:T(8,128)(2,1)S(1)}, bf16[1024,256]{1,0:T(8,128)(2,1)S(1)}, u32[]{:S(2)}, u32[]{:S(2)}) %collective-permute-start.11) | collective-permute-done | bytes 524320 | tf_op jit(solution)/shard_map/ppermute | solution.py:30
  99.6 0.2 add_convert_fusion.4
  99.8 0.0 copy-start.5
  99.8 0.0 copy-start.3
  99.8 0.0 copy-start.4
  99.8 7.0 %collective-permute-start.12 = (bf16[1024,256]{1,0:T(8,128)(2,1)S(1)}, bf16[1024,256]{1,0:T(8,128)(2,1)S(1)}, u32[]{:S(2)}, u32[]{:S(2)}) collective-permute-start(bf16[1024,256]{1,0:T(8,128)(2,1)S(1)} %add_convert_fusion.4), channel_id=1, source_target_pairs={{0,1},{1,2},{2,3},{3,4},{4,5},{5,6},{6,7},{7,0},{32,39},{33,32},{3... | collective-permute-start | bytes 1572872 | tf_op jit(solution)/shard_map/ppermute | solution.py:30
  106.8 0.6 collective-permute-done.17
  107.4 0.1 add_convert_fusion.1
  107.6 3.0 %collective-permute-start.18 = (bf16[1024,256]{1,0:T(8,128)(2,1)S(1)}, bf16[1024,256]{1,0:T(8,128)(2,1)S(1)}, u32[]{:S(2)}, u32[]{:S(2)}) collective-permute-start(bf16[1024,256]{1,0:T(8,128)(2,1)S(1)} %add_convert_fusion.1), channel_id=1, source_target_pairs={{0,1},{1,2},{2,3},{3,4},{4,5},{5,6},{6,7},{7,0},{32,39},{33,32},{3... | collective-permute-start | bytes 1572872 | tf_op jit(solution)/shard_map/ppermute | solution.py:30
  110.5 3.4 %collective-permute-done.12 = bf16[1024,256]{1,0:T(8,128)(2,1)S(1)} collective-permute-done((bf16[1024,256]{1,0:T(8,128)(2,1)S(1)}, bf16[1024,256]{1,0:T(8,128)(2,1)S(1)}, u32[]{:S(2)}, u32[]{:S(2)}) %collective-permute-start.12) | collective-permute-done | bytes 524320 | tf_op jit(solution)/shard_map/ppermute | solution.py:30
  113.9 0.1 add_convert_fusion.3
  114.1 5.2 %collective-permute-start.13 = (bf16[1024,256]{1,0:T(8,128)(2,1)S(1)}, bf16[1024,256]{1,0:T(8,128)(2,1)S(1)}, u32[]{:S(2)}, u32[]{:S(2)}) collective-permute-start(bf16[1024,256]{1,0:T(8,128)(2,1)S(1)} %add_convert_fusion.3), channel_id=1, source_target_pairs={{0,1},{1,2},{2,3},{3,4},{4,5},{5,6},{6,7},{7,0},{32,39},{33,32},{3... | collective-permute-start | bytes 1572872 | tf_op jit(solution)/shard_map/ppermute | solution.py:30
  119.3 0.3 collective-permute-done.18
  119.5 1.9 %collective-permute-start.19 = (bf16[1024,256]{1,0:T(8,128)(2,1)S(1)}, bf16[1024,256]{1,0:T(8,128)(2,1)S(1)}, u32[]{:S(2)}, u32[]{:S(2)}) collective-permute-start(bf16[1024,256]{1,0:T(8,128)(2,1)S(1)} %collective-permute-done.18), channel_id=1, source_target_pairs={{0,32},{32,0},{1,33},{33,1},{2,34},{34,2},{3,35},{35,3},{4,36},{36... | collective-permute-start | bytes 1572872 | tf_op jit(solution)/shard_map/ppermute | solution.py:21
  121.5 0.0 copy-done.5
  121.5 0.0 copy-done.3
  121.5 0.0 copy-done.4
  121.5 0.1 multiply_add_fusion
  121.6 4.3 %collective-permute-done.13 = bf16[1024,256]{1,0:T(8,128)(2,1)S(1)} collective-permute-done((bf16[1024,256]{1,0:T(8,128)(2,1)S(1)}, bf16[1024,256]{1,0:T(8,128)(2,1)S(1)}, u32[]{:S(2)}, u32[]{:S(2)}) %collective-permute-start.13) | collective-permute-done | bytes 524320 | tf_op jit(solution)/shard_map/ppermute | solution.py:30
  125.9 0.0 collective-permute-done.19
  125.9 0.2 add_convert_fusion
  126.2 22.2 %all_to_all.9 = bf16[4,256,256]{2,1,0:T(8,128)(2,1)S(1)} all-to-all(bf16[4,256,256]{2,1,0:T(8,128)(2,1)S(1)} %bitcast.1), channel_id=1, replica_groups=mesh['ylo'=2,'z'=8,'core'=2,'yhi'=4,'x'=8] {'yhi'}, dimensions={0} | all-to-all | bytes 1048576 | tf_op jit(solution)/shard_map/all_to_all | solution.py:172
  148.4 0.1 convert_reduce_fusion
  148.5 0.7 add_convert_fusion.5
  (12 shorter events, 0.2 us)
Async XLA Ops:
  0.0 7.3 %collective-permute-start = (bf16[256,256]{1,0:T(8,128)(2,1)}, bf16[256,256]{1,0:T(8,128)(2,1)S(1)}, u32[]{:S(2)}, u32[]{:S(2)}) collective-permute-start(bf16[256,256]{1,0:T(8,128)(2,1)} %param.7), channel_id=1, source_target_pairs={{0,512},{512,0},{1,513},{513,1},{2,514},{514,2},{3,515},{515,3},{4... | collective-permute-start | bytes 393224 | tf_op jit(solution)/shard_map/ppermute | solution.py:21
  7.4 53.8 %copy-start = (bf16[24,256,256]{2,1,0:T(8,128)(2,1)S(1)}, bf16[24,256,256]{2,1,0:T(8,128)(2,1)}, u32[]{:S(2)}) copy-start(bf16[24,256,256]{2,1,0:T(8,128)(2,1)} %tiles.3) | copy-start | bytes 9437188
  7.4 53.8 %copy-start.1 = (s32[24]{0:T(128)S(1)}, s32[24]{0:T(128)}, u32[]{:S(2)}) copy-start(s32[24]{0:T(128)} %rows.3) | copy-start | bytes 292
  7.4 53.8 %copy-start.2 = (s32[24]{0:T(128)S(1)}, s32[24]{0:T(128)}, u32[]{:S(2)}) copy-start(s32[24]{0:T(128)} %srcs.3) | copy-start | bytes 292
  7.4 28.7 %collective-permute-start.3 = (bf16[512,256]{1,0:T(8,128)(2,1)S(1)}, bf16[512,256]{1,0:T(8,128)(2,1)S(1)}, u32[]{:S(2)}, u32[]{:S(2)}) collective-permute-start(bf16[512,256]{1,0:T(8,128)(2,1)S(1)} %get-tuple-element.23), channel_id=1, source_target_pairs={{0,128},{64,192},{128,256},{192,320},{256,384},{320,448},{384,0},{... | collective-permute-start | bytes 786440 | tf_op jit(solution)/shard_map/ppermute | solution.py:21
  15.6 22.5 %collective-permute-start.4 = (bf16[512,256]{1,0:T(8,128)(2,1)S(1)}, bf16[512,256]{1,0:T(8,128)(2,1)S(1)}, u32[]{:S(2)}, u32[]{:S(2)}) collective-permute-start(bf16[512,256]{1,0:T(8,128)(2,1)S(1)} %get-tuple-element.23), channel_id=1, source_target_pairs={{0,384},{64,448},{128,0},{192,64},{256,128},{320,192},{384,256},{4... | collective-permute-start | bytes 786440 | tf_op jit(solution)/shard_map/ppermute | solution.py:21
  26.0 20.7 %collective-permute-start.1 = (bf16[512,256]{1,0:T(8,128)(2,1)S(1)}, bf16[512,256]{1,0:T(8,128)(2,1)S(1)}, u32[]{:S(2)}, u32[]{:S(2)}) collective-permute-start(bf16[512,256]{1,0:T(8,128)(2,1)S(1)} %get-tuple-element.23), channel_id=1, source_target_pairs={{0,64},{64,128},{128,192},{192,256},{256,320},{320,384},{384,448},... | collective-permute-start | bytes 786440 | tf_op jit(solution)/shard_map/ppermute | solution.py:21
  30.3 20.9 %collective-permute-start.2 = (bf16[512,256]{1,0:T(8,128)(2,1)S(1)}, bf16[512,256]{1,0:T(8,128)(2,1)S(1)}, u32[]{:S(2)}, u32[]{:S(2)}) collective-permute-start(bf16[512,256]{1,0:T(8,128)(2,1)S(1)} %get-tuple-element.23), channel_id=1, source_target_pairs={{0,448},{64,0},{128,64},{192,128},{256,192},{320,256},{384,320},{4... | collective-permute-start | bytes 786440 | tf_op jit(solution)/shard_map/ppermute | solution.py:21
  36.1 19.0 %collective-permute-start.7 = (bf16[256,256]{1,0:T(8,128)(2,1)S(1)}, bf16[256,256]{1,0:T(8,128)(2,1)S(1)}, u32[]{:S(2)}, u32[]{:S(2)}) collective-permute-start(bf16[256,256]{1,0:T(8,128)(2,1)S(1)} %slice.16), channel_id=1, source_target_pairs={{0,128},{64,192},{128,256},{192,320},{256,384},{320,448},{384,0},{... | collective-permute-start | bytes 393224 | tf_op jit(solution)/shard_map/ppermute | solution.py:21
  38.0 17.0 %collective-permute-start.8 = (bf16[256,256]{1,0:T(8,128)(2,1)S(1)}, bf16[256,256]{1,0:T(8,128)(2,1)S(1)}, u32[]{:S(2)}, u32[]{:S(2)}) collective-permute-start(bf16[256,256]{1,0:T(8,128)(2,1)S(1)} %slice.17), channel_id=1, source_target_pairs={{0,384},{64,448},{128,0},{192,64},{256,128},{320,192},{384,256},{4... | collective-permute-start | bytes 393224 | tf_op jit(solution)/shard_map/ppermute | solution.py:21
  44.1 9.5 %collective-permute-start.5 = (bf16[512,256]{1,0:T(8,128)(2,1)S(1)}, bf16[512,256]{1,0:T(8,128)(2,1)S(1)}, u32[]{:S(2)}, u32[]{:S(2)}) collective-permute-start(bf16[512,256]{1,0:T(8,128)(2,1)S(1)} %collective-permute-done.3), channel_id=1, source_target_pairs={{0,64},{64,128},{128,192},{192,256},{256,320},{320,384},{384,448},... | collective-permute-start | bytes 786440 | tf_op jit(solution)/shard_map/ppermute | solution.py:21
  46.7 8.3 %collective-permute-start.6 = (bf16[512,256]{1,0:T(8,128)(2,1)S(1)}, bf16[512,256]{1,0:T(8,128)(2,1)S(1)}, u32[]{:S(2)}, u32[]{:S(2)}) collective-permute-start(bf16[512,256]{1,0:T(8,128)(2,1)S(1)} %collective-permute-done.4), channel_id=1, source_target_pairs={{0,448},{64,0},{128,64},{192,128},{256,192},{320,256},{384,320},{4... | collective-permute-start | bytes 786440 | tf_op jit(solution)/shard_map/ppermute | solution.py:21
  55.1 6.1 %collective-permute-start.9 = (bf16[4096,256]{1,0:T(8,128)(2,1)S(1)}, bf16[4096,256]{1,0:T(8,128)(2,1)S(1)}, u32[]{:S(2)}, u32[]{:S(2)}) collective-permute-start(bf16[4096,256]{1,0:T(8,128)(2,1)S(1)} %constant_dynamic-update-slice_fusion.2.near), channel_id=1, source_target_pairs={{0,32},{32,0},{1,33},{33,1},{2,34},{34,2},{3,35},{35,3},{4,36},{36... | collective-permute-start | bytes 6291464 | tf_op jit(solution)/shard_map/ppermute | solution.py:21
  64.3 9.4 %collective-permute-start.15 = (bf16[1024,256]{1,0:T(8,128)(2,1)S(1)}, bf16[1024,256]{1,0:T(8,128)(2,1)S(1)}, u32[]{:S(2)}, u32[]{:S(2)}) collective-permute-start(bf16[1024,256]{1,0:T(8,128)(2,1)S(1)} %get-tuple-element.20), channel_id=1, source_target_pairs={{0,32},{32,0},{1,33},{33,1},{2,34},{34,2},{3,35},{35,3},{4,36},{36... | collective-permute-start | bytes 1572872 | tf_op jit(solution)/shard_map/ppermute | solution.py:21
  71.2 13.7 %collective-permute-start.14 = (bf16[2048,256]{1,0:T(8,128)(2,1)S(1)}, bf16[2048,256]{1,0:T(8,128)(2,1)S(1)}, u32[]{:S(2)}, u32[]{:S(2)}) collective-permute-start(bf16[2048,256]{1,0:T(8,128)(2,1)S(1)} %get-tuple-element.19), channel_id=1, source_target_pairs={{0,32},{32,0},{1,33},{33,1},{2,34},{34,2},{3,35},{35,3},{4,36},{36... | collective-permute-start | bytes 3145736 | tf_op jit(solution)/shard_map/ppermute | solution.py:21
  73.7 11.2 %collective-permute-start.16 = (bf16[1024,256]{1,0:T(8,128)(2,1)S(1)}, bf16[1024,256]{1,0:T(8,128)(2,1)S(1)}, u32[]{:S(2)}, u32[]{:S(2)}) collective-permute-start(bf16[1024,256]{1,0:T(8,128)(2,1)S(1)} %collective-permute-done.15), channel_id=1, source_target_pairs={{0,1},{1,2},{2,3},{3,4},{4,5},{5,6},{6,7},{7,0},{32,39},{33,32},{3... | collective-permute-start | bytes 1572872 | tf_op jit(solution)/shard_map/ppermute | solution.py:30
  75.6 14.9 %collective-permute-start.10 = (bf16[1024,256]{1,0:T(8,128)(2,1)S(1)}, bf16[1024,256]{1,0:T(8,128)(2,1)S(1)}, u32[]{:S(2)}, u32[]{:S(2)}) collective-permute-start(bf16[1024,256]{1,0:T(8,128)(2,1)S(1)} %get-tuple-element.17), channel_id=1, source_target_pairs={{0,1},{1,2},{2,3},{3,4},{4,5},{5,6},{6,7},{7,0},{32,39},{33,32},{3... | collective-permute-start | bytes 1572872 | tf_op jit(solution)/shard_map/ppermute | solution.py:30
  79.9 19.6 %collective-permute-start.11 = (bf16[1024,256]{1,0:T(8,128)(2,1)S(1)}, bf16[1024,256]{1,0:T(8,128)(2,1)S(1)}, u32[]{:S(2)}, u32[]{:S(2)}) collective-permute-start(bf16[1024,256]{1,0:T(8,128)(2,1)S(1)} %get-tuple-element.18), channel_id=1, source_target_pairs={{0,2},{1,3},{2,4},{3,5},{4,6},{5,7},{6,0},{7,1},{32,38},{33,39},{3... | collective-permute-start | bytes 1572872 | tf_op jit(solution)/shard_map/ppermute | solution.py:30
  85.1 22.4 %collective-permute-start.17 = (bf16[1024,256]{1,0:T(8,128)(2,1)S(1)}, bf16[1024,256]{1,0:T(8,128)(2,1)S(1)}, u32[]{:S(2)}, u32[]{:S(2)}) collective-permute-start(bf16[1024,256]{1,0:T(8,128)(2,1)S(1)} %add_convert_fusion.2), channel_id=1, source_target_pairs={{0,1},{1,2},{2,3},{3,4},{4,5},{5,6},{6,7},{7,0},{32,39},{33,32},{3... | collective-permute-start | bytes 1572872 | tf_op jit(solution)/shard_map/ppermute | solution.py:30
  99.8 21.7 %copy-start.5 = (s32[256]{0:T(256)S(1)}, s32[256]{0:T(256)}, u32[]{:S(2)}) copy-start(s32[256]{0:T(256)} %param.13) | copy-start | bytes 3076
  99.8 21.7 %copy-start.3 = (bf16[256,256]{1,0:T(8,128)(2,1)S(1)}, bf16[256,256]{1,0:T(8,128)(2,1)}, u32[]{:S(2)}) copy-start(bf16[256,256]{1,0:T(8,128)(2,1)} %param.7) | copy-start | bytes 393220
  99.8 21.7 %copy-start.4 = (bf16[256,256]{1,0:T(8,128)(2,1)S(1)}, bf16[256,256]{1,0:T(8,128)(2,1)}, u32[]{:S(2)}) copy-start(bf16[256,256]{1,0:T(8,128)(2,1)} %param.8) | copy-start | bytes 393220
  99.8 14.1 %collective-permute-start.12 = (bf16[1024,256]{1,0:T(8,128)(2,1)S(1)}, bf16[1024,256]{1,0:T(8,128)(2,1)S(1)}, u32[]{:S(2)}, u32[]{:S(2)}) collective-permute-start(bf16[1024,256]{1,0:T(8,128)(2,1)S(1)} %add_convert_fusion.4), channel_id=1, source_target_pairs={{0,1},{1,2},{2,3},{3,4},{4,5},{5,6},{6,7},{7,0},{32,39},{33,32},{3... | collective-permute-start | bytes 1572872 | tf_op jit(solution)/shard_map/ppermute | solution.py:30
  107.6 12.0 %collective-permute-start.18 = (bf16[1024,256]{1,0:T(8,128)(2,1)S(1)}, bf16[1024,256]{1,0:T(8,128)(2,1)S(1)}, u32[]{:S(2)}, u32[]{:S(2)}) collective-permute-start(bf16[1024,256]{1,0:T(8,128)(2,1)S(1)} %add_convert_fusion.1), channel_id=1, source_target_pairs={{0,1},{1,2},{2,3},{3,4},{4,5},{5,6},{6,7},{7,0},{32,39},{33,32},{3... | collective-permute-start | bytes 1572872 | tf_op jit(solution)/shard_map/ppermute | solution.py:30
  114.1 11.9 %collective-permute-start.13 = (bf16[1024,256]{1,0:T(8,128)(2,1)S(1)}, bf16[1024,256]{1,0:T(8,128)(2,1)S(1)}, u32[]{:S(2)}, u32[]{:S(2)}) collective-permute-start(bf16[1024,256]{1,0:T(8,128)(2,1)S(1)} %add_convert_fusion.3), channel_id=1, source_target_pairs={{0,1},{1,2},{2,3},{3,4},{4,5},{5,6},{6,7},{7,0},{32,39},{33,32},{3... | collective-permute-start | bytes 1572872 | tf_op jit(solution)/shard_map/ppermute | solution.py:30
  119.5 6.4 %collective-permute-start.19 = (bf16[1024,256]{1,0:T(8,128)(2,1)S(1)}, bf16[1024,256]{1,0:T(8,128)(2,1)S(1)}, u32[]{:S(2)}, u32[]{:S(2)}) collective-permute-start(bf16[1024,256]{1,0:T(8,128)(2,1)S(1)} %collective-permute-done.18), channel_id=1, source_target_pairs={{0,32},{32,0},{1,33},{33,1},{2,34},{34,2},{3,35},{35,3},{4,36},{36... | collective-permute-start | bytes 1572872 | tf_op jit(solution)/shard_map/ppermute | solution.py:21

commit v6 on v5

v6 whole, which is shorter than its diff:
```python
import functools

import jax
import jax.numpy as jnp
from jax import lax
from jax.experimental import pallas as pl
from jax.experimental.pallas import tpu as pltpu
from jax.sharding import Mesh, PartitionSpec as P

DAMP = 0.85
LOOP = (("ylo", 2), ("z", 8), ("core", 2))
LAYER = (("yhi", 4), ("x", 8))
SIZES = dict(LOOP + LAYER)
N_YLO, N_Z, N_CORE = SIZES["ylo"], SIZES["z"], SIZES["core"]
N_YHI, N_X = SIZES["yhi"], SIZES["x"]
ROW_TILES = N_YHI * N_X


def shifted(value, axis, by):
    size = SIZES[axis]
    return lax.ppermute(value, axis, [(i, (i + by) % size) for i in range(size)])


def sent_outward(value, axis, by):
    size = SIZES[axis]
    names = tuple(name for name in SIZES if name in (axis, "core"))

    def index(core, place):
        return place * N_CORE + core if names[1] == "core" else core * size + place

    pairs = [
        (index(core, i), index(core, (i + (by if core == 0 else -by)) % size))
        for core in range(N_CORE)
        for i in range(size)
    ]
    return lax.ppermute(value, names, pairs)


def tiles_kernel(chunks, count, rows, srcs, tiles, panels, *refs):
    outs, (head, following, acc) = refs[: len(chunks)], refs[len(chunks) :]
    side = tiles.shape[1]
    my_ylo, my_z, my_core = lax.axis_index("ylo"), lax.axis_index("z"), lax.axis_index("core")
    my_x = lax.axis_index("x")

    def clear(r, carry):
        head[r] = -1
        return carry

    lax.fori_loop(0, ROW_TILES, clear, 0)

    def link(s, carry):
        r = rows[s]
        following[s] = head[r]
        head[r] = s
        return carry

    lax.fori_loop(0, count[0], link, 0)

    def product(s):
        place = panel_place(srcs[s], my_ylo, my_z, my_core)
        panel = pl.ds(pl.multiple_of(place * side, side), side)
        return jnp.dot(tiles[s], panels[panel, :], preferred_element_type=jnp.float32)

    def add_product(s):
        acc[...] += product(s)
        return following[s]

    def chunk(out, base, k):
        x = (my_x + jnp.where(my_core == 0, k, -k) + N_X) % N_X

        def block(yhi, carry):
            first = head[yhi * N_X + x]
            where = pl.ds(pl.multiple_of((base + yhi) * side, side), side)

            @pl.when(first < 0)
            def _():
                out[where, :] = jnp.zeros((side, out.shape[1]), out.dtype)

            @pl.when(first >= 0)
            def _():
                acc[...] = product(first)
                lax.while_loop(lambda s: s >= 0, add_product, following[first])
                out[where, :] = acc[...].astype(out.dtype)

            return carry

        lax.fori_loop(0, N_YHI, block, 0)

    for out, ks in zip(outs, chunks):
        for i, k in enumerate(ks):
            chunk(out, i * N_YHI, k)


def partial_products(chunks, tile_blocks, tile_rows, tile_srcs, tile_count, panels):
    slots, side = tile_blocks.shape[:2]
    columns = panels.shape[1]
    smem = pl.BlockSpec(memory_space=pltpu.SMEM)
    vmem = pl.BlockSpec(memory_space=pltpu.VMEM)
    row_tiles = N_YHI * sum(len(ks) for ks in chunks)
    return pl.pallas_call(
        functools.partial(tiles_kernel, chunks),
        out_shape=[
            jax.ShapeDtypeStruct((len(ks) * N_YHI * side, columns), jnp.bfloat16) for ks in chunks
        ],
        in_specs=[smem, smem, smem, vmem, vmem],
        out_specs=[vmem] * len(chunks),
        scratch_shapes=[
            pltpu.SMEM((ROW_TILES,), jnp.int32),
            pltpu.SMEM((slots,), jnp.int32),
            pltpu.VMEM((side, columns), jnp.float32),
        ],
        compiler_params=pltpu.CompilerParams(vmem_limit_bytes=24 << 20),
        cost_estimate=pl.CostEstimate(
            flops=2 * row_tiles * side * side * columns,
            transcendentals=0,
            bytes_accessed=4 * row_tiles * side * columns,
        ),
        name="tile_products",
    )(tile_count, tile_rows, tile_srcs, tile_blocks, panels)


def gather_panels(flow_cols):
    side = flow_cols.shape[0]
    pair = jnp.concatenate([flow_cols, shifted(flow_cols, "core", 1)], 0)
    far2, far1 = sent_outward(pair, "z", 2), sent_outward(pair, "z", 1)
    far3, far4 = sent_outward(far2, "z", 1), sent_outward(far2[:side], "z", 2)
    far12, far34 = jnp.concatenate([far1, far2], 0), jnp.concatenate([far3, far4], 0)
    first = [shifted(flow_cols, "ylo", 1), far12, shifted(far12, "ylo", 1)]
    second = [far34, shifted(far34, "ylo", 1)]
    swapped = [shifted(jnp.concatenate(part, 0), "core", 1) for part in (first, second)]
    return jnp.concatenate([pair] + first + second + swapped, 0)


def panel_place(src, my_ylo, my_z, my_core):
    off_ylo = (src // (N_CORE * N_Z) + N_YLO - my_ylo) % N_YLO
    off_z = (src // N_CORE % N_Z + N_Z - my_z) % N_Z
    off_core = (src % N_CORE + N_CORE - my_core) % N_CORE
    far = jnp.where(my_core == 0, (N_Z - off_z) % N_Z, off_z)
    half = N_Z // 2
    theirs = (
        ((far == 0) & (off_ylo + off_core == 2)) | ((far == half) & (off_core == 1)) | (far > half)
    )
    far = jnp.where(theirs, (N_Z - far) % N_Z, far)
    off_core = jnp.where(theirs, 1 - off_core, off_core)
    place = jnp.where(
        far == 0,
        jnp.where(off_ylo == 0, off_core, 2),
        jnp.where(
            far <= 2,
            1 + 2 * far + off_core + 4 * off_ylo,
            jnp.where(far == 3, 11 + off_core, 13) + 3 * off_ylo,
        ),
    )
    return place + jnp.where(theirs, 15, 0)


def add(*terms):
    total = terms[0].astype(jnp.float32)
    for term in terms[1:]:
        total = total + term.astype(jnp.float32)
    return total.astype(jnp.bfloat16)


def reduce_along_x(products):
    give, keep4, keep3, keep2, keep1, own = products
    chunk = own.shape[0]
    got = shifted(give, "core", 1)
    got3, got2, got1 = (got[i * chunk : (i + 1) * chunk] for i in range(3))
    other, mine = sent_outward(got3, "x", 1), sent_outward(keep3, "x", 1)
    mine = add(keep2, mine, sent_outward(keep4, "x", 2))
    other = sent_outward(add(got2, other), "x", 1)
    mine = sent_outward(mine, "x", 1)
    other = sent_outward(add(got1, other), "x", 1)
    mine = sent_outward(add(keep1, mine), "x", 1)
    return add(own, mine, shifted(other, "core", 1))


def body(flow_cols, restart, tile_blocks, tile_rows, tile_srcs, tile_count, dangling):
    side, columns = flow_cols.shape
    panels = gather_panels(flow_cols)

    products = partial_products(
        [(-3, -2, -1), (4,), (3,), (2,), (1,), (0,)],
        tile_blocks,
        tile_rows,
        tile_srcs,
        tile_count,
        panels,
    )
    own_flow = flow_cols.astype(jnp.float32)
    mask_col = dangling.astype(jnp.float32)[:, None]
    constant = DAMP * (mask_col * own_flow) + (1.0 - DAMP) * restart.astype(jnp.float32)
    along_x, constant = lax.optimization_barrier((reduce_along_x(products), constant))
    shares = lax.all_to_all(along_x, "yhi", 0, 0, tiled=True).reshape(N_YHI, side, columns)
    summed = jnp.sum(shares.astype(jnp.float32), axis=0)
    return (DAMP * summed + constant).astype(jnp.bfloat16)


def solution(mesh):
    names = tuple(SIZES)
    fine = Mesh(mesh.devices.reshape(tuple(SIZES.values())), names)
    rows = P(names, None)
    in_specs = (rows, rows, P(names, None, None), P(names), P(names), P(names), P(names))
    return jax.shard_map(body, mesh=fine, in_specs=in_specs, out_specs=rows, check_vma=False)
```

time: 151 us -> 157 us (1.040)
  waiting for transfers between devices: 32.5 us -> 58.5 us
  starting transfers between devices: 82.7 us -> 63.3 us
    ppermute x13 -> x8, starting transfers between devices: 53.4 us -> 19.2 us  [shifted(): lax.ppermute(value, axis, [(i, (i + by) % size) for i in range(size)])]
    ppermute x7 -> x11, waiting for transfers between devices: 20.1 us -> 38.4 us  [sent_outward(): return lax.ppermute(value, names, pairs)]
    ppermute x7 -> x11, starting transfers between devices: 29.3 us -> 44.1 us  [sent_outward(): return lax.ppermute(value, names, pairs)]
    ppermute x13 -> x8, waiting for transfers between devices: 12.4 us -> 20.1 us  [shifted(): lax.ppermute(value, axis, [(i, (i + by) % size) for i in range(size)])]
    pallas_call x2 -> x1, Pallas kernels: 7.75 us -> 6.41 us  [partial_products(): pl.pallas_call(functools.partial(tiles_kernel, chunks), out_shape=[jax.Sh...]
  transfers between devices with their start and end apart: 20 -> 19, of which waited for: 11 -> 15; matrix products, arithmetic and copies ran while one was open for 1% -> 1% of each run, Pallas kernels for 3% -> 0%
where the time goes in v6:
time: 157 us; the launch traced here: 156 us
  starting transfers between devices  63.3 us (40%)
  waiting for transfers between devices  58.5 us (37%)
  blocking collectives  23.4 us (15%)
  Pallas kernels  6.41 us (4%)
  other arithmetic  1.93 us (1%)
    ppermute x11, starting transfers between devices, sent_outward(): return lax.ppermute(value, names, pairs)  44.1 us
    ppermute x11, waiting for transfers between devices, sent_outward(): return lax.ppermute(value, names, pairs)  38.4 us
    all_to_all x1, blocking collectives, body(): lax.all_to_all(along_x, 'yhi', 0, 0, tiled=True)  23.4 us
    ppermute x8, waiting for transfers between devices, shifted(): lax.ppermute(value, axis, [(i, (i + by) % size) for i in range(size)])  20.1 us
    ppermute x8, starting transfers between devices, shifted(): lax.ppermute(value, axis, [(i, (i + by) % size) for i in range(size)])  19.2 us
    pallas_call x1, Pallas kernels, partial_products(): pl.pallas_call(functools.partial(tiles_kernel, chunks), out_shape=[jax.Sh...  6.41 us
  transfers between devices with their start and end apart: 19, of which 15 were waited for; matrix products, arithmetic and copies ran while one was open for 1% of the time, Pallas kernels for 0%

profile of v6, /device:TPU:14, one launch (start us, length us, event | category | flops | bytes accessed | tf_op | source)
XLA Modules:
  0.0 155.9 jit_solution(6052678698570668250)
XLA Ops:
  0.0 1.9 %collective-permute-start = (bf16[256,256]{1,0:T(8,128)(2,1)}, bf16[256,256]{1,0:T(8,128)(2,1)S(1)}, u32[]{:S(2)}, u32[]{:S(2)}) collective-permute-start(bf16[256,256]{1,0:T(8,128)(2,1)} %param.7), channel_id=1, source_target_pairs={{0,32},{32,0},{1,33},{33,1},{2,34},{34,2},{3,35},{35,3},{4,36},{36... | collective-permute-start | bytes 393224 | tf_op jit(solution)/shard_map/ppermute | solution.py:21
  1.9 0.9 constant_dynamic-update-slice_fusion.1
  2.8 0.6 collective-permute-done
  3.5 5.2 %collective-permute-start.2 = (bf16[512,256]{1,0:T(8,128)(2,1)S(1)}, bf16[512,256]{1,0:T(8,128)(2,1)S(1)}, u32[]{:S(2)}, u32[]{:S(2)}) collective-permute-start(bf16[512,256]{1,0:T(8,128)(2,1)S(1)} %get-tuple-element.21), channel_id=1, source_target_pairs={{0,64},{64,128},{128,192},{192,256},{256,320},{320,384},{384,448},... | collective-permute-start | bytes 786440 | tf_op jit(solution)/shard_map/ppermute | solution.py:36
  8.7 7.9 %collective-permute-start.3 = (bf16[512,256]{1,0:T(8,128)(2,1)S(1)}, bf16[512,256]{1,0:T(8,128)(2,1)S(1)}, u32[]{:S(2)}, u32[]{:S(2)}) collective-permute-start(bf16[512,256]{1,0:T(8,128)(2,1)S(1)} %get-tuple-element.21), channel_id=1, source_target_pairs={{0,128},{64,192},{128,256},{192,320},{256,384},{320,448},{384,0},{... | collective-permute-start | bytes 786440 | tf_op jit(solution)/shard_map/ppermute | solution.py:36
  16.6 8.5 %collective-permute-done.2 = bf16[512,256]{1,0:T(8,128)(2,1)S(1)} collective-permute-done((bf16[512,256]{1,0:T(8,128)(2,1)S(1)}, bf16[512,256]{1,0:T(8,128)(2,1)S(1)}, u32[]{:S(2)}, u32[]{:S(2)}) %collective-permute-start.2) | collective-permute-done | bytes 262176 | tf_op jit(solution)/shard_map/ppermute | solution.py:36
  25.1 6.9 %collective-permute-done.3 = bf16[512,256]{1,0:T(8,128)(2,1)S(1)} collective-permute-done((bf16[512,256]{1,0:T(8,128)(2,1)S(1)}, bf16[512,256]{1,0:T(8,128)(2,1)S(1)}, u32[]{:S(2)}, u32[]{:S(2)}) %collective-permute-start.3) | collective-permute-done | bytes 262176 | tf_op jit(solution)/shard_map/ppermute | solution.py:36
  32.1 3.6 %collective-permute-start.4 = (bf16[1024,256]{1,0:T(8,128)(2,1)S(1)}, bf16[1024,256]{1,0:T(8,128)(2,1)S(1)}, u32[]{:S(2)}, u32[]{:S(2)}) collective-permute-start(bf16[1024,256]{1,0:T(8,128)(2,1)S(1)} %pad_maximum_fusion.2), channel_id=1, source_target_pairs={{0,512},{512,0},{1,513},{513,1},{2,514},{514,2},{3,515},{515,3},{4... | collective-permute-start | bytes 1572872 | tf_op jit(solution)/shard_map/ppermute | solution.py:21
  35.7 2.2 %collective-permute-start.1 = (bf16[256,256]{1,0:T(8,128)(2,1)}, bf16[256,256]{1,0:T(8,128)(2,1)S(1)}, u32[]{:S(2)}, u32[]{:S(2)}) collective-permute-start(bf16[256,256]{1,0:T(8,128)(2,1)} %param.7), channel_id=1, source_target_pairs={{0,512},{512,0},{1,513},{513,1},{2,514},{514,2},{3,515},{515,3},{4... | collective-permute-start | bytes 393224 | tf_op jit(solution)/shard_map/ppermute | solution.py:21
  38.0 1.9 %collective-permute-start.6 = (bf16[256,256]{1,0:T(8,128)(2,1)S(1)}, bf16[256,256]{1,0:T(8,128)(2,1)S(1)}, u32[]{:S(2)}, u32[]{:S(2)}) collective-permute-start(bf16[256,256]{1,0:T(8,128)(2,1)S(1)} %slice.16), channel_id=1, source_target_pairs={{0,128},{64,192},{128,256},{192,320},{256,384},{320,448},{384,0},{... | collective-permute-start | bytes 393224 | tf_op jit(solution)/shard_map/ppermute | solution.py:36
  39.9 1.9 %collective-permute-start.5 = (bf16[512,256]{1,0:T(8,128)(2,1)S(1)}, bf16[512,256]{1,0:T(8,128)(2,1)S(1)}, u32[]{:S(2)}, u32[]{:S(2)}) collective-permute-start(bf16[512,256]{1,0:T(8,128)(2,1)S(1)} %collective-permute-done.3), channel_id=1, source_target_pairs={{0,64},{64,128},{128,192},{192,256},{256,320},{320,384},{384,448},... | collective-permute-start | bytes 786440 | tf_op jit(solution)/shard_map/ppermute | solution.py:36
  41.8 5.8 %collective-permute-done.1 = bf16[256,256]{1,0:T(8,128)(2,1)S(1)} collective-permute-done((bf16[256,256]{1,0:T(8,128)(2,1)}, bf16[256,256]{1,0:T(8,128)(2,1)S(1)}, u32[]{:S(2)}, u32[]{:S(2)}) %collective-permute-start.1) | collective-permute-done | bytes 131104 | tf_op jit(solution)/shard_map/ppermute | solution.py:21
  47.6 0.0 collective-permute-done.4
  47.6 0.1 pad_maximum_fusion
  47.7 1.9 %collective-permute-start.8 = (bf16[2304,256]{1,0:T(8,128)(2,1)S(1)}, bf16[2304,256]{1,0:T(8,128)(2,1)S(1)}, u32[]{:S(2)}, u32[]{:S(2)}) collective-permute-start(bf16[2304,256]{1,0:T(8,128)(2,1)S(1)} %pad_maximum_fusion), channel_id=1, source_target_pairs={{0,32},{32,0},{1,33},{33,1},{2,34},{34,2},{3,35},{35,3},{4,36},{36... | collective-permute-start | bytes 3538952 | tf_op jit(solution)/shard_map/ppermute | solution.py:21
  49.6 0.0 collective-permute-done.6
  49.6 0.7 collective-permute-done.5
  50.3 3.6 %collective-permute-start.7 = (bf16[768,256]{1,0:T(8,128)(2,1)S(1)}, bf16[768,256]{1,0:T(8,128)(2,1)S(1)}, u32[]{:S(2)}, u32[]{:S(2)}) collective-permute-start(bf16[768,256]{1,0:T(8,128)(2,1)S(1)} %pad_maximum_fusion.3), channel_id=1, source_target_pairs={{0,512},{512,0},{1,513},{513,1},{2,514},{514,2},{3,515},{515,3},{4... | collective-permute-start | bytes 1179656 | tf_op jit(solution)/shard_map/ppermute | solution.py:21
  54.6 0.0 copy-start
  54.7 0.0 copy-start.1
  54.7 0.0 copy-start.2
  54.7 8.4 %collective-permute-done.7 = bf16[768,256]{1,0:T(8,128)(2,1)S(1)} collective-permute-done((bf16[768,256]{1,0:T(8,128)(2,1)S(1)}, bf16[768,256]{1,0:T(8,128)(2,1)S(1)}, u32[]{:S(2)}, u32[]{:S(2)}) %collective-permute-start.7) | collective-permute-done | bytes 393248 | tf_op jit(solution)/shard_map/ppermute | solution.py:21
  63.1 0.1 pad_maximum_fusion.1
  63.1 1.9 %collective-permute-start.9 = (bf16[1536,256]{1,0:T(8,128)(2,1)S(1)}, bf16[1536,256]{1,0:T(8,128)(2,1)S(1)}, u32[]{:S(2)}, u32[]{:S(2)}) collective-permute-start(bf16[1536,256]{1,0:T(8,128)(2,1)S(1)} %pad_maximum_fusion.1), channel_id=1, source_target_pairs={{0,32},{32,0},{1,33},{33,1},{2,34},{34,2},{3,35},{35,3},{4,36},{36... | collective-permute-start | bytes 2359304 | tf_op jit(solution)/shard_map/ppermute | solution.py:21
  65.2 0.0 collective-permute-done.8
  65.2 0.1 constant_dynamic-update-slice_fusion.3
  65.3 2.0 %collective-permute-done.9 = bf16[1536,256]{1,0:T(8,128)(2,1)S(1)} collective-permute-done((bf16[1536,256]{1,0:T(8,128)(2,1)S(1)}, bf16[1536,256]{1,0:T(8,128)(2,1)S(1)}, u32[]{:S(2)}, u32[]{:S(2)}) %collective-permute-start.9) | collective-permute-done | bytes 786464 | tf_op jit(solution)/shard_map/ppermute | solution.py:21
  67.3 0.1 constant_dynamic-update-slice_fusion.2.panels
  67.4 0.0 copy-done
  67.4 0.0 copy-done.1
  67.4 0.0 copy-done.2
  67.4 6.4 %tile_products.1 = (bf16[3072,256]{1,0:T(8,128)(2,1)S(1)}, bf16[1024,256]{1,0:T(8,128)(2,1)S(1)}, bf16[1024,256]{1,0:T(8,128)(2,1)S(1)}, bf16[1024,256]{1,0:T(8,...) custom-call(s32[1]{0:T(128)S(6)} %copy.19.count, s32[24]{0:T(128)S(1)} %copy-done.1, ...), custom_call_target="tpu_custom_call" | custom-call | flops 1073741824 | bytes 8388608 | tf_op jit(solution)/shard_map/tile_products/pallas_call | solution.py:100
  73.8 0.0 copy-start.5
  73.8 0.0 copy-start.3
  73.8 0.0 copy-start.4
  73.8 2.1 %collective-permute-start.14 = (bf16[3072,256]{1,0:T(8,128)(2,1)S(1)}, bf16[3072,256]{1,0:T(8,128)(2,1)S(1)}, u32[]{:S(2)}, u32[]{:S(2)}) collective-permute-start(bf16[3072,256]{1,0:T(8,128)(2,1)S(1)} %get-tuple-element.18), channel_id=1, source_target_pairs={{0,32},{32,0},{1,33},{33,1},{2,34},{34,2},{3,35},{35,3},{4,36},{36... | collective-permute-start | bytes 4718600 | tf_op jit(solution)/shard_map/ppermute | solution.py:21
  75.9 3.4 %collective-permute-done.14 = bf16[3072,256]{1,0:T(8,128)(2,1)S(1)} collective-permute-done((bf16[3072,256]{1,0:T(8,128)(2,1)S(1)}, bf16[3072,256]{1,0:T(8,128)(2,1)S(1)}, u32[]{:S(2)}, u32[]{:S(2)}) %collective-permute-start.14) | collective-permute-done | bytes 1572896 | tf_op jit(solution)/shard_map/ppermute | solution.py:21
  79.3 4.3 %collective-permute-start.15 = (bf16[1024,256]{1,0:T(8,128)(2,1)S(1)}, bf16[1024,256]{1,0:T(8,128)(2,1)S(1)}, u32[]{:S(2)}, u32[]{:S(2)}) collective-permute-start(bf16[1024,256]{1,0:T(8,128)(2,1)S(1)} %slice.19), channel_id=1, source_target_pairs={{0,1},{1,2},{2,3},{3,4},{4,5},{5,6},{6,7},{7,0},{32,39},{33,32},{3... | collective-permute-start | bytes 1572872 | tf_op jit(solution)/shard_map/ppermute | solution.py:36
  83.6 1.9 %collective-permute-start.10 = (bf16[1024,256]{1,0:T(8,128)(2,1)S(1)}, bf16[1024,256]{1,0:T(8,128)(2,1)S(1)}, u32[]{:S(2)}, u32[]{:S(2)}) collective-permute-start(bf16[1024,256]{1,0:T(8,128)(2,1)S(1)} %get-tuple-element.16), channel_id=1, source_target_pairs={{0,1},{1,2},{2,3},{3,4},{4,5},{5,6},{6,7},{7,0},{32,39},{33,32},{3... | collective-permute-start | bytes 1572872 | tf_op jit(solution)/shard_map/ppermute | solution.py:36
  85.5 4.0 %collective-permute-start.11 = (bf16[1024,256]{1,0:T(8,128)(2,1)S(1)}, bf16[1024,256]{1,0:T(8,128)(2,1)S(1)}, u32[]{:S(2)}, u32[]{:S(2)}) collective-permute-start(bf16[1024,256]{1,0:T(8,128)(2,1)S(1)} %get-tuple-element.17), channel_id=1, source_target_pairs={{0,2},{1,3},{2,4},{3,5},{4,6},{5,7},{6,0},{7,1},{32,38},{33,39},{3... | collective-permute-start | bytes 1572872 | tf_op jit(solution)/shard_map/ppermute | solution.py:36
  89.6 0.8 collective-permute-done.15
  90.4 0.1 add_convert_fusion.2
  90.5 5.5 %collective-permute-start.16 = (bf16[1024,256]{1,0:T(8,128)(2,1)S(1)}, bf16[1024,256]{1,0:T(8,128)(2,1)S(1)}, u32[]{:S(2)}, u32[]{:S(2)}) collective-permute-start(bf16[1024,256]{1,0:T(8,128)(2,1)S(1)} %add_convert_fusion.2), channel_id=1, source_target_pairs={{0,1},{1,2},{2,3},{3,4},{4,5},{5,6},{6,7},{7,0},{32,39},{33,32},{3... | collective-permute-start | bytes 1572872 | tf_op jit(solution)/shard_map/ppermute | solution.py:36
  96.0 1.2 collective-permute-done.10
  97.2 11.4 %collective-permute-done.11 = bf16[1024,256]{1,0:T(8,128)(2,1)S(1)} collective-permute-done((bf16[1024,256]{1,0:T(8,128)(2,1)S(1)}, bf16[1024,256]{1,0:T(8,128)(2,1)S(1)}, u32[]{:S(2)}, u32[]{:S(2)}) %collective-permute-start.11) | collective-permute-done | bytes 524320 | tf_op jit(solution)/shard_map/ppermute | solution.py:36
  108.6 0.2 add_convert_fusion.4
  108.9 1.9 %collective-permute-start.12 = (bf16[1024,256]{1,0:T(8,128)(2,1)S(1)}, bf16[1024,256]{1,0:T(8,128)(2,1)S(1)}, u32[]{:S(2)}, u32[]{:S(2)}) collective-permute-start(bf16[1024,256]{1,0:T(8,128)(2,1)S(1)} %add_convert_fusion.4), channel_id=1, source_target_pairs={{0,1},{1,2},{2,3},{3,4},{4,5},{5,6},{6,7},{7,0},{32,39},{33,32},{3... | collective-permute-start | bytes 1572872 | tf_op jit(solution)/shard_map/ppermute | solution.py:36
  110.8 2.2 %collective-permute-done.16 = bf16[1024,256]{1,0:T(8,128)(2,1)S(1)} collective-permute-done((bf16[1024,256]{1,0:T(8,128)(2,1)S(1)}, bf16[1024,256]{1,0:T(8,128)(2,1)S(1)}, u32[]{:S(2)}, u32[]{:S(2)}) %collective-permute-start.16) | collective-permute-done | bytes 524320 | tf_op jit(solution)/shard_map/ppermute | solution.py:36
  113.0 0.1 add_convert_fusion.1
  113.1 5.4 %collective-permute-start.17 = (bf16[1024,256]{1,0:T(8,128)(2,1)S(1)}, bf16[1024,256]{1,0:T(8,128)(2,1)S(1)}, u32[]{:S(2)}, u32[]{:S(2)}) collective-permute-start(bf16[1024,256]{1,0:T(8,128)(2,1)S(1)} %add_convert_fusion.1), channel_id=1, source_target_pairs={{0,1},{1,2},{2,3},{3,4},{4,5},{5,6},{6,7},{7,0},{32,39},{33,32},{3... | collective-permute-start | bytes 1572872 | tf_op jit(solution)/shard_map/ppermute | solution.py:36
  118.5 1.4 collective-permute-done.12
  119.9 0.1 add_convert_fusion.3
  120.1 4.1 %collective-permute-start.13 = (bf16[1024,256]{1,0:T(8,128)(2,1)S(1)}, bf16[1024,256]{1,0:T(8,128)(2,1)S(1)}, u32[]{:S(2)}, u32[]{:S(2)}) collective-permute-start(bf16[1024,256]{1,0:T(8,128)(2,1)S(1)} %add_convert_fusion.3), channel_id=1, source_target_pairs={{0,1},{1,2},{2,3},{3,4},{4,5},{5,6},{6,7},{7,0},{32,39},{33,32},{3... | collective-permute-start | bytes 1572872 | tf_op jit(solution)/shard_map/ppermute | solution.py:36
  124.2 1.4 collective-permute-done.17
  125.5 1.9 %collective-permute-start.18 = (bf16[1024,256]{1,0:T(8,128)(2,1)S(1)}, bf16[1024,256]{1,0:T(8,128)(2,1)S(1)}, u32[]{:S(2)}, u32[]{:S(2)}) collective-permute-start(bf16[1024,256]{1,0:T(8,128)(2,1)S(1)} %collective-permute-done.17), channel_id=1, source_target_pairs={{0,32},{32,0},{1,33},{33,1},{2,34},{34,2},{3,35},{35,3},{4,36},{36... | collective-permute-start | bytes 1572872 | tf_op jit(solution)/shard_map/ppermute | solution.py:21
  127.5 0.0 copy-done.5
  127.5 0.0 copy-done.3
  127.5 0.1 multiply_add_fusion
  127.6 3.8 %collective-permute-done.13 = bf16[1024,256]{1,0:T(8,128)(2,1)S(1)} collective-permute-done((bf16[1024,256]{1,0:T(8,128)(2,1)S(1)}, bf16[1024,256]{1,0:T(8,128)(2,1)S(1)}, u32[]{:S(2)}, u32[]{:S(2)}) %collective-permute-start.13) | collective-permute-done | bytes 524320 | tf_op jit(solution)/shard_map/ppermute | solution.py:36
  131.5 0.0 collective-permute-done.18
  131.5 0.2 add_convert_fusion
  131.7 23.4 %all_to_all.9 = bf16[4,256,256]{2,1,0:T(8,128)(2,1)S(1)} all-to-all(bf16[4,256,256]{2,1,0:T(8,128)(2,1)S(1)} %bitcast.1), channel_id=1, replica_groups=mesh['ylo'=2,'z'=8,'core'=2,'yhi'=4,'x'=8] {'yhi'}, dimensions={0} | all-to-all | bytes 1048576 | tf_op jit(solution)/shard_map/all_to_all | solution.py:194
  155.1 0.1 convert_reduce_fusion
  155.2 0.7 add_convert_fusion.5
  (14 shorter events, 0.3 us)
Async XLA Ops:
  0.0 3.4 %collective-permute-start = (bf16[256,256]{1,0:T(8,128)(2,1)}, bf16[256,256]{1,0:T(8,128)(2,1)S(1)}, u32[]{:S(2)}, u32[]{:S(2)}) collective-permute-start(bf16[256,256]{1,0:T(8,128)(2,1)} %param.7), channel_id=1, source_target_pairs={{0,32},{32,0},{1,33},{33,1},{2,34},{34,2},{3,35},{35,3},{4,36},{36... | collective-permute-start | bytes 393224 | tf_op jit(solution)/shard_map/ppermute | solution.py:21
  3.5 21.7 %collective-permute-start.2 = (bf16[512,256]{1,0:T(8,128)(2,1)S(1)}, bf16[512,256]{1,0:T(8,128)(2,1)S(1)}, u32[]{:S(2)}, u32[]{:S(2)}) collective-permute-start(bf16[512,256]{1,0:T(8,128)(2,1)S(1)} %get-tuple-element.21), channel_id=1, source_target_pairs={{0,64},{64,128},{128,192},{192,256},{256,320},{320,384},{384,448},... | collective-permute-start | bytes 786440 | tf_op jit(solution)/shard_map/ppermute | solution.py:36
  8.7 23.4 %collective-permute-start.3 = (bf16[512,256]{1,0:T(8,128)(2,1)S(1)}, bf16[512,256]{1,0:T(8,128)(2,1)S(1)}, u32[]{:S(2)}, u32[]{:S(2)}) collective-permute-start(bf16[512,256]{1,0:T(8,128)(2,1)S(1)} %get-tuple-element.21), channel_id=1, source_target_pairs={{0,128},{64,192},{128,256},{192,320},{256,384},{320,448},{384,0},{... | collective-permute-start | bytes 786440 | tf_op jit(solution)/shard_map/ppermute | solution.py:36
  32.1 15.5 %collective-permute-start.4 = (bf16[1024,256]{1,0:T(8,128)(2,1)S(1)}, bf16[1024,256]{1,0:T(8,128)(2,1)S(1)}, u32[]{:S(2)}, u32[]{:S(2)}) collective-permute-start(bf16[1024,256]{1,0:T(8,128)(2,1)S(1)} %pad_maximum_fusion.2), channel_id=1, source_target_pairs={{0,512},{512,0},{1,513},{513,1},{2,514},{514,2},{3,515},{515,3},{4... | collective-permute-start | bytes 1572872 | tf_op jit(solution)/shard_map/ppermute | solution.py:21
  35.7 11.9 %collective-permute-start.1 = (bf16[256,256]{1,0:T(8,128)(2,1)}, bf16[256,256]{1,0:T(8,128)(2,1)S(1)}, u32[]{:S(2)}, u32[]{:S(2)}) collective-permute-start(bf16[256,256]{1,0:T(8,128)(2,1)} %param.7), channel_id=1, source_target_pairs={{0,512},{512,0},{1,513},{513,1},{2,514},{514,2},{3,515},{515,3},{4... | collective-permute-start | bytes 393224 | tf_op jit(solution)/shard_map/ppermute | solution.py:21
  38.0 11.6 %collective-permute-start.6 = (bf16[256,256]{1,0:T(8,128)(2,1)S(1)}, bf16[256,256]{1,0:T(8,128)(2,1)S(1)}, u32[]{:S(2)}, u32[]{:S(2)}) collective-permute-start(bf16[256,256]{1,0:T(8,128)(2,1)S(1)} %slice.16), channel_id=1, source_target_pairs={{0,128},{64,192},{128,256},{192,320},{256,384},{320,448},{384,0},{... | collective-permute-start | bytes 393224 | tf_op jit(solution)/shard_map/ppermute | solution.py:36
  39.9 10.4 %collective-permute-start.5 = (bf16[512,256]{1,0:T(8,128)(2,1)S(1)}, bf16[512,256]{1,0:T(8,128)(2,1)S(1)}, u32[]{:S(2)}, u32[]{:S(2)}) collective-permute-start(bf16[512,256]{1,0:T(8,128)(2,1)S(1)} %collective-permute-done.3), channel_id=1, source_target_pairs={{0,64},{64,128},{128,192},{192,256},{256,320},{320,384},{384,448},... | collective-permute-start | bytes 786440 | tf_op jit(solution)/shard_map/ppermute | solution.py:36
  47.7 17.5 %collective-permute-start.8 = (bf16[2304,256]{1,0:T(8,128)(2,1)S(1)}, bf16[2304,256]{1,0:T(8,128)(2,1)S(1)}, u32[]{:S(2)}, u32[]{:S(2)}) collective-permute-start(bf16[2304,256]{1,0:T(8,128)(2,1)S(1)} %pad_maximum_fusion), channel_id=1, source_target_pairs={{0,32},{32,0},{1,33},{33,1},{2,34},{34,2},{3,35},{35,3},{4,36},{36... | collective-permute-start | bytes 3538952 | tf_op jit(solution)/shard_map/ppermute | solution.py:21
  50.3 12.7 %collective-permute-start.7 = (bf16[768,256]{1,0:T(8,128)(2,1)S(1)}, bf16[768,256]{1,0:T(8,128)(2,1)S(1)}, u32[]{:S(2)}, u32[]{:S(2)}) collective-permute-start(bf16[768,256]{1,0:T(8,128)(2,1)S(1)} %pad_maximum_fusion.3), channel_id=1, source_target_pairs={{0,512},{512,0},{1,513},{513,1},{2,514},{514,2},{3,515},{515,3},{4... | collective-permute-start | bytes 1179656 | tf_op jit(solution)/shard_map/ppermute | solution.py:21
  54.6 12.7 %copy-start = (bf16[24,256,256]{2,1,0:T(8,128)(2,1)S(1)}, bf16[24,256,256]{2,1,0:T(8,128)(2,1)}, u32[]{:S(2)}) copy-start(bf16[24,256,256]{2,1,0:T(8,128)(2,1)} %tiles.1) | copy-start | bytes 9437188
  54.7 12.7 %copy-start.1 = (s32[24]{0:T(128)S(1)}, s32[24]{0:T(128)}, u32[]{:S(2)}) copy-start(s32[24]{0:T(128)} %rows.1) | copy-start | bytes 292
  54.7 12.7 %copy-start.2 = (s32[24]{0:T(128)S(1)}, s32[24]{0:T(128)}, u32[]{:S(2)}) copy-start(s32[24]{0:T(128)} %srcs.1) | copy-start | bytes 292
  63.1 4.2 %collective-permute-start.9 = (bf16[1536,256]{1,0:T(8,128)(2,1)S(1)}, bf16[1536,256]{1,0:T(8,128)(2,1)S(1)}, u32[]{:S(2)}, u32[]{:S(2)}) collective-permute-start(bf16[1536,256]{1,0:T(8,128)(2,1)S(1)} %pad_maximum_fusion.1), channel_id=1, source_target_pairs={{0,32},{32,0},{1,33},{33,1},{2,34},{34,2},{3,35},{35,3},{4,36},{36... | collective-permute-start | bytes 2359304 | tf_op jit(solution)/shard_map/ppermute | solution.py:21
  73.8 53.7 %copy-start.5 = (s32[256]{0:T(256)S(1)}, s32[256]{0:T(256)}, u32[]{:S(2)}) copy-start(s32[256]{0:T(256)} %param.13) | copy-start | bytes 3076
  73.8 53.7 %copy-start.3 = (bf16[256,256]{1,0:T(8,128)(2,1)S(1)}, bf16[256,256]{1,0:T(8,128)(2,1)}, u32[]{:S(2)}) copy-start(bf16[256,256]{1,0:T(8,128)(2,1)} %param.7) | copy-start | bytes 393220
  73.8 53.7 %copy-start.4 = (bf16[256,256]{1,0:T(8,128)(2,1)S(1)}, bf16[256,256]{1,0:T(8,128)(2,1)}, u32[]{:S(2)}) copy-start(bf16[256,256]{1,0:T(8,128)(2,1)} %param.8) | copy-start | bytes 393220
  73.8 5.4 %collective-permute-start.14 = (bf16[3072,256]{1,0:T(8,128)(2,1)S(1)}, bf16[3072,256]{1,0:T(8,128)(2,1)S(1)}, u32[]{:S(2)}, u32[]{:S(2)}) collective-permute-start(bf16[3072,256]{1,0:T(8,128)(2,1)S(1)} %get-tuple-element.18), channel_id=1, source_target_pairs={{0,32},{32,0},{1,33},{33,1},{2,34},{34,2},{3,35},{35,3},{4,36},{36... | collective-permute-start | bytes 4718600 | tf_op jit(solution)/shard_map/ppermute | solution.py:21
  79.3 11.1 %collective-permute-start.15 = (bf16[1024,256]{1,0:T(8,128)(2,1)S(1)}, bf16[1024,256]{1,0:T(8,128)(2,1)S(1)}, u32[]{:S(2)}, u32[]{:S(2)}) collective-permute-start(bf16[1024,256]{1,0:T(8,128)(2,1)S(1)} %slice.19), channel_id=1, source_target_pairs={{0,1},{1,2},{2,3},{3,4},{4,5},{5,6},{6,7},{7,0},{32,39},{33,32},{3... | collective-permute-start | bytes 1572872 | tf_op jit(solution)/shard_map/ppermute | solution.py:36
  83.6 13.6 %collective-permute-start.10 = (bf16[1024,256]{1,0:T(8,128)(2,1)S(1)}, bf16[1024,256]{1,0:T(8,128)(2,1)S(1)}, u32[]{:S(2)}, u32[]{:S(2)}) collective-permute-start(bf16[1024,256]{1,0:T(8,128)(2,1)S(1)} %get-tuple-element.16), channel_id=1, source_target_pairs={{0,1},{1,2},{2,3},{3,4},{4,5},{5,6},{6,7},{7,0},{32,39},{33,32},{3... | collective-permute-start | bytes 1572872 | tf_op jit(solution)/shard_map/ppermute | solution.py:36
  85.5 23.1 %collective-permute-start.11 = (bf16[1024,256]{1,0:T(8,128)(2,1)S(1)}, bf16[1024,256]{1,0:T(8,128)(2,1)S(1)}, u32[]{:S(2)}, u32[]{:S(2)}) collective-permute-start(bf16[1024,256]{1,0:T(8,128)(2,1)S(1)} %get-tuple-element.17), channel_id=1, source_target_pairs={{0,2},{1,3},{2,4},{3,5},{4,6},{5,7},{6,0},{7,1},{32,38},{33,39},{3... | collective-permute-start | bytes 1572872 | tf_op jit(solution)/shard_map/ppermute | solution.py:36
  90.5 22.4 %collective-permute-start.16 = (bf16[1024,256]{1,0:T(8,128)(2,1)S(1)}, bf16[1024,256]{1,0:T(8,128)(2,1)S(1)}, u32[]{:S(2)}, u32[]{:S(2)}) collective-permute-start(bf16[1024,256]{1,0:T(8,128)(2,1)S(1)} %add_convert_fusion.2), channel_id=1, source_target_pairs={{0,1},{1,2},{2,3},{3,4},{4,5},{5,6},{6,7},{7,0},{32,39},{33,32},{3... | collective-permute-start | bytes 1572872 | tf_op jit(solution)/shard_map/ppermute | solution.py:36
  108.9 11.1 %collective-permute-start.12 = (bf16[1024,256]{1,0:T(8,128)(2,1)S(1)}, bf16[1024,256]{1,0:T(8,128)(2,1)S(1)}, u32[]{:S(2)}, u32[]{:S(2)}) collective-permute-start(bf16[1024,256]{1,0:T(8,128)(2,1)S(1)} %add_convert_fusion.4), channel_id=1, source_target_pairs={{0,1},{1,2},{2,3},{3,4},{4,5},{5,6},{6,7},{7,0},{32,39},{33,32},{3... | collective-permute-start | bytes 1572872 | tf_op jit(solution)/shard_map/ppermute | solution.py:36
  113.1 12.5 %collective-permute-start.17 = (bf16[1024,256]{1,0:T(8,128)(2,1)S(1)}, bf16[1024,256]{1,0:T(8,128)(2,1)S(1)}, u32[]{:S(2)}, u32[]{:S(2)}) collective-permute-start(bf16[1024,256]{1,0:T(8,128)(2,1)S(1)} %add_convert_fusion.1), channel_id=1, source_target_pairs={{0,1},{1,2},{2,3},{3,4},{4,5},{5,6},{6,7},{7,0},{32,39},{33,32},{3... | collective-permute-start | bytes 1572872 | tf_op jit(solution)/shard_map/ppermute | solution.py:36
  120.1 11.4 %collective-permute-start.13 = (bf16[1024,256]{1,0:T(8,128)(2,1)S(1)}, bf16[1024,256]{1,0:T(8,128)(2,1)S(1)}, u32[]{:S(2)}, u32[]{:S(2)}) collective-permute-start(bf16[1024,256]{1,0:T(8,128)(2,1)S(1)} %add_convert_fusion.3), channel_id=1, source_target_pairs={{0,1},{1,2},{2,3},{3,4},{4,5},{5,6},{6,7},{7,0},{32,39},{33,32},{3... | collective-permute-start | bytes 1572872 | tf_op jit(solution)/shard_map/ppermute | solution.py:36
  125.5 5.9 %collective-permute-start.18 = (bf16[1024,256]{1,0:T(8,128)(2,1)S(1)}, bf16[1024,256]{1,0:T(8,128)(2,1)S(1)}, u32[]{:S(2)}, u32[]{:S(2)}) collective-permute-start(bf16[1024,256]{1,0:T(8,128)(2,1)S(1)} %collective-permute-done.17), channel_id=1, source_target_pairs={{0,32},{32,0},{1,33},{33,1},{2,34},{34,2},{3,35},{35,3},{4,36},{36... | collective-permute-start | bytes 1572872 | tf_op jit(solution)/shard_map/ppermute | solution.py:21

commit v7 on v6

--- a/solution.py
+++ b/solution.py
@@ -121,37 +121,23 @@
 
 def gather_panels(flow_cols):
     side = flow_cols.shape[0]
-    pair = jnp.concatenate([flow_cols, shifted(flow_cols, "core", 1)], 0)
-    far2, far1 = sent_outward(pair, "z", 2), sent_outward(pair, "z", 1)
-    far3, far4 = sent_outward(far2, "z", 1), sent_outward(far2[:side], "z", 2)
-    far12, far34 = jnp.concatenate([far1, far2], 0), jnp.concatenate([far3, far4], 0)
-    first = [shifted(flow_cols, "ylo", 1), far12, shifted(far12, "ylo", 1)]
-    second = [far34, shifted(far34, "ylo", 1)]
-    swapped = [shifted(jnp.concatenate(part, 0), "core", 1) for part in (first, second)]
-    return jnp.concatenate([pair] + first + second + swapped, 0)
+    own = jnp.concatenate([flow_cols, shifted(flow_cols, "ylo", 1)], 0)
+    below1, above1 = shifted(own, "z", 1), shifted(own, "z", -1)
+    below2, above2 = shifted(own, "z", 2), shifted(own, "z", -2)
+    below3, above3 = shifted(below2, "z", 1), shifted(above2, "z", -1)
+    below4, above4 = shifted(below2[:side], "z", 2), shifted(above2[side:], "z", -2)
+    near = jnp.concatenate(
+        [own, below1, above1, below2, above2, below3, above3, below4, above4], 0
+    )
+    return jnp.concatenate([near, shifted(near, "core", 1)], 0)
 
 
 def panel_place(src, my_ylo, my_z, my_core):
     off_ylo = (src // (N_CORE * N_Z) + N_YLO - my_ylo) % N_YLO
     off_z = (src // N_CORE % N_Z + N_Z - my_z) % N_Z
     off_core = (src % N_CORE + N_CORE - my_core) % N_CORE
-    far = jnp.where(my_core == 0, (N_Z - off_z) % N_Z, off_z)
-    half = N_Z // 2
-    theirs = (
-        ((far == 0) & (off_ylo + off_core == 2)) | ((far == half) & (off_core == 1)) | (far > half)
-    )
-    far = jnp.where(theirs, (N_Z - far) % N_Z, far)
-    off_core = jnp.where(theirs, 1 - off_core, off_core)
-    place = jnp.where(
-        far == 0,
-        jnp.where(off_ylo == 0, off_core, 2),
-        jnp.where(
-            far <= 2,
-            1 + 2 * far + off_core + 4 * off_ylo,
-            jnp.where(far == 3, 11 + off_core, 13) + 3 * off_ylo,
-        ),
-    )
-    return place + jnp.where(theirs, 15, 0)
+    slot = jnp.where(off_z >= N_Z // 2, (N_Z - off_z) * 2 - 1, 2 * off_z)
+    return (off_core * N_Z + slot) * N_YLO + off_ylo
 
 
 def add(*terms):
@@ -162,14 +148,16 @@
 
 
 def reduce_along_x(products):
-    give, keep4, keep3, keep2, keep1, own = products
+    (keep4,) = products([(4,)])
+    give, keep3, keep2, keep1, own = products([(-3, -2, -1), (3,), (2,), (1,), (0,)])
     chunk = own.shape[0]
+    mine = sent_outward(keep4, "x", 1)
     got = shifted(give, "core", 1)
     got3, got2, got1 = (got[i * chunk : (i + 1) * chunk] for i in range(3))
-    other, mine = sent_outward(got3, "x", 1), sent_outward(keep3, "x", 1)
-    mine = add(keep2, mine, sent_outward(keep4, "x", 2))
+    other = sent_outward(got3, "x", 1)
+    mine = sent_outward(add(keep3, mine), "x", 1)
     other = sent_outward(add(got2, other), "x", 1)
-    mine = sent_outward(mine, "x", 1)
+    mine = sent_outward(add(keep2, mine), "x", 1)
     other = sent_outward(add(got1, other), "x", 1)
     mine = sent_outward(add(keep1, mine), "x", 1)
     return add(own, mine, shifted(other, "core", 1))
@@ -179,14 +167,9 @@
     side, columns = flow_cols.shape
     panels = gather_panels(flow_cols)
 
-    products = partial_products(
-        [(-3, -2, -1), (4,), (3,), (2,), (1,), (0,)],
-        tile_blocks,
-        tile_rows,
-        tile_srcs,
-        tile_count,
-        panels,
-    )
+    def products(chunks):
+        return partial_products(chunks, tile_blocks, tile_rows, tile_srcs, tile_count, panels)
+
     own_flow = flow_cols.astype(jnp.float32)
     mask_col = dangling.astype(jnp.float32)[:, None]
     constant = DAMP * (mask_col * own_flow) + (1.0 - DAMP) * restart.astype(jnp.float32)

time: 157 us -> 145 us (0.924)
  waiting for transfers between devices: 58.5 us -> 29.6 us
  starting transfers between devices: 63.3 us -> 76.7 us
  local copies, waits for them, and re-layouts: 1.3 us -> 3.18 us
    ppermute x8 -> x12, starting transfers between devices: 19.2 us -> 50.7 us  [shifted(): lax.ppermute(value, axis, [(i, (i + by) % size) for i in range(size)])]
    ppermute x11 -> x7, waiting for transfers between devices: 38.4 us -> 17.3 us  [sent_outward(): return lax.ppermute(value, names, pairs)]
    ppermute x11 -> x7, starting transfers between devices: 44.1 us -> 26 us  [sent_outward(): return lax.ppermute(value, names, pairs)]
    ppermute x8 -> x12, waiting for transfers between devices: 20.1 us -> 12.3 us  [shifted(): lax.ppermute(value, axis, [(i, (i + by) % size) for i in range(size)])]
    unnamed x21, local copies, waits for them, and re-layouts: 1.19 us -> 2.97 us
    pallas_call x1 -> x2, Pallas kernels: 6.41 us -> 6.83 us  [partial_products(): pl.pallas_call(functools.partial(tiles_kernel, chunks), out_shape=[jax.Sh...]
  transfers between devices with their start and end apart: 19 -> 19, of which waited for: 15 -> 11; matrix products, arithmetic and copies ran while one was open for 1% -> 1% of each run, Pallas kernels for 0% -> 1%
where the time goes in v7:
time: 145 us; the launch traced here: 143 us
  starting transfers between devices  76.7 us (53%)
  waiting for transfers between devices  29.6 us (20%)
  blocking collectives  23.4 us (16%)
  Pallas kernels  6.83 us (5%)
  local copies, waits for them, and re-layouts  3.18 us (2%)
  other arithmetic  1.84 us (1%)
    ppermute x12, starting transfers between devices, shifted(): lax.ppermute(value, axis, [(i, (i + by) % size) for i in range(size)])  50.7 us
    ppermute x7, starting transfers between devices, sent_outward(): return lax.ppermute(value, names, pairs)  26 us
    all_to_all x1, blocking collectives, body(): lax.all_to_all(along_x, 'yhi', 0, 0, tiled=True)  23.4 us
    ppermute x7, waiting for transfers between devices, sent_outward(): return lax.ppermute(value, names, pairs)  17.3 us
    ppermute x12, waiting for transfers between devices, shifted(): lax.ppermute(value, axis, [(i, (i + by) % size) for i in range(size)])  12.3 us
    pallas_call x2, Pallas kernels, partial_products(): pl.pallas_call(functools.partial(tiles_kernel, chunks), out_shape=[jax.Sh...  6.83 us
    unnamed x21, local copies, waits for them, and re-layouts  2.97 us
  transfers between devices with their start and end apart: 19, of which 11 were waited for; matrix products, arithmetic and copies ran while one was open for 1% of the time, Pallas kernels for 1%

profile of v7, /device:TPU:14, one launch (start us, length us, event | category | flops | bytes accessed | tf_op | source)
XLA Modules:
  0.0 142.6 jit_solution(12706512642913556775)
XLA Ops:
  0.0 3.6 %collective-permute-start = (bf16[256,256]{1,0:T(8,128)(2,1)}, bf16[256,256]{1,0:T(8,128)(2,1)S(1)}, u32[]{:S(2)}, u32[]{:S(2)}) collective-permute-start(bf16[256,256]{1,0:T(8,128)(2,1)} %param.7), channel_id=1, source_target_pairs={{0,512},{512,0},{1,513},{513,1},{2,514},{514,2},{3,515},{515,3},{4... | collective-permute-start | bytes 393224 | tf_op jit(solution)/shard_map/ppermute | solution.py:21
  3.6 0.9 constant_dynamic-update-slice_fusion.11
  4.5 2.8 %collective-permute-done = bf16[256,256]{1,0:T(8,128)(2,1)S(1)} collective-permute-done((bf16[256,256]{1,0:T(8,128)(2,1)}, bf16[256,256]{1,0:T(8,128)(2,1)S(1)}, u32[]{:S(2)}, u32[]{:S(2)}) %collective-permute-start) | collective-permute-done | bytes 131104 | tf_op jit(solution)/shard_map/ppermute | solution.py:21
  7.4 7.9 %collective-permute-start.3 = (bf16[512,256]{1,0:T(8,128)(2,1)S(1)}, bf16[512,256]{1,0:T(8,128)(2,1)S(1)}, u32[]{:S(2)}, u32[]{:S(2)}) collective-permute-start(bf16[512,256]{1,0:T(8,128)(2,1)S(1)} %get-tuple-element.37), channel_id=1, source_target_pairs={{0,128},{64,192},{128,256},{192,320},{256,384},{320,448},{384,0},{... | collective-permute-start | bytes 786440 | tf_op jit(solution)/shard_map/ppermute | solution.py:21
  15.3 10.4 %collective-permute-start.4 = (bf16[512,256]{1,0:T(8,128)(2,1)S(1)}, bf16[512,256]{1,0:T(8,128)(2,1)S(1)}, u32[]{:S(2)}, u32[]{:S(2)}) collective-permute-start(bf16[512,256]{1,0:T(8,128)(2,1)S(1)} %get-tuple-element.37), channel_id=1, source_target_pairs={{0,384},{64,448},{128,0},{192,64},{256,128},{320,192},{384,256},{4... | collective-permute-start | bytes 786440 | tf_op jit(solution)/shard_map/ppermute | solution.py:21
  25.7 4.3 %collective-permute-start.1 = (bf16[512,256]{1,0:T(8,128)(2,1)S(1)}, bf16[512,256]{1,0:T(8,128)(2,1)S(1)}, u32[]{:S(2)}, u32[]{:S(2)}) collective-permute-start(bf16[512,256]{1,0:T(8,128)(2,1)S(1)} %get-tuple-element.37), channel_id=1, source_target_pairs={{0,64},{64,128},{128,192},{192,256},{256,320},{320,384},{384,448},... | collective-permute-start | bytes 786440 | tf_op jit(solution)/shard_map/ppermute | solution.py:21
  30.0 3.4 %collective-permute-start.2 = (bf16[512,256]{1,0:T(8,128)(2,1)S(1)}, bf16[512,256]{1,0:T(8,128)(2,1)S(1)}, u32[]{:S(2)}, u32[]{:S(2)}) collective-permute-start(bf16[512,256]{1,0:T(8,128)(2,1)S(1)} %get-tuple-element.37), channel_id=1, source_target_pairs={{0,448},{64,0},{128,64},{192,128},{256,192},{320,256},{384,320},{4... | collective-permute-start | bytes 786440 | tf_op jit(solution)/shard_map/ppermute | solution.py:21
  33.4 2.4 %collective-permute-done.3 = bf16[512,256]{1,0:T(8,128)(2,1)S(1)} collective-permute-done((bf16[512,256]{1,0:T(8,128)(2,1)S(1)}, bf16[512,256]{1,0:T(8,128)(2,1)S(1)}, u32[]{:S(2)}, u32[]{:S(2)}) %collective-permute-start.3) | collective-permute-done | bytes 262176 | tf_op jit(solution)/shard_map/ppermute | solution.py:21
  35.8 1.9 %collective-permute-start.7 = (bf16[256,256]{1,0:T(8,128)(2,1)S(1)}, bf16[256,256]{1,0:T(8,128)(2,1)S(1)}, u32[]{:S(2)}, u32[]{:S(2)}) collective-permute-start(bf16[256,256]{1,0:T(8,128)(2,1)S(1)} %slice.20), channel_id=1, source_target_pairs={{0,128},{64,192},{128,256},{192,320},{256,384},{320,448},{384,0},{... | collective-permute-start | bytes 393224 | tf_op jit(solution)/shard_map/ppermute | solution.py:21
  37.7 0.0 collective-permute-done.4
  37.8 6.0 %collective-permute-start.8 = (bf16[256,256]{1,0:T(8,128)(2,1)S(1)}, bf16[256,256]{1,0:T(8,128)(2,1)S(1)}, u32[]{:S(2)}, u32[]{:S(2)}) collective-permute-start(bf16[256,256]{1,0:T(8,128)(2,1)S(1)} %slice.21), channel_id=1, source_target_pairs={{0,384},{64,448},{128,0},{192,64},{256,128},{320,192},{384,256},{4... | collective-permute-start | bytes 393224 | tf_op jit(solution)/shard_map/ppermute | solution.py:21
  43.8 2.6 %collective-permute-start.5 = (bf16[512,256]{1,0:T(8,128)(2,1)S(1)}, bf16[512,256]{1,0:T(8,128)(2,1)S(1)}, u32[]{:S(2)}, u32[]{:S(2)}) collective-permute-start(bf16[512,256]{1,0:T(8,128)(2,1)S(1)} %collective-permute-done.3), channel_id=1, source_target_pairs={{0,64},{64,128},{128,192},{192,256},{256,320},{320,384},{384,448},... | collective-permute-start | bytes 786440 | tf_op jit(solution)/shard_map/ppermute | solution.py:21
  46.4 0.0 collective-permute-done.1
  46.4 4.4 %collective-permute-start.6 = (bf16[512,256]{1,0:T(8,128)(2,1)S(1)}, bf16[512,256]{1,0:T(8,128)(2,1)S(1)}, u32[]{:S(2)}, u32[]{:S(2)}) collective-permute-start(bf16[512,256]{1,0:T(8,128)(2,1)S(1)} %collective-permute-done.4), channel_id=1, source_target_pairs={{0,448},{64,0},{128,64},{192,128},{256,192},{320,256},{384,320},{4... | collective-permute-start | bytes 786440 | tf_op jit(solution)/shard_map/ppermute | solution.py:21
  50.9 0.0 collective-permute-done.2
  51.1 2.2 %collective-permute-done.5 = bf16[512,256]{1,0:T(8,128)(2,1)S(1)} collective-permute-done((bf16[512,256]{1,0:T(8,128)(2,1)S(1)}, bf16[512,256]{1,0:T(8,128)(2,1)S(1)}, u32[]{:S(2)}, u32[]{:S(2)}) %collective-permute-start.5) | collective-permute-done | bytes 262176 | tf_op jit(solution)/shard_map/ppermute | solution.py:21
  53.3 1.4 %collective-permute-done.6 = bf16[512,256]{1,0:T(8,128)(2,1)S(1)} collective-permute-done((bf16[512,256]{1,0:T(8,128)(2,1)S(1)}, bf16[512,256]{1,0:T(8,128)(2,1)S(1)}, u32[]{:S(2)}, u32[]{:S(2)}) %collective-permute-start.6) | collective-permute-done | bytes 262176 | tf_op jit(solution)/shard_map/ppermute | solution.py:21
  54.8 0.0 collective-permute-done.7
  54.8 0.0 collective-permute-done.8
  54.9 1.9 %collective-permute-start.9 = (bf16[4096,256]{1,0:T(8,128)(2,1)S(1)}, bf16[4096,256]{1,0:T(8,128)(2,1)S(1)}, u32[]{:S(2)}, u32[]{:S(2)}) collective-permute-start(bf16[4096,256]{1,0:T(8,128)(2,1)S(1)} %get-tuple-element.31), channel_id=1, source_target_pairs={{0,32},{32,0},{1,33},{33,1},{2,34},{34,2},{3,35},{35,3},{4,36},{36... | collective-permute-start | bytes 6291464 | tf_op jit(solution)/shard_map/ppermute | solution.py:21
  57.4 3.5 %collective-permute-done.9 = bf16[4096,256]{1,0:T(8,128)(2,1)S(1)} collective-permute-done((bf16[4096,256]{1,0:T(8,128)(2,1)S(1)}, bf16[4096,256]{1,0:T(8,128)(2,1)S(1)}, u32[]{:S(2)}, u32[]{:S(2)}) %collective-permute-start.9) | collective-permute-done | bytes 2097184 | tf_op jit(solution)/shard_map/ppermute | solution.py:21
  60.9 0.0 copy-start
  60.9 0.0 copy-start.1
  60.9 0.0 copy-start.2
  60.9 0.1 constant_dynamic-update-slice_fusion.12.panels
  61.1 1.7 %copy-done = bf16[24,256,256]{2,1,0:T(8,128)(2,1)S(1)} copy-done((bf16[24,256,256]{2,1,0:T(8,128)(2,1)S(1)}, bf16[24,256,256]{2,1,0:T(8,128)(2,1)}, u32[]{:S(2)}) %copy-start) | copy-done | bytes 3145752
  62.8 0.0 copy-done.1
  62.8 0.0 copy-done.2
  62.8 5.4 %tile_products.2 = (bf16[3072,256]{1,0:T(8,128)(2,1)S(1)}, bf16[1024,256]{1,0:T(8,128)(2,1)S(1)}, bf16[1024,256]{1,0:T(8,128)(2,1)S(1)}, bf16[1024,256]{1,0:T(8,128)(2,1)S(1)}, bf16[1024,256]{1,0:T(8,128)(2,1)S(1)}) custom-call(s32[1]{0:T(128)S(6)} %copy.28.count, s32[24]{0:T(128)S(1)} %copy-done.1, s32[24]{0:T(128)S(1)} %copy-done.2, ...), custom_call_target="tpu_custom_call" | custom-call | flops 939524096 | bytes 7340032 | tf_op jit(solution)/shard_map/tile_products/pallas_call | solution.py:100
  68.2 2.3 %collective-permute-start.14 = (bf16[3072,256]{1,0:T(8,128)(2,1)S(1)}, bf16[3072,256]{1,0:T(8,128)(2,1)S(1)}, u32[]{:S(2)}, u32[]{:S(2)}) collective-permute-start(bf16[3072,256]{1,0:T(8,128)(2,1)S(1)} %get-tuple-element.16), channel_id=1, source_target_pairs={{0,32},{32,0},{1,33},{33,1},{2,34},{34,2},{3,35},{35,3},{4,36},{36... | collective-permute-start | bytes 4718600 | tf_op jit(solution)/shard_map/ppermute | solution.py:21
  70.5 1.5 %tile_products.3 = bf16[1024,256]{1,0:T(8,128)(2,1)S(1)} custom-call(s32[1]{0:T(128)S(6)} %copy.28.count, s32[24]{0:T(128)S(1)} %copy-done.1, s32[24]{0:T(128)S(1)} %copy-done.2, bf16[24,256,256]{2,1,0:T(8,128)(2,1)S(1)} %copy-done, bf16[8192,256]{1,0:T(8,128)(2,1)S(1)} %constant_dynamic-update-slice_fusion.12.panels), custom_call_target="tpu_custom_call" | custom-call | flops 134217728 | bytes 1048576 | tf_op jit(solution)/shard_map/tile_products/pallas_call | solution.py:100
  71.9 2.2 %collective-permute-start.10 = (bf16[1024,256]{1,0:T(8,128)(2,1)S(1)}, bf16[1024,256]{1,0:T(8,128)(2,1)S(1)}, u32[]{:S(2)}, u32[]{:S(2)}) collective-permute-start(bf16[1024,256]{1,0:T(8,128)(2,1)S(1)} %tile_products.3), channel_id=1, source_target_pairs={{0,1},{1,2},{2,3},{3,4},{4,5},{5,6},{6,7},{7,0},{32,39},{33,32},{3... | collective-permute-start | bytes 1572872 | tf_op jit(solution)/shard_map/ppermute | solution.py:36
  74.2 0.0 collective-permute-done.14
  74.2 3.1 %collective-permute-start.15 = (bf16[1024,256]{1,0:T(8,128)(2,1)S(1)}, bf16[1024,256]{1,0:T(8,128)(2,1)S(1)}, u32[]{:S(2)}, u32[]{:S(2)}) collective-permute-start(bf16[1024,256]{1,0:T(8,128)(2,1)S(1)} %slice.24), channel_id=1, source_target_pairs={{0,1},{1,2},{2,3},{3,4},{4,5},{5,6},{6,7},{7,0},{32,39},{33,32},{3... | collective-permute-start | bytes 1572872 | tf_op jit(solution)/shard_map/ppermute | solution.py:36
  77.3 6.0 %collective-permute-done.10 = bf16[1024,256]{1,0:T(8,128)(2,1)S(1)} collective-permute-done((bf16[1024,256]{1,0:T(8,128)(2,1)S(1)}, bf16[1024,256]{1,0:T(8,128)(2,1)S(1)}, u32[]{:S(2)}, u32[]{:S(2)}) %collective-permute-start.10) | collective-permute-done | bytes 524320 | tf_op jit(solution)/shard_map/ppermute | solution.py:36
  83.3 0.2 add_convert_fusion.5
  83.4 3.2 %collective-permute-start.11 = (bf16[1024,256]{1,0:T(8,128)(2,1)S(1)}, bf16[1024,256]{1,0:T(8,128)(2,1)S(1)}, u32[]{:S(2)}, u32[]{:S(2)}) collective-permute-start(bf16[1024,256]{1,0:T(8,128)(2,1)S(1)} %add_convert_fusion.5), channel_id=1, source_target_pairs={{0,1},{1,2},{2,3},{3,4},{4,5},{5,6},{6,7},{7,0},{32,39},{33,32},{3... | collective-permute-start | bytes 1572872 | tf_op jit(solution)/shard_map/ppermute | solution.py:36
  86.6 2.3 %collective-permute-done.15 = bf16[1024,256]{1,0:T(8,128)(2,1)S(1)} collective-permute-done((bf16[1024,256]{1,0:T(8,128)(2,1)S(1)}, bf16[1024,256]{1,0:T(8,128)(2,1)S(1)}, u32[]{:S(2)}, u32[]{:S(2)}) %collective-permute-start.15) | collective-permute-done | bytes 524320 | tf_op jit(solution)/shard_map/ppermute | solution.py:36
  88.9 0.2 add_convert_fusion.2
  89.0 3.2 %collective-permute-start.16 = (bf16[1024,256]{1,0:T(8,128)(2,1)S(1)}, bf16[1024,256]{1,0:T(8,128)(2,1)S(1)}, u32[]{:S(2)}, u32[]{:S(2)}) collective-permute-start(bf16[1024,256]{1,0:T(8,128)(2,1)S(1)} %add_convert_fusion.2), channel_id=1, source_target_pairs={{0,1},{1,2},{2,3},{3,4},{4,5},{5,6},{6,7},{7,0},{32,39},{33,32},{3... | collective-permute-start | bytes 1572872 | tf_op jit(solution)/shard_map/ppermute | solution.py:36
  92.2 2.3 %collective-permute-done.11 = bf16[1024,256]{1,0:T(8,128)(2,1)S(1)} collective-permute-done((bf16[1024,256]{1,0:T(8,128)(2,1)S(1)}, bf16[1024,256]{1,0:T(8,128)(2,1)S(1)}, u32[]{:S(2)}, u32[]{:S(2)}) %collective-permute-start.11) | collective-permute-done | bytes 524320 | tf_op jit(solution)/shard_map/ppermute | solution.py:36
  94.5 0.0 copy-start.5
  94.5 0.0 copy-start.3
  94.5 0.0 copy-start.4
  94.5 0.1 add_convert_fusion.4
  94.6 4.4 %collective-permute-start.12 = (bf16[1024,256]{1,0:T(8,128)(2,1)S(1)}, bf16[1024,256]{1,0:T(8,128)(2,1)S(1)}, u32[]{:S(2)}, u32[]{:S(2)}) collective-permute-start(bf16[1024,256]{1,0:T(8,128)(2,1)S(1)} %add_convert_fusion.4), channel_id=1, source_target_pairs={{0,1},{1,2},{2,3},{3,4},{4,5},{5,6},{6,7},{7,0},{32,39},{33,32},{3... | collective-permute-start | bytes 1572872 | tf_op jit(solution)/shard_map/ppermute | solution.py:36
  99.0 1.1 collective-permute-done.16
  100.1 0.2 add_convert_fusion.1
  100.3 4.4 %collective-permute-start.17 = (bf16[1024,256]{1,0:T(8,128)(2,1)S(1)}, bf16[1024,256]{1,0:T(8,128)(2,1)S(1)}, u32[]{:S(2)}, u32[]{:S(2)}) collective-permute-start(bf16[1024,256]{1,0:T(8,128)(2,1)S(1)} %add_convert_fusion.1), channel_id=1, source_target_pairs={{0,1},{1,2},{2,3},{3,4},{4,5},{5,6},{6,7},{7,0},{32,39},{33,32},{3... | collective-permute-start | bytes 1572872 | tf_op jit(solution)/shard_map/ppermute | solution.py:36
  104.7 1.1 collective-permute-done.12
  105.7 0.1 add_convert_fusion.3
  105.9 5.6 %collective-permute-start.13 = (bf16[1024,256]{1,0:T(8,128)(2,1)S(1)}, bf16[1024,256]{1,0:T(8,128)(2,1)S(1)}, u32[]{:S(2)}, u32[]{:S(2)}) collective-permute-start(bf16[1024,256]{1,0:T(8,128)(2,1)S(1)} %add_convert_fusion.3), channel_id=1, source_target_pairs={{0,1},{1,2},{2,3},{3,4},{4,5},{5,6},{6,7},{7,0},{32,39},{33,32},{3... | collective-permute-start | bytes 1572872 | tf_op jit(solution)/shard_map/ppermute | solution.py:36
  111.5 0.0 collective-permute-done.17
  111.5 1.9 %collective-permute-start.18 = (bf16[1024,256]{1,0:T(8,128)(2,1)S(1)}, bf16[1024,256]{1,0:T(8,128)(2,1)S(1)}, u32[]{:S(2)}, u32[]{:S(2)}) collective-permute-start(bf16[1024,256]{1,0:T(8,128)(2,1)S(1)} %collective-permute-done.17), channel_id=1, source_target_pairs={{0,32},{32,0},{1,33},{33,1},{2,34},{34,2},{3,35},{35,3},{4,36},{36... | collective-permute-start | bytes 1572872 | tf_op jit(solution)/shard_map/ppermute | solution.py:21
  113.4 0.0 copy-done.5
  113.4 0.0 copy-done.3
  113.4 0.0 copy-done.4
  113.4 0.1 multiply_add_fusion
  113.6 4.6 %collective-permute-done.13 = bf16[1024,256]{1,0:T(8,128)(2,1)S(1)} collective-permute-done((bf16[1024,256]{1,0:T(8,128)(2,1)S(1)}, bf16[1024,256]{1,0:T(8,128)(2,1)S(1)}, u32[]{:S(2)}, u32[]{:S(2)}) %collective-permute-start.13) | collective-permute-done | bytes 524320 | tf_op jit(solution)/shard_map/ppermute | solution.py:36
  118.1 0.0 collective-permute-done.18
  118.1 0.2 add_convert_fusion
  118.4 23.4 %all_to_all.9 = bf16[4,256,256]{2,1,0:T(8,128)(2,1)S(1)} all-to-all(bf16[4,256,256]{2,1,0:T(8,128)(2,1)S(1)} %bitcast.1), channel_id=1, replica_groups=mesh['ylo'=2,'z'=8,'core'=2,'yhi'=4,'x'=8] {'yhi'}, dimensions={0} | all-to-all | bytes 1048576 | tf_op jit(solution)/shard_map/all_to_all | solution.py:177
  141.8 0.1 convert_reduce_fusion
  141.9 0.7 add_convert_fusion.6
  (13 shorter events, 0.3 us)
Async XLA Ops:
  0.0 7.3 %collective-permute-start = (bf16[256,256]{1,0:T(8,128)(2,1)}, bf16[256,256]{1,0:T(8,128)(2,1)S(1)}, u32[]{:S(2)}, u32[]{:S(2)}) collective-permute-start(bf16[256,256]{1,0:T(8,128)(2,1)} %param.7), channel_id=1, source_target_pairs={{0,512},{512,0},{1,513},{513,1},{2,514},{514,2},{3,515},{515,3},{4... | collective-permute-start | bytes 393224 | tf_op jit(solution)/shard_map/ppermute | solution.py:21
  7.4 28.4 %collective-permute-start.3 = (bf16[512,256]{1,0:T(8,128)(2,1)S(1)}, bf16[512,256]{1,0:T(8,128)(2,1)S(1)}, u32[]{:S(2)}, u32[]{:S(2)}) collective-permute-start(bf16[512,256]{1,0:T(8,128)(2,1)S(1)} %get-tuple-element.37), channel_id=1, source_target_pairs={{0,128},{64,192},{128,256},{192,320},{256,384},{320,448},{384,0},{... | collective-permute-start | bytes 786440 | tf_op jit(solution)/shard_map/ppermute | solution.py:21
  15.3 22.5 %collective-permute-start.4 = (bf16[512,256]{1,0:T(8,128)(2,1)S(1)}, bf16[512,256]{1,0:T(8,128)(2,1)S(1)}, u32[]{:S(2)}, u32[]{:S(2)}) collective-permute-start(bf16[512,256]{1,0:T(8,128)(2,1)S(1)} %get-tuple-element.37), channel_id=1, source_target_pairs={{0,384},{64,448},{128,0},{192,64},{256,128},{320,192},{384,256},{4... | collective-permute-start | bytes 786440 | tf_op jit(solution)/shard_map/ppermute | solution.py:21
  25.7 20.7 %collective-permute-start.1 = (bf16[512,256]{1,0:T(8,128)(2,1)S(1)}, bf16[512,256]{1,0:T(8,128)(2,1)S(1)}, u32[]{:S(2)}, u32[]{:S(2)}) collective-permute-start(bf16[512,256]{1,0:T(8,128)(2,1)S(1)} %get-tuple-element.37), channel_id=1, source_target_pairs={{0,64},{64,128},{128,192},{192,256},{256,320},{320,384},{384,448},... | collective-permute-start | bytes 786440 | tf_op jit(solution)/shard_map/ppermute | solution.py:21
  30.0 20.9 %collective-permute-start.2 = (bf16[512,256]{1,0:T(8,128)(2,1)S(1)}, bf16[512,256]{1,0:T(8,128)(2,1)S(1)}, u32[]{:S(2)}, u32[]{:S(2)}) collective-permute-start(bf16[512,256]{1,0:T(8,128)(2,1)S(1)} %get-tuple-element.37), channel_id=1, source_target_pairs={{0,448},{64,0},{128,64},{192,128},{256,192},{320,256},{384,320},{4... | collective-permute-start | bytes 786440 | tf_op jit(solution)/shard_map/ppermute | solution.py:21
  35.8 19.0 %collective-permute-start.7 = (bf16[256,256]{1,0:T(8,128)(2,1)S(1)}, bf16[256,256]{1,0:T(8,128)(2,1)S(1)}, u32[]{:S(2)}, u32[]{:S(2)}) collective-permute-start(bf16[256,256]{1,0:T(8,128)(2,1)S(1)} %slice.20), channel_id=1, source_target_pairs={{0,128},{64,192},{128,256},{192,320},{256,384},{320,448},{384,0},{... | collective-permute-start | bytes 393224 | tf_op jit(solution)/shard_map/ppermute | solution.py:21
  37.8 17.1 %collective-permute-start.8 = (bf16[256,256]{1,0:T(8,128)(2,1)S(1)}, bf16[256,256]{1,0:T(8,128)(2,1)S(1)}, u32[]{:S(2)}, u32[]{:S(2)}) collective-permute-start(bf16[256,256]{1,0:T(8,128)(2,1)S(1)} %slice.21), channel_id=1, source_target_pairs={{0,384},{64,448},{128,0},{192,64},{256,128},{320,192},{384,256},{4... | collective-permute-start | bytes 393224 | tf_op jit(solution)/shard_map/ppermute | solution.py:21
  43.8 9.5 %collective-permute-start.5 = (bf16[512,256]{1,0:T(8,128)(2,1)S(1)}, bf16[512,256]{1,0:T(8,128)(2,1)S(1)}, u32[]{:S(2)}, u32[]{:S(2)}) collective-permute-start(bf16[512,256]{1,0:T(8,128)(2,1)S(1)} %collective-permute-done.3), channel_id=1, source_target_pairs={{0,64},{64,128},{128,192},{192,256},{256,320},{320,384},{384,448},... | collective-permute-start | bytes 786440 | tf_op jit(solution)/shard_map/ppermute | solution.py:21
  46.4 8.3 %collective-permute-start.6 = (bf16[512,256]{1,0:T(8,128)(2,1)S(1)}, bf16[512,256]{1,0:T(8,128)(2,1)S(1)}, u32[]{:S(2)}, u32[]{:S(2)}) collective-permute-start(bf16[512,256]{1,0:T(8,128)(2,1)S(1)} %collective-permute-done.4), channel_id=1, source_target_pairs={{0,448},{64,0},{128,64},{192,128},{256,192},{320,256},{384,320},{4... | collective-permute-start | bytes 786440 | tf_op jit(solution)/shard_map/ppermute | solution.py:21
  54.9 6.1 %collective-permute-start.9 = (bf16[4096,256]{1,0:T(8,128)(2,1)S(1)}, bf16[4096,256]{1,0:T(8,128)(2,1)S(1)}, u32[]{:S(2)}, u32[]{:S(2)}) collective-permute-start(bf16[4096,256]{1,0:T(8,128)(2,1)S(1)} %get-tuple-element.31), channel_id=1, source_target_pairs={{0,32},{32,0},{1,33},{33,1},{2,34},{34,2},{3,35},{35,3},{4,36},{36... | collective-permute-start | bytes 6291464 | tf_op jit(solution)/shard_map/ppermute | solution.py:21
  60.9 1.9 %copy-start = (bf16[24,256,256]{2,1,0:T(8,128)(2,1)S(1)}, bf16[24,256,256]{2,1,0:T(8,128)(2,1)}, u32[]{:S(2)}) copy-start(bf16[24,256,256]{2,1,0:T(8,128)(2,1)} %tiles.3) | copy-start | bytes 9437188
  60.9 1.9 %copy-start.1 = (s32[24]{0:T(128)S(1)}, s32[24]{0:T(128)}, u32[]{:S(2)}) copy-start(s32[24]{0:T(128)} %rows.3) | copy-start | bytes 292
  60.9 1.9 %copy-start.2 = (s32[24]{0:T(128)S(1)}, s32[24]{0:T(128)}, u32[]{:S(2)}) copy-start(s32[24]{0:T(128)} %srcs.3) | copy-start | bytes 292
  68.2 6.0 %collective-permute-start.14 = (bf16[3072,256]{1,0:T(8,128)(2,1)S(1)}, bf16[3072,256]{1,0:T(8,128)(2,1)S(1)}, u32[]{:S(2)}, u32[]{:S(2)}) collective-permute-start(bf16[3072,256]{1,0:T(8,128)(2,1)S(1)} %get-tuple-element.16), channel_id=1, source_target_pairs={{0,32},{32,0},{1,33},{33,1},{2,34},{34,2},{3,35},{35,3},{4,36},{36... | collective-permute-start | bytes 4718600 | tf_op jit(solution)/shard_map/ppermute | solution.py:21
  71.9 11.3 %collective-permute-start.10 = (bf16[1024,256]{1,0:T(8,128)(2,1)S(1)}, bf16[1024,256]{1,0:T(8,128)(2,1)S(1)}, u32[]{:S(2)}, u32[]{:S(2)}) collective-permute-start(bf16[1024,256]{1,0:T(8,128)(2,1)S(1)} %tile_products.3), channel_id=1, source_target_pairs={{0,1},{1,2},{2,3},{3,4},{4,5},{5,6},{6,7},{7,0},{32,39},{33,32},{3... | collective-permute-start | bytes 1572872 | tf_op jit(solution)/shard_map/ppermute | solution.py:36
  74.2 14.7 %collective-permute-start.15 = (bf16[1024,256]{1,0:T(8,128)(2,1)S(1)}, bf16[1024,256]{1,0:T(8,128)(2,1)S(1)}, u32[]{:S(2)}, u32[]{:S(2)}) collective-permute-start(bf16[1024,256]{1,0:T(8,128)(2,1)S(1)} %slice.24), channel_id=1, source_target_pairs={{0,1},{1,2},{2,3},{3,4},{4,5},{5,6},{6,7},{7,0},{32,39},{33,32},{3... | collective-permute-start | bytes 1572872 | tf_op jit(solution)/shard_map/ppermute | solution.py:36
  83.4 11.1 %collective-permute-start.11 = (bf16[1024,256]{1,0:T(8,128)(2,1)S(1)}, bf16[1024,256]{1,0:T(8,128)(2,1)S(1)}, u32[]{:S(2)}, u32[]{:S(2)}) collective-permute-start(bf16[1024,256]{1,0:T(8,128)(2,1)S(1)} %add_convert_fusion.5), channel_id=1, source_target_pairs={{0,1},{1,2},{2,3},{3,4},{4,5},{5,6},{6,7},{7,0},{32,39},{33,32},{3... | collective-permute-start | bytes 1572872 | tf_op jit(solution)/shard_map/ppermute | solution.py:36
  89.0 11.1 %collective-permute-start.16 = (bf16[1024,256]{1,0:T(8,128)(2,1)S(1)}, bf16[1024,256]{1,0:T(8,128)(2,1)S(1)}, u32[]{:S(2)}, u32[]{:S(2)}) collective-permute-start(bf16[1024,256]{1,0:T(8,128)(2,1)S(1)} %add_convert_fusion.2), channel_id=1, source_target_pairs={{0,1},{1,2},{2,3},{3,4},{4,5},{5,6},{6,7},{7,0},{32,39},{33,32},{3... | collective-permute-start | bytes 1572872 | tf_op jit(solution)/shard_map/ppermute | solution.py:36
  94.5 18.9 %copy-start.5 = (s32[256]{0:T(256)S(1)}, s32[256]{0:T(256)}, u32[]{:S(2)}) copy-start(s32[256]{0:T(256)} %param.13) | copy-start | bytes 3076
  94.5 18.9 %copy-start.3 = (bf16[256,256]{1,0:T(8,128)(2,1)S(1)}, bf16[256,256]{1,0:T(8,128)(2,1)}, u32[]{:S(2)}) copy-start(bf16[256,256]{1,0:T(8,128)(2,1)} %param.7) | copy-start | bytes 393220
  94.5 18.9 %copy-start.4 = (bf16[256,256]{1,0:T(8,128)(2,1)S(1)}, bf16[256,256]{1,0:T(8,128)(2,1)}, u32[]{:S(2)}) copy-start(bf16[256,256]{1,0:T(8,128)(2,1)} %param.8) | copy-start | bytes 393220
  94.6 11.1 %collective-permute-start.12 = (bf16[1024,256]{1,0:T(8,128)(2,1)S(1)}, bf16[1024,256]{1,0:T(8,128)(2,1)S(1)}, u32[]{:S(2)}, u32[]{:S(2)}) collective-permute-start(bf16[1024,256]{1,0:T(8,128)(2,1)S(1)} %add_convert_fusion.4), channel_id=1, source_target_pairs={{0,1},{1,2},{2,3},{3,4},{4,5},{5,6},{6,7},{7,0},{32,39},{33,32},{3... | collective-permute-start | bytes 1572872 | tf_op jit(solution)/shard_map/ppermute | solution.py:36
  100.3 11.2 %collective-permute-start.17 = (bf16[1024,256]{1,0:T(8,128)(2,1)S(1)}, bf16[1024,256]{1,0:T(8,128)(2,1)S(1)}, u32[]{:S(2)}, u32[]{:S(2)}) collective-permute-start(bf16[1024,256]{1,0:T(8,128)(2,1)S(1)} %add_convert_fusion.1), channel_id=1, source_target_pairs={{0,1},{1,2},{2,3},{3,4},{4,5},{5,6},{6,7},{7,0},{32,39},{33,32},{3... | collective-permute-start | bytes 1572872 | tf_op jit(solution)/shard_map/ppermute | solution.py:36
  105.9 12.3 %collective-permute-start.13 = (bf16[1024,256]{1,0:T(8,128)(2,1)S(1)}, bf16[1024,256]{1,0:T(8,128)(2,1)S(1)}, u32[]{:S(2)}, u32[]{:S(2)}) collective-permute-start(bf16[1024,256]{1,0:T(8,128)(2,1)S(1)} %add_convert_fusion.3), channel_id=1, source_target_pairs={{0,1},{1,2},{2,3},{3,4},{4,5},{5,6},{6,7},{7,0},{32,39},{33,32},{3... | collective-permute-start | bytes 1572872 | tf_op jit(solution)/shard_map/ppermute | solution.py:36
  111.5 6.7 %collective-permute-start.18 = (bf16[1024,256]{1,0:T(8,128)(2,1)S(1)}, bf16[1024,256]{1,0:T(8,128)(2,1)S(1)}, u32[]{:S(2)}, u32[]{:S(2)}) collective-permute-start(bf16[1024,256]{1,0:T(8,128)(2,1)S(1)} %collective-permute-done.17), channel_id=1, source_target_pairs={{0,32},{32,0},{1,33},{33,1},{2,34},{34,2},{3,35},{35,3},{4,36},{36... | collective-permute-start | bytes 1572872 | tf_op jit(solution)/shard_map/ppermute | solution.py:21

commit v8 on v7

--- a/solution.py
+++ b/solution.py
@@ -36,7 +36,7 @@
     return lax.ppermute(value, names, pairs)
 
 
-def tiles_kernel(chunks, count, rows, srcs, tiles, panels, *refs):
+def tiles_kernel(chunks, count, rows, srcs, tiles, near, across, *refs):
     outs, (head, following, acc) = refs[: len(chunks)], refs[len(chunks) :]
     side = tiles.shape[1]
     my_ylo, my_z, my_core = lax.axis_index("ylo"), lax.axis_index("z"), lax.axis_index("core")
@@ -56,13 +56,18 @@
 
     lax.fori_loop(0, count[0], link, 0)
 
-    def product(s):
-        place = panel_place(srcs[s], my_ylo, my_z, my_core)
+    def add_product(s):
+        same_core, place = panel_place(srcs[s], my_ylo, my_z, my_core)
         panel = pl.ds(pl.multiple_of(place * side, side), side)
-        return jnp.dot(tiles[s], panels[panel, :], preferred_element_type=jnp.float32)
 
-    def add_product(s):
-        acc[...] += product(s)
+        @pl.when(same_core)
+        def _():
+            acc[...] += jnp.dot(tiles[s], near[panel, :], preferred_element_type=jnp.float32)
+
+        @pl.when(jnp.logical_not(same_core))
+        def _():
+            acc[...] += jnp.dot(tiles[s], across[panel, :], preferred_element_type=jnp.float32)
+
         return following[s]
 
     def chunk(out, base, k):
@@ -78,8 +83,8 @@
 
             @pl.when(first >= 0)
             def _():
-                acc[...] = product(first)
-                lax.while_loop(lambda s: s >= 0, add_product, following[first])
+                acc[...] = jnp.zeros_like(acc)
+                lax.while_loop(lambda s: s >= 0, add_product, first)
                 out[where, :] = acc[...].astype(out.dtype)
 
             return carry
@@ -91,9 +96,9 @@
             chunk(out, i * N_YHI, k)
 
 
-def partial_products(chunks, tile_blocks, tile_rows, tile_srcs, tile_count, panels):
+def partial_products(chunks, tile_blocks, tile_rows, tile_srcs, tile_count, near, across):
     slots, side = tile_blocks.shape[:2]
-    columns = panels.shape[1]
+    columns = near.shape[1]
     smem = pl.BlockSpec(memory_space=pltpu.SMEM)
     vmem = pl.BlockSpec(memory_space=pltpu.VMEM)
     row_tiles = N_YHI * sum(len(ks) for ks in chunks)
@@ -102,7 +107,7 @@
         out_shape=[
             jax.ShapeDtypeStruct((len(ks) * N_YHI * side, columns), jnp.bfloat16) for ks in chunks
         ],
-        in_specs=[smem, smem, smem, vmem, vmem],
+        in_specs=[smem, smem, smem, vmem, vmem, vmem],
         out_specs=[vmem] * len(chunks),
         scratch_shapes=[
             pltpu.SMEM((ROW_TILES,), jnp.int32),
@@ -116,7 +121,7 @@
             bytes_accessed=4 * row_tiles * side * columns,
         ),
         name="tile_products",
-    )(tile_count, tile_rows, tile_srcs, tile_blocks, panels)
+    )(tile_count, tile_rows, tile_srcs, tile_blocks, near, across)
 
 
 def gather_panels(flow_cols):
@@ -129,7 +134,7 @@
     near = jnp.concatenate(
         [own, below1, above1, below2, above2, below3, above3, below4, above4], 0
     )
-    return jnp.concatenate([near, shifted(near, "core", 1)], 0)
+    return near, shifted(near, "core", 1)
 
 
 def panel_place(src, my_ylo, my_z, my_core):
@@ -137,7 +142,7 @@
     off_z = (src // N_CORE % N_Z + N_Z - my_z) % N_Z
     off_core = (src % N_CORE + N_CORE - my_core) % N_CORE
     slot = jnp.where(off_z >= N_Z // 2, (N_Z - off_z) * 2 - 1, 2 * off_z)
-    return (off_core * N_Z + slot) * N_YLO + off_ylo
+    return off_core == 0, slot * N_YLO + off_ylo
 
 
 def add(*terms):
@@ -165,10 +170,12 @@
 
 def body(flow_cols, restart, tile_blocks, tile_rows, tile_srcs, tile_count, dangling):
     side, columns = flow_cols.shape
-    panels = gather_panels(flow_cols)
+    near, across = gather_panels(flow_cols)
 
     def products(chunks):
-        return partial_products(chunks, tile_blocks, tile_rows, tile_srcs, tile_count, panels)
+        return partial_products(
+            chunks, tile_blocks, tile_rows, tile_srcs, tile_count, near, across
+        )
 
     own_flow = flow_cols.astype(jnp.float32)
     mask_col = dangling.astype(jnp.float32)[:, None]

time: 145 us -> 143 us (0.986)
  starting transfers between devices: 76.7 us -> 82.8 us
  waiting for transfers between devices: 29.6 us -> 25.7 us
  local copies, waits for them, and re-layouts: 3.18 us -> 1.17 us
    ppermute x7, starting transfers between devices: 26 us -> 30.9 us  [sent_outward(): return lax.ppermute(value, names, pairs)]
    ppermute x7, waiting for transfers between devices: 17.3 us -> 13.3 us  [sent_outward(): return lax.ppermute(value, names, pairs)]
    unnamed x21 -> x20, local copies, waits for them, and re-layouts: 2.97 us -> 1.09 us
  transfers between devices with their start and end apart: 19 -> 19, of which waited for: 11 -> 10; matrix products, arithmetic and copies ran while one was open for 1% -> 1% of each run, Pallas kernels for 1% -> 1%
where the time goes in v8:
time: 143 us; the launch traced here: 141 us
  starting transfers between devices  82.8 us (58%)
  waiting for transfers between devices  25.7 us (18%)
  blocking collectives  22.1 us (15%)
  Pallas kernels  6.81 us (5%)
  other arithmetic  1.77 us (1%)
    ppermute x12, starting transfers between devices, shifted(): lax.ppermute(value, axis, [(i, (i + by) % size) for i in range(size)])  51.9 us
    ppermute x7, starting transfers between devices, sent_outward(): return lax.ppermute(value, names, pairs)  30.9 us
    all_to_all x1, blocking collectives, body(): lax.all_to_all(along_x, 'yhi', 0, 0, tiled=True)  22.1 us
    ppermute x7, waiting for transfers between devices, sent_outward(): return lax.ppermute(value, names, pairs)  13.3 us
    ppermute x12, waiting for transfers between devices, shifted(): lax.ppermute(value, axis, [(i, (i + by) % size) for i in range(size)])  12.4 us
    pallas_call x2, Pallas kernels, partial_products(): pl.pallas_call(functools.partial(tiles_kernel, chunks), out_shape=[jax.Sh...  6.81 us
  transfers between devices with their start and end apart: 19, of which 10 were waited for; matrix products, arithmetic and copies ran while one was open for 1% of the time, Pallas kernels for 1%

profile of v8, /device:TPU:14, one launch (start us, length us, event | category | flops | bytes accessed | tf_op | source)
XLA Modules:
  0.0 141.4 jit_solution(10704191295180896404)
XLA Ops:
  0.0 3.6 %collective-permute-start = (bf16[256,256]{1,0:T(8,128)(2,1)}, bf16[256,256]{1,0:T(8,128)(2,1)S(1)}, u32[]{:S(2)}, u32[]{:S(2)}) collective-permute-start(bf16[256,256]{1,0:T(8,128)(2,1)} %param.7), channel_id=1, source_target_pairs={{0,512},{512,0},{1,513},{513,1},{2,514},{514,2},{3,515},{515,3},{4... | collective-permute-start | bytes 393224 | tf_op jit(solution)/shard_map/ppermute | solution.py:21
  3.6 0.9 constant_dynamic-update-slice_fusion.1
  4.5 2.8 %collective-permute-done = bf16[256,256]{1,0:T(8,128)(2,1)S(1)} collective-permute-done((bf16[256,256]{1,0:T(8,128)(2,1)}, bf16[256,256]{1,0:T(8,128)(2,1)S(1)}, u32[]{:S(2)}, u32[]{:S(2)}) %collective-permute-start) | collective-permute-done | bytes 131104 | tf_op jit(solution)/shard_map/ppermute | solution.py:21
  7.4 0.0 copy-start
  7.4 0.0 copy-start.1
  7.4 0.0 copy-start.2
  7.4 8.2 %collective-permute-start.3 = (bf16[512,256]{1,0:T(8,128)(2,1)S(1)}, bf16[512,256]{1,0:T(8,128)(2,1)S(1)}, u32[]{:S(2)}, u32[]{:S(2)}) collective-permute-start(bf16[512,256]{1,0:T(8,128)(2,1)S(1)} %get-tuple-element.19), channel_id=1, source_target_pairs={{0,128},{64,192},{128,256},{192,320},{256,384},{320,448},{384,0},{... | collective-permute-start | bytes 786440 | tf_op jit(solution)/shard_map/ppermute | solution.py:21
  15.6 10.4 %collective-permute-start.4 = (bf16[512,256]{1,0:T(8,128)(2,1)S(1)}, bf16[512,256]{1,0:T(8,128)(2,1)S(1)}, u32[]{:S(2)}, u32[]{:S(2)}) collective-permute-start(bf16[512,256]{1,0:T(8,128)(2,1)S(1)} %get-tuple-element.19), channel_id=1, source_target_pairs={{0,384},{64,448},{128,0},{192,64},{256,128},{320,192},{384,256},{4... | collective-permute-start | bytes 786440 | tf_op jit(solution)/shard_map/ppermute | solution.py:21
  26.0 4.3 %collective-permute-start.1 = (bf16[512,256]{1,0:T(8,128)(2,1)S(1)}, bf16[512,256]{1,0:T(8,128)(2,1)S(1)}, u32[]{:S(2)}, u32[]{:S(2)}) collective-permute-start(bf16[512,256]{1,0:T(8,128)(2,1)S(1)} %get-tuple-element.19), channel_id=1, source_target_pairs={{0,64},{64,128},{128,192},{192,256},{256,320},{320,384},{384,448},... | collective-permute-start | bytes 786440 | tf_op jit(solution)/shard_map/ppermute | solution.py:21
  30.3 3.4 %collective-permute-start.2 = (bf16[512,256]{1,0:T(8,128)(2,1)S(1)}, bf16[512,256]{1,0:T(8,128)(2,1)S(1)}, u32[]{:S(2)}, u32[]{:S(2)}) collective-permute-start(bf16[512,256]{1,0:T(8,128)(2,1)S(1)} %get-tuple-element.19), channel_id=1, source_target_pairs={{0,448},{64,0},{128,64},{192,128},{256,192},{320,256},{384,320},{4... | collective-permute-start | bytes 786440 | tf_op jit(solution)/shard_map/ppermute | solution.py:21
  33.7 2.4 %collective-permute-done.3 = bf16[512,256]{1,0:T(8,128)(2,1)S(1)} collective-permute-done((bf16[512,256]{1,0:T(8,128)(2,1)S(1)}, bf16[512,256]{1,0:T(8,128)(2,1)S(1)}, u32[]{:S(2)}, u32[]{:S(2)}) %collective-permute-start.3) | collective-permute-done | bytes 262176 | tf_op jit(solution)/shard_map/ppermute | solution.py:21
  36.1 1.9 %collective-permute-start.7 = (bf16[256,256]{1,0:T(8,128)(2,1)S(1)}, bf16[256,256]{1,0:T(8,128)(2,1)S(1)}, u32[]{:S(2)}, u32[]{:S(2)}) collective-permute-start(bf16[256,256]{1,0:T(8,128)(2,1)S(1)} %slice.20), channel_id=1, source_target_pairs={{0,128},{64,192},{128,256},{192,320},{256,384},{320,448},{384,0},{... | collective-permute-start | bytes 393224 | tf_op jit(solution)/shard_map/ppermute | solution.py:21
  38.0 0.0 collective-permute-done.4
  38.0 6.0 %collective-permute-start.8 = (bf16[256,256]{1,0:T(8,128)(2,1)S(1)}, bf16[256,256]{1,0:T(8,128)(2,1)S(1)}, u32[]{:S(2)}, u32[]{:S(2)}) collective-permute-start(bf16[256,256]{1,0:T(8,128)(2,1)S(1)} %slice.21), channel_id=1, source_target_pairs={{0,384},{64,448},{128,0},{192,64},{256,128},{320,192},{384,256},{4... | collective-permute-start | bytes 393224 | tf_op jit(solution)/shard_map/ppermute | solution.py:21
  44.1 2.6 %collective-permute-start.5 = (bf16[512,256]{1,0:T(8,128)(2,1)S(1)}, bf16[512,256]{1,0:T(8,128)(2,1)S(1)}, u32[]{:S(2)}, u32[]{:S(2)}) collective-permute-start(bf16[512,256]{1,0:T(8,128)(2,1)S(1)} %collective-permute-done.3), channel_id=1, source_target_pairs={{0,64},{64,128},{128,192},{192,256},{256,320},{320,384},{384,448},... | collective-permute-start | bytes 786440 | tf_op jit(solution)/shard_map/ppermute | solution.py:21
  46.7 0.0 collective-permute-done.1
  46.7 4.4 %collective-permute-start.6 = (bf16[512,256]{1,0:T(8,128)(2,1)S(1)}, bf16[512,256]{1,0:T(8,128)(2,1)S(1)}, u32[]{:S(2)}, u32[]{:S(2)}) collective-permute-start(bf16[512,256]{1,0:T(8,128)(2,1)S(1)} %collective-permute-done.4), channel_id=1, source_target_pairs={{0,448},{64,0},{128,64},{192,128},{256,192},{320,256},{384,320},{4... | collective-permute-start | bytes 786440 | tf_op jit(solution)/shard_map/ppermute | solution.py:21
  51.2 0.0 collective-permute-done.2
  51.3 2.3 %collective-permute-done.5 = bf16[512,256]{1,0:T(8,128)(2,1)S(1)} collective-permute-done((bf16[512,256]{1,0:T(8,128)(2,1)S(1)}, bf16[512,256]{1,0:T(8,128)(2,1)S(1)}, u32[]{:S(2)}, u32[]{:S(2)}) %collective-permute-start.5) | collective-permute-done | bytes 262176 | tf_op jit(solution)/shard_map/ppermute | solution.py:21
  53.6 1.4 %collective-permute-done.6 = bf16[512,256]{1,0:T(8,128)(2,1)S(1)} collective-permute-done((bf16[512,256]{1,0:T(8,128)(2,1)S(1)}, bf16[512,256]{1,0:T(8,128)(2,1)S(1)}, u32[]{:S(2)}, u32[]{:S(2)}) %collective-permute-start.6) | collective-permute-done | bytes 262176 | tf_op jit(solution)/shard_map/ppermute | solution.py:21
  55.1 0.0 collective-permute-done.7
  55.1 0.0 collective-permute-done.8
  55.1 1.9 %collective-permute-start.9 = (bf16[4096,256]{1,0:T(8,128)(2,1)S(1)}, bf16[4096,256]{1,0:T(8,128)(2,1)S(1)}, u32[]{:S(2)}, u32[]{:S(2)}) collective-permute-start(bf16[4096,256]{1,0:T(8,128)(2,1)S(1)} %constant_dynamic-update-slice_fusion.2.near), channel_id=1, source_target_pairs={{0,32},{32,0},{1,33},{33,1},{2,34},{34,2},{3,35},{35,3},{4,36},{36... | collective-permute-start | bytes 6291464 | tf_op jit(solution)/shard_map/ppermute | solution.py:21
  57.7 3.5 %collective-permute-done.9.across = bf16[4096,256]{1,0:T(8,128)(2,1)S(1)} collective-permute-done((bf16[4096,256]{1,0:T(8,128)(2,1)S(1)}, bf16[4096,256]{1,0:T(8,128)(2,1)S(1)}, u32[]{:S(2)}, u32[]{:S(2)}) %collective-permute-start.9) | collective-permute-done | bytes 2097184 | tf_op jit(solution)/shard_map/ppermute | solution.py:21
  61.2 0.0 copy-done
  61.2 0.0 copy-done.1
  61.2 0.0 copy-done.2
  61.2 5.1 %tile_products.2 = (bf16[3072,256]{1,0:T(8,128)(2,1)S(1)}, bf16[1024,256]{1,0:T(8,128)(2,1)S(1)}, bf16[1024,256]{1,0:T(8,128)(2,1)S(1)}, bf16[1024,256]{1,0:T(8,128)(2,1)S(1)}, bf16[1024,256]{1,0:T(8,128)(2,1)S(1)}) custom-call(s32[1]{0:T(128)S(6)} %copy.18.count, s32[24]{0:T(128)S(1)} %copy-done.1, s32[24]{0:T(128)S(1)} %copy-done.2, ...), custom_call_target="tpu_custom_call" | custom-call | flops 939524096 | bytes 7340032 | tf_op jit(solution)/shard_map/tile_products/pallas_call | solution.py:105
  66.2 3.2 %collective-permute-start.14 = (bf16[3072,256]{1,0:T(8,128)(2,1)S(1)}, bf16[3072,256]{1,0:T(8,128)(2,1)S(1)}, u32[]{:S(2)}, u32[]{:S(2)}) collective-permute-start(bf16[3072,256]{1,0:T(8,128)(2,1)S(1)} %get-tuple-element.16), channel_id=1, source_target_pairs={{0,32},{32,0},{1,33},{33,1},{2,34},{34,2},{3,35},{35,3},{4,36},{36... | collective-permute-start | bytes 4718600 | tf_op jit(solution)/shard_map/ppermute | solution.py:21
  69.5 1.8 %tile_products.3 = bf16[1024,256]{1,0:T(8,128)(2,1)S(1)} custom-call(s32[1]{0:T(128)S(6)} %copy.18.count, s32[24]{0:T(128)S(1)} %copy-done.1, s32[24]{0:T(128)S(1)} %copy-done.2, bf16[24,256,256]{2,1,0:T(8,128)(2,1)S(1)} %copy-done, bf16[4096,256]{1,0:T(8,128)(2,1)S(1)} %constant_dynamic-update-slice_fusion.2.near, ...), custom_call_target="tpu_custom_call" | custom-call | flops 134217728 | bytes 1048576 | tf_op jit(solution)/shard_map/tile_products/pallas_call | solution.py:105
  71.2 3.1 %collective-permute-start.10 = (bf16[1024,256]{1,0:T(8,128)(2,1)S(1)}, bf16[1024,256]{1,0:T(8,128)(2,1)S(1)}, u32[]{:S(2)}, u32[]{:S(2)}) collective-permute-start(bf16[1024,256]{1,0:T(8,128)(2,1)S(1)} %tile_products.3), channel_id=1, source_target_pairs={{0,1},{1,2},{2,3},{3,4},{4,5},{5,6},{6,7},{7,0},{32,39},{33,32},{3... | collective-permute-start | bytes 1572872 | tf_op jit(solution)/shard_map/ppermute | solution.py:36
  74.3 0.0 collective-permute-done.14
  74.4 2.6 %collective-permute-start.15 = (bf16[1024,256]{1,0:T(8,128)(2,1)S(1)}, bf16[1024,256]{1,0:T(8,128)(2,1)S(1)}, u32[]{:S(2)}, u32[]{:S(2)}) collective-permute-start(bf16[1024,256]{1,0:T(8,128)(2,1)S(1)} %slice.24), channel_id=1, source_target_pairs={{0,1},{1,2},{2,3},{3,4},{4,5},{5,6},{6,7},{7,0},{32,39},{33,32},{3... | collective-permute-start | bytes 1572872 | tf_op jit(solution)/shard_map/ppermute | solution.py:36
  77.0 5.3 %collective-permute-done.10 = bf16[1024,256]{1,0:T(8,128)(2,1)S(1)} collective-permute-done((bf16[1024,256]{1,0:T(8,128)(2,1)S(1)}, bf16[1024,256]{1,0:T(8,128)(2,1)S(1)}, u32[]{:S(2)}, u32[]{:S(2)}) %collective-permute-start.10) | collective-permute-done | bytes 524320 | tf_op jit(solution)/shard_map/ppermute | solution.py:36
  82.3 0.1 add_convert_fusion.5
  82.5 4.3 %collective-permute-start.11 = (bf16[1024,256]{1,0:T(8,128)(2,1)S(1)}, bf16[1024,256]{1,0:T(8,128)(2,1)S(1)}, u32[]{:S(2)}, u32[]{:S(2)}) collective-permute-start(bf16[1024,256]{1,0:T(8,128)(2,1)S(1)} %add_convert_fusion.5), channel_id=1, source_target_pairs={{0,1},{1,2},{2,3},{3,4},{4,5},{5,6},{6,7},{7,0},{32,39},{33,32},{3... | collective-permute-start | bytes 1572872 | tf_op jit(solution)/shard_map/ppermute | solution.py:36
  86.8 1.1 collective-permute-done.15
  87.9 0.1 add_convert_fusion.2
  88.1 4.3 %collective-permute-start.16 = (bf16[1024,256]{1,0:T(8,128)(2,1)S(1)}, bf16[1024,256]{1,0:T(8,128)(2,1)S(1)}, u32[]{:S(2)}, u32[]{:S(2)}) collective-permute-start(bf16[1024,256]{1,0:T(8,128)(2,1)S(1)} %add_convert_fusion.2), channel_id=1, source_target_pairs={{0,1},{1,2},{2,3},{3,4},{4,5},{5,6},{6,7},{7,0},{32,39},{33,32},{3... | collective-permute-start | bytes 1572872 | tf_op jit(solution)/shard_map/ppermute | solution.py:36
  92.4 1.2 collective-permute-done.11
  93.5 0.0 copy-start.5
  93.5 0.0 copy-start.3
  93.5 0.0 copy-start.4
  93.5 0.1 add_convert_fusion.4
  93.7 5.5 %collective-permute-start.12 = (bf16[1024,256]{1,0:T(8,128)(2,1)S(1)}, bf16[1024,256]{1,0:T(8,128)(2,1)S(1)}, u32[]{:S(2)}, u32[]{:S(2)}) collective-permute-start(bf16[1024,256]{1,0:T(8,128)(2,1)S(1)} %add_convert_fusion.4), channel_id=1, source_target_pairs={{0,1},{1,2},{2,3},{3,4},{4,5},{5,6},{6,7},{7,0},{32,39},{33,32},{3... | collective-permute-start | bytes 1572872 | tf_op jit(solution)/shard_map/ppermute | solution.py:36
  99.2 0.0 collective-permute-done.16
  99.2 0.1 add_convert_fusion.1
  99.4 5.4 %collective-permute-start.17 = (bf16[1024,256]{1,0:T(8,128)(2,1)S(1)}, bf16[1024,256]{1,0:T(8,128)(2,1)S(1)}, u32[]{:S(2)}, u32[]{:S(2)}) collective-permute-start(bf16[1024,256]{1,0:T(8,128)(2,1)S(1)} %add_convert_fusion.1), channel_id=1, source_target_pairs={{0,1},{1,2},{2,3},{3,4},{4,5},{5,6},{6,7},{7,0},{32,39},{33,32},{3... | collective-permute-start | bytes 1572872 | tf_op jit(solution)/shard_map/ppermute | solution.py:36
  104.8 1.1 collective-permute-done.12
  105.9 0.1 add_convert_fusion.3
  106.0 5.6 %collective-permute-start.13 = (bf16[1024,256]{1,0:T(8,128)(2,1)S(1)}, bf16[1024,256]{1,0:T(8,128)(2,1)S(1)}, u32[]{:S(2)}, u32[]{:S(2)}) collective-permute-start(bf16[1024,256]{1,0:T(8,128)(2,1)S(1)} %add_convert_fusion.3), channel_id=1, source_target_pairs={{0,1},{1,2},{2,3},{3,4},{4,5},{5,6},{6,7},{7,0},{32,39},{33,32},{3... | collective-permute-start | bytes 1572872 | tf_op jit(solution)/shard_map/ppermute | solution.py:36
  111.7 0.0 collective-permute-done.17
  111.7 1.9 %collective-permute-start.18 = (bf16[1024,256]{1,0:T(8,128)(2,1)S(1)}, bf16[1024,256]{1,0:T(8,128)(2,1)S(1)}, u32[]{:S(2)}, u32[]{:S(2)}) collective-permute-start(bf16[1024,256]{1,0:T(8,128)(2,1)S(1)} %collective-permute-done.17), channel_id=1, source_target_pairs={{0,32},{32,0},{1,33},{33,1},{2,34},{34,2},{3,35},{35,3},{4,36},{36... | collective-permute-start | bytes 1572872 | tf_op jit(solution)/shard_map/ppermute | solution.py:21
  113.6 0.0 copy-done.5
  113.6 0.0 copy-done.3
  113.6 0.0 copy-done.4
  113.6 0.1 multiply_add_fusion
  113.8 4.6 %collective-permute-done.13 = bf16[1024,256]{1,0:T(8,128)(2,1)S(1)} collective-permute-done((bf16[1024,256]{1,0:T(8,128)(2,1)S(1)}, bf16[1024,256]{1,0:T(8,128)(2,1)S(1)}, u32[]{:S(2)}, u32[]{:S(2)}) %collective-permute-start.13) | collective-permute-done | bytes 524320 | tf_op jit(solution)/shard_map/ppermute | solution.py:36
  118.3 0.0 collective-permute-done.18
  118.3 0.2 add_convert_fusion
  118.5 22.1 %all_to_all.9 = bf16[4,256,256]{2,1,0:T(8,128)(2,1)S(1)} all-to-all(bf16[4,256,256]{2,1,0:T(8,128)(2,1)S(1)} %bitcast.1), channel_id=1, replica_groups=mesh['ylo'=2,'z'=8,'core'=2,'yhi'=4,'x'=8] {'yhi'}, dimensions={0} | all-to-all | bytes 1048576 | tf_op jit(solution)/shard_map/all_to_all | solution.py:184
  140.7 0.1 convert_reduce_fusion
  140.7 0.7 add_convert_fusion.6
  (13 shorter events, 0.2 us)
Async XLA Ops:
  0.0 7.3 %collective-permute-start = (bf16[256,256]{1,0:T(8,128)(2,1)}, bf16[256,256]{1,0:T(8,128)(2,1)S(1)}, u32[]{:S(2)}, u32[]{:S(2)}) collective-permute-start(bf16[256,256]{1,0:T(8,128)(2,1)} %param.7), channel_id=1, source_target_pairs={{0,512},{512,0},{1,513},{513,1},{2,514},{514,2},{3,515},{515,3},{4... | collective-permute-start | bytes 393224 | tf_op jit(solution)/shard_map/ppermute | solution.py:21
  7.4 53.8 %copy-start = (bf16[24,256,256]{2,1,0:T(8,128)(2,1)S(1)}, bf16[24,256,256]{2,1,0:T(8,128)(2,1)}, u32[]{:S(2)}) copy-start(bf16[24,256,256]{2,1,0:T(8,128)(2,1)} %tiles.3) | copy-start | bytes 9437188
  7.4 53.8 %copy-start.1 = (s32[24]{0:T(128)S(1)}, s32[24]{0:T(128)}, u32[]{:S(2)}) copy-start(s32[24]{0:T(128)} %rows.3) | copy-start | bytes 292
  7.4 53.8 %copy-start.2 = (s32[24]{0:T(128)S(1)}, s32[24]{0:T(128)}, u32[]{:S(2)}) copy-start(s32[24]{0:T(128)} %srcs.3) | copy-start | bytes 292
  7.4 28.7 %collective-permute-start.3 = (bf16[512,256]{1,0:T(8,128)(2,1)S(1)}, bf16[512,256]{1,0:T(8,128)(2,1)S(1)}, u32[]{:S(2)}, u32[]{:S(2)}) collective-permute-start(bf16[512,256]{1,0:T(8,128)(2,1)S(1)} %get-tuple-element.19), channel_id=1, source_target_pairs={{0,128},{64,192},{128,256},{192,320},{256,384},{320,448},{384,0},{... | collective-permute-start | bytes 786440 | tf_op jit(solution)/shard_map/ppermute | solution.py:21
  15.6 22.5 %collective-permute-start.4 = (bf16[512,256]{1,0:T(8,128)(2,1)S(1)}, bf16[512,256]{1,0:T(8,128)(2,1)S(1)}, u32[]{:S(2)}, u32[]{:S(2)}) collective-permute-start(bf16[512,256]{1,0:T(8,128)(2,1)S(1)} %get-tuple-element.19), channel_id=1, source_target_pairs={{0,384},{64,448},{128,0},{192,64},{256,128},{320,192},{384,256},{4... | collective-permute-start | bytes 786440 | tf_op jit(solution)/shard_map/ppermute | solution.py:21
  26.0 20.7 %collective-permute-start.1 = (bf16[512,256]{1,0:T(8,128)(2,1)S(1)}, bf16[512,256]{1,0:T(8,128)(2,1)S(1)}, u32[]{:S(2)}, u32[]{:S(2)}) collective-permute-start(bf16[512,256]{1,0:T(8,128)(2,1)S(1)} %get-tuple-element.19), channel_id=1, source_target_pairs={{0,64},{64,128},{128,192},{192,256},{256,320},{320,384},{384,448},... | collective-permute-start | bytes 786440 | tf_op jit(solution)/shard_map/ppermute | solution.py:21
  30.3 20.9 %collective-permute-start.2 = (bf16[512,256]{1,0:T(8,128)(2,1)S(1)}, bf16[512,256]{1,0:T(8,128)(2,1)S(1)}, u32[]{:S(2)}, u32[]{:S(2)}) collective-permute-start(bf16[512,256]{1,0:T(8,128)(2,1)S(1)} %get-tuple-element.19), channel_id=1, source_target_pairs={{0,448},{64,0},{128,64},{192,128},{256,192},{320,256},{384,320},{4... | collective-permute-start | bytes 786440 | tf_op jit(solution)/shard_map/ppermute | solution.py:21
  36.1 19.0 %collective-permute-start.7 = (bf16[256,256]{1,0:T(8,128)(2,1)S(1)}, bf16[256,256]{1,0:T(8,128)(2,1)S(1)}, u32[]{:S(2)}, u32[]{:S(2)}) collective-permute-start(bf16[256,256]{1,0:T(8,128)(2,1)S(1)} %slice.20), channel_id=1, source_target_pairs={{0,128},{64,192},{128,256},{192,320},{256,384},{320,448},{384,0},{... | collective-permute-start | bytes 393224 | tf_op jit(solution)/shard_map/ppermute | solution.py:21
  38.0 17.0 %collective-permute-start.8 = (bf16[256,256]{1,0:T(8,128)(2,1)S(1)}, bf16[256,256]{1,0:T(8,128)(2,1)S(1)}, u32[]{:S(2)}, u32[]{:S(2)}) collective-permute-start(bf16[256,256]{1,0:T(8,128)(2,1)S(1)} %slice.21), channel_id=1, source_target_pairs={{0,384},{64,448},{128,0},{192,64},{256,128},{320,192},{384,256},{4... | collective-permute-start | bytes 393224 | tf_op jit(solution)/shard_map/ppermute | solution.py:21
  44.1 9.5 %collective-permute-start.5 = (bf16[512,256]{1,0:T(8,128)(2,1)S(1)}, bf16[512,256]{1,0:T(8,128)(2,1)S(1)}, u32[]{:S(2)}, u32[]{:S(2)}) collective-permute-start(bf16[512,256]{1,0:T(8,128)(2,1)S(1)} %collective-permute-done.3), channel_id=1, source_target_pairs={{0,64},{64,128},{128,192},{192,256},{256,320},{320,384},{384,448},... | collective-permute-start | bytes 786440 | tf_op jit(solution)/shard_map/ppermute | solution.py:21
  46.7 8.3 %collective-permute-start.6 = (bf16[512,256]{1,0:T(8,128)(2,1)S(1)}, bf16[512,256]{1,0:T(8,128)(2,1)S(1)}, u32[]{:S(2)}, u32[]{:S(2)}) collective-permute-start(bf16[512,256]{1,0:T(8,128)(2,1)S(1)} %collective-permute-done.4), channel_id=1, source_target_pairs={{0,448},{64,0},{128,64},{192,128},{256,192},{320,256},{384,320},{4... | collective-permute-start | bytes 786440 | tf_op jit(solution)/shard_map/ppermute | solution.py:21
  55.1 6.1 %collective-permute-start.9 = (bf16[4096,256]{1,0:T(8,128)(2,1)S(1)}, bf16[4096,256]{1,0:T(8,128)(2,1)S(1)}, u32[]{:S(2)}, u32[]{:S(2)}) collective-permute-start(bf16[4096,256]{1,0:T(8,128)(2,1)S(1)} %constant_dynamic-update-slice_fusion.2.near), channel_id=1, source_target_pairs={{0,32},{32,0},{1,33},{33,1},{2,34},{34,2},{3,35},{35,3},{4,36},{36... | collective-permute-start | bytes 6291464 | tf_op jit(solution)/shard_map/ppermute | solution.py:21
  66.2 8.1 %collective-permute-start.14 = (bf16[3072,256]{1,0:T(8,128)(2,1)S(1)}, bf16[3072,256]{1,0:T(8,128)(2,1)S(1)}, u32[]{:S(2)}, u32[]{:S(2)}) collective-permute-start(bf16[3072,256]{1,0:T(8,128)(2,1)S(1)} %get-tuple-element.16), channel_id=1, source_target_pairs={{0,32},{32,0},{1,33},{33,1},{2,34},{34,2},{3,35},{35,3},{4,36},{36... | collective-permute-start | bytes 4718600 | tf_op jit(solution)/shard_map/ppermute | solution.py:21
  71.2 11.1 %collective-permute-start.10 = (bf16[1024,256]{1,0:T(8,128)(2,1)S(1)}, bf16[1024,256]{1,0:T(8,128)(2,1)S(1)}, u32[]{:S(2)}, u32[]{:S(2)}) collective-permute-start(bf16[1024,256]{1,0:T(8,128)(2,1)S(1)} %tile_products.3), channel_id=1, source_target_pairs={{0,1},{1,2},{2,3},{3,4},{4,5},{5,6},{6,7},{7,0},{32,39},{33,32},{3... | collective-permute-start | bytes 1572872 | tf_op jit(solution)/shard_map/ppermute | solution.py:36
  74.4 13.5 %collective-permute-start.15 = (bf16[1024,256]{1,0:T(8,128)(2,1)S(1)}, bf16[1024,256]{1,0:T(8,128)(2,1)S(1)}, u32[]{:S(2)}, u32[]{:S(2)}) collective-permute-start(bf16[1024,256]{1,0:T(8,128)(2,1)S(1)} %slice.24), channel_id=1, source_target_pairs={{0,1},{1,2},{2,3},{3,4},{4,5},{5,6},{6,7},{7,0},{32,39},{33,32},{3... | collective-permute-start | bytes 1572872 | tf_op jit(solution)/shard_map/ppermute | solution.py:36
  82.5 11.1 %collective-permute-start.11 = (bf16[1024,256]{1,0:T(8,128)(2,1)S(1)}, bf16[1024,256]{1,0:T(8,128)(2,1)S(1)}, u32[]{:S(2)}, u32[]{:S(2)}) collective-permute-start(bf16[1024,256]{1,0:T(8,128)(2,1)S(1)} %add_convert_fusion.5), channel_id=1, source_target_pairs={{0,1},{1,2},{2,3},{3,4},{4,5},{5,6},{6,7},{7,0},{32,39},{33,32},{3... | collective-permute-start | bytes 1572872 | tf_op jit(solution)/shard_map/ppermute | solution.py:36
  88.1 11.2 %collective-permute-start.16 = (bf16[1024,256]{1,0:T(8,128)(2,1)S(1)}, bf16[1024,256]{1,0:T(8,128)(2,1)S(1)}, u32[]{:S(2)}, u32[]{:S(2)}) collective-permute-start(bf16[1024,256]{1,0:T(8,128)(2,1)S(1)} %add_convert_fusion.2), channel_id=1, source_target_pairs={{0,1},{1,2},{2,3},{3,4},{4,5},{5,6},{6,7},{7,0},{32,39},{33,32},{3... | collective-permute-start | bytes 1572872 | tf_op jit(solution)/shard_map/ppermute | solution.py:36
  93.5 20.1 %copy-start.5 = (s32[256]{0:T(256)S(1)}, s32[256]{0:T(256)}, u32[]{:S(2)}) copy-start(s32[256]{0:T(256)} %param.13) | copy-start | bytes 3076
  93.5 20.1 %copy-start.3 = (bf16[256,256]{1,0:T(8,128)(2,1)S(1)}, bf16[256,256]{1,0:T(8,128)(2,1)}, u32[]{:S(2)}) copy-start(bf16[256,256]{1,0:T(8,128)(2,1)} %param.7) | copy-start | bytes 393220
  93.5 20.1 %copy-start.4 = (bf16[256,256]{1,0:T(8,128)(2,1)S(1)}, bf16[256,256]{1,0:T(8,128)(2,1)}, u32[]{:S(2)}) copy-start(bf16[256,256]{1,0:T(8,128)(2,1)} %param.8) | copy-start | bytes 393220
  93.7 12.2 %collective-permute-start.12 = (bf16[1024,256]{1,0:T(8,128)(2,1)S(1)}, bf16[1024,256]{1,0:T(8,128)(2,1)S(1)}, u32[]{:S(2)}, u32[]{:S(2)}) collective-permute-start(bf16[1024,256]{1,0:T(8,128)(2,1)S(1)} %add_convert_fusion.4), channel_id=1, source_target_pairs={{0,1},{1,2},{2,3},{3,4},{4,5},{5,6},{6,7},{7,0},{32,39},{33,32},{3... | collective-permute-start | bytes 1572872 | tf_op jit(solution)/shard_map/ppermute | solution.py:36
  99.4 12.3 %collective-permute-start.17 = (bf16[1024,256]{1,0:T(8,128)(2,1)S(1)}, bf16[1024,256]{1,0:T(8,128)(2,1)S(1)}, u32[]{:S(2)}, u32[]{:S(2)}) collective-permute-start(bf16[1024,256]{1,0:T(8,128)(2,1)S(1)} %add_convert_fusion.1), channel_id=1, source_target_pairs={{0,1},{1,2},{2,3},{3,4},{4,5},{5,6},{6,7},{7,0},{32,39},{33,32},{3... | collective-permute-start | bytes 1572872 | tf_op jit(solution)/shard_map/ppermute | solution.py:36
  106.0 12.3 %collective-permute-start.13 = (bf16[1024,256]{1,0:T(8,128)(2,1)S(1)}, bf16[1024,256]{1,0:T(8,128)(2,1)S(1)}, u32[]{:S(2)}, u32[]{:S(2)}) collective-permute-start(bf16[1024,256]{1,0:T(8,128)(2,1)S(1)} %add_convert_fusion.3), channel_id=1, source_target_pairs={{0,1},{1,2},{2,3},{3,4},{4,5},{5,6},{6,7},{7,0},{32,39},{33,32},{3... | collective-permute-start | bytes 1572872 | tf_op jit(solution)/shard_map/ppermute | solution.py:36
  111.7 6.7 %collective-permute-start.18 = (bf16[1024,256]{1,0:T(8,128)(2,1)S(1)}, bf16[1024,256]{1,0:T(8,128)(2,1)S(1)}, u32[]{:S(2)}, u32[]{:S(2)}) collective-permute-start(bf16[1024,256]{1,0:T(8,128)(2,1)S(1)} %collective-permute-done.17), channel_id=1, source_target_pairs={{0,32},{32,0},{1,33},{33,1},{2,34},{34,2},{3,35},{35,3},{4,36},{36... | collective-permute-start | bytes 1572872 | tf_op jit(solution)/shard_map/ppermute | solution.py:21
